TPU v7x, 512 devices: a whole 4x8x8 slice. The times are simulated.
512 devices in a mesh: shot: 32 (over z_hi, y, core), tx: 4 (over x), ty: 4 (over z_lo).
Axes of the slice: x: 4, y: 8, z: 8 (z_hi: 2, z_lo: 4; z = z_hi * 4 + z_lo), core: 2. Of those that a mesh axis runs over, the one named last changes fastest.
Arguments:
- wave_now: float32 [128, 64, 64, 128], P('shot', 'tx', 'ty'), may hold values from -6 to 6
- wave_prev: float32 [128, 64, 64, 128], P('shot', 'tx', 'ty'), may hold values from -6 to 6
- courant: float32 [64, 64, 128], P('tx', 'ty'), may hold values from 0.02 to 0.3
- rec_index: int32 [4, 4, 512], P('tx', 'ty'), may hold values from 0 to 32767
- rec_history: bfloat16 [128, 8, 4, 4, 512], P('shot', None, 'tx', 'ty'), may hold values from -6 to 6
- green: bfloat16 [2, 8192, 8192], P(None, ('tx', 'ty'), 'shot'), may hold values from -0.046875 to 0.046875
- lag_delay: int32 [2], replicated, may hold values from 1 to 8, as said below
- emit_cells: int32 [4, 4, 8, 512], P('tx', 'ty'), may hold values from 0 to 32767
- emit_weights: float32 [4, 4, 8, 512], P('tx', 'ty'), may hold values from 0.25 to 1
Outputs:
- wave_out: float32 [128, 64, 64, 128], P('shot', 'tx', 'ty')
- wave_last: float32 [128, 64, 64, 128], P('shot', 'tx', 'ty')
- emission: float32 [128, 8, 4, 4, 512], P('shot', None, 'tx', 'ty')
Inputs may be any that keep to these rules, and one draw needn't show every extreme that they name: `lag_delay`: one lag group has delay 8, the other a smaller one.
All inputs are finite; a program needn't handle non-finite values.
Results may differ from a plain program's by a relative error of at most 0.0023.
Values may be sent and summed in bfloat16 or wider, within the bound.
No kernel may reach another device: no remote copies, remote signals or barrier semaphores. Data moves between devices by JAX's collectives and lax.ppermute only.
A program may use at most 128 MiB of HBM per device.

v0:
```python
import jax
import jax.numpy as jnp
from jax import lax
from jax.experimental import pallas as pl
from jax.experimental.pallas import tpu as pltpu
from jax.sharding import PartitionSpec as P


STEPS = 8
HIST = 8
BAND = 8
TILE = 16
WIDE = TILE + 2 * BAND
DEPTH = 128
PAD = 8
F32 = jnp.float32
BF16 = jnp.bfloat16
NT = (((1,), (1,)), ((), ()))


def shot_id(half, row, core):
    return (half * 8 + row) * 2 + core


SHOT_COORDS = [(h, r, c) for h in range(2) for r in range(8) for c in range(2)]
CORE_SWAP = [(shot_id(h, r, c), shot_id(h, r, 1 - c)) for h, r, c in SHOT_COORDS]
HALF_SWAP = [(shot_id(h, r, c), shot_id(1 - h, r, c)) for h, r, c in SHOT_COORDS]
ROW_GROUPS = [[shot_id(h, r, c) for r in range(8)] for h in range(2) for c in range(2)]
UP = [(i, i + 1) for i in range(3)]
DOWN = [(i + 1, i) for i in range(3)]


def row_exchange(x):
    return lax.all_to_all(
        x, "shot", split_axis=0, concat_axis=0, tiled=True, axis_index_groups=ROW_GROUPS
    )


def spread_rows(x):
    return row_exchange(jnp.broadcast_to(x[None], (8, *x.shape)))


def stencil_kernel(
    now, prev, speed_in, xm, xp, ym, yp, cmm, cmp, cpm, cpp, rows_hot, lanes_hot,
    next_out, last_out, rec_out, cur, prv, spd, sems, out_sems,
):
    shots = now.shape[0]
    low = slice(0, BAND)
    mid = slice(BAND, BAND + TILE)
    high = slice(BAND + TILE, WIDE)
    ylow = slice(PAD, PAD + BAND)
    ymid = slice(PAD + BAND, PAD + BAND + TILE)
    yhigh = slice(PAD + BAND + TILE, PAD + WIDE)
    copies = []

    def add(src, dst):
        copies.append(pltpu.make_async_copy(src, dst, sems.at[len(copies)]))

    add(now, cur.at[:, mid, ymid])
    add(prev, prv.at[:, mid, ymid])
    add(speed_in, spd.at[mid, ymid])
    for block, xs, ys in (
        (xm, low, ymid), (xp, high, ymid), (ym, mid, ylow), (yp, mid, yhigh),
        (cmm, low, ylow), (cmp, low, yhigh), (cpm, high, ylow), (cpp, high, yhigh),
    ):
        add(block.at[pl.ds(0, shots)], cur.at[:, xs, ys])
        add(block.at[pl.ds(shots, shots)], prv.at[:, xs, ys])
        add(block.at[2 * shots], spd.at[xs, ys])
    for copy in copies:
        copy.start()
    for copy in copies:
        copy.wait()

    bufs = (cur, prv)
    lanes = lax.broadcasted_iota(jnp.int32, (WIDE, DEPTH), 1)
    sel_row = lax.broadcasted_iota(jnp.int32, (shots * STEPS, shots * DEPTH), 0)
    sel_col = lax.broadcasted_iota(jnp.int32, (shots * STEPS, shots * DEPTH), 1)
    records = jnp.zeros((shots * STEPS, rows_hot.shape[0]), F32)
    for step in range(1, STEPS + 1):
        src, dst = bufs[(step - 1) % 2], bufs[step % 2]
        if step < STEPS:
            start, count = PAD, WIDE
        else:
            start, count = PAD + BAND, TILE
        lane = lanes[:count]

        def body(x, carry, src=src, dst=dst, start=start, count=count, lane=lane):
            speed = spd[x, pl.ds(start, count), :]
            centre = 2.0 - 6.0 * speed
            for s in range(shots):
                u = src[s, x, pl.ds(start, count), :]
                total = src[s, x - 1, pl.ds(start, count), :] + src[s, x + 1, pl.ds(start, count), :]
                total = total + src[s, x, pl.ds(start - 1, count), :]
                total = total + src[s, x, pl.ds(start + 1, count), :]
                total = total + jnp.where(lane > 0, pltpu.roll(u, 1, 1), 0.0)
                total = total + jnp.where(lane < DEPTH - 1, pltpu.roll(u, DEPTH - 1, 1), 0.0)
                dst[s, x, pl.ds(start, count), :] = (
                    centre * u - dst[s, x, pl.ds(start, count), :] + speed * total
                )
            return carry

        lax.fori_loop(step, WIDE - step, body, 0)
        if step < STEPS:
            field = jnp.concatenate(
                [dst[s, mid, ymid, :].reshape(TILE * TILE, DEPTH).astype(BF16) for s in range(shots)],
                axis=1,
            )
            picked = jnp.dot(rows_hot[...], field, preferred_element_type=F32)
            mask = jnp.concatenate([lanes_hot[...]] * shots, axis=1)
            picked = (picked * mask).astype(BF16)
            sel = (sel_row == (sel_col // DEPTH) * STEPS + (step - 1)).astype(F32).astype(BF16)
            records = records + lax.dot_general(sel, picked, NT, preferred_element_type=F32)
    rec_out[...] = records.astype(BF16)
    out_next = pltpu.make_async_copy(bufs[STEPS % 2].at[:, mid, ymid], next_out, out_sems.at[0])
    out_last = pltpu.make_async_copy(bufs[(STEPS - 1) % 2].at[:, mid, ymid], last_out, out_sems.at[1])
    out_next.start()
    out_last.start()
    out_next.wait()
    out_last.wait()


def stencil(now, prev, speed, halos, rows_hot, lanes_hot):
    shots = now.shape[0]
    points = rows_hot.shape[0]
    anywhere = pl.BlockSpec(memory_space=pl.ANY)
    vmem = pl.BlockSpec(memory_space=pltpu.VMEM)
    wide = (shots, WIDE, WIDE + 2 * PAD, DEPTH)
    return pl.pallas_call(
        stencil_kernel,
        out_shape=(
            jax.ShapeDtypeStruct(now.shape, F32),
            jax.ShapeDtypeStruct(now.shape, F32),
            jax.ShapeDtypeStruct((shots * STEPS, points), BF16),
        ),
        in_specs=[anywhere] * 11 + [vmem] * 2,
        out_specs=(anywhere, anywhere, vmem),
        scratch_shapes=[
            pltpu.VMEM(wide, F32),
            pltpu.VMEM(wide, F32),
            pltpu.VMEM(wide[1:], F32),
            pltpu.SemaphoreType.DMA((27,)),
            pltpu.SemaphoreType.DMA((2,)),
        ],
        compiler_params=pltpu.CompilerParams(vmem_limit_bytes=16 << 20),
        cost_estimate=pl.CostEstimate(flops=2_000_000_000, bytes_accessed=12_000_000, transcendentals=0),
        name="stencil",
    )(now, prev, speed, *halos, rows_hot, lanes_hot)


def columns_kernel(delay, old, new, green, out):
    groups, rows, _ = old.shape
    half = rows // 2
    lags = green.shape[0]
    width = green.shape[2]
    sel_row = lax.broadcasted_iota(jnp.int32, (half, 2 * rows), 0)
    sel_col = lax.broadcasted_iota(jnp.int32, (half, 2 * rows), 1)
    col_shot = (sel_col % rows) // STEPS
    col_time = (sel_col // rows) * HIST + sel_col % STEPS
    both = [jnp.concatenate([old[g], new[g]], axis=0) for g in range(groups)]
    parts = []
    for h in range(2):
        row_shot = sel_row // STEPS + h * (half // STEPS)
        total = None
        for lag in range(lags):
            wanted = HIST + sel_row % STEPS - delay[lag]
            sel = jnp.logical_and(col_shot == row_shot, col_time == wanted)
            sel = sel.astype(F32).astype(BF16)
            window = jnp.concatenate(
                [jnp.dot(sel, b, preferred_element_type=F32).astype(BF16) for b in both], axis=0
            )
            term = jnp.dot(window, green[lag], preferred_element_type=F32)
            total = term if total is None else total + term
        parts.append(total)
    lane = lax.broadcasted_iota(jnp.int32, (groups * half, 128), 1)
    for m in range(width // 128):
        a = parts[0][:, m * 128 : (m + 1) * 128]
        b = parts[1][:, m * 128 : (m + 1) * 128]
        out[2 * m] = jnp.where(lane < 64, a, pltpu.roll(b, 64, 1))
        out[2 * m + 1] = jnp.where(lane < 64, pltpu.roll(a, 64, 1), b)


def columns(delay, old, new, green):
    vmem = pl.BlockSpec(memory_space=pltpu.VMEM)
    return pl.pallas_call(
        columns_kernel,
        out_shape=jax.ShapeDtypeStruct((16, 128, 128), F32),
        in_specs=[pl.BlockSpec(memory_space=pltpu.SMEM), vmem, vmem, vmem],
        out_specs=vmem,
        compiler_params=pltpu.CompilerParams(vmem_limit_bytes=12 << 20),
        cost_estimate=pl.CostEstimate(flops=1_000_000_000, bytes_accessed=4_000_000, transcendentals=0),
        name="columns",
    )(delay, old, new, green)


def inject_kernel(em, cells, weights, field, wave_out, emission, rhs_high, rhs_low, acc):
    shots = field.shape[0]
    points = cells.shape[1]
    lane = lax.broadcasted_iota(jnp.int32, (16, 128), 1)
    for sh in range(2):
        for tile in range(4):
            z = tile // 2
            block = None
            for i in range(4):
                piece = em[(tile % 2) * 4 + i]
                shift = (i * 32 - sh * 64 - z * 32) % 128
                if shift:
                    piece = pltpu.roll(piece, shift, 1)
                block = piece if block is None else jnp.where(lane >= i * 32, piece, block)
            emission[pl.ds(sh * 16, 16), pl.ds(tile * 128, 128)] = block

    acc[...] = jnp.zeros_like(acc)
    row_iota = lax.broadcasted_iota(jnp.int32, (TILE * TILE, points), 0)
    lane_iota = lax.broadcasted_iota(jnp.int32, (DEPTH, points), 0)

    def body(k, carry):
        cell = cells[pl.ds(k, 1), :]
        weight = weights[pl.ds(k, 1), :]
        rows_hot = (row_iota == lax.shift_right_logical(cell, 7)).astype(F32).astype(BF16)
        lane_hot = lane_iota == jnp.bitwise_and(cell, DEPTH - 1)
        for s in range(shots):
            value = weight * emission[pl.ds(s * STEPS + STEPS - 1, 1), :]
            top = value.astype(BF16).astype(F32)
            rest = value - top
            rhs_high[pl.ds(s * DEPTH, DEPTH), :] = jnp.where(lane_hot, top, 0.0).astype(BF16)
            rhs_low[pl.ds(s * DEPTH, DEPTH), :] = jnp.where(lane_hot, rest, 0.0).astype(BF16)
        acc[...] += lax.dot_general(
            rows_hot, rhs_high[...], NT, preferred_element_type=F32
        ) + lax.dot_general(rows_hot, rhs_low[...], NT, preferred_element_type=F32)
        return carry

    lax.fori_loop(0, cells.shape[0], body, 0)
    for s in range(shots):
        wave_out[s] = field[s] + acc[:, s * DEPTH : (s + 1) * DEPTH].reshape(TILE, TILE, DEPTH)


def inject(em, cells, weights, field):
    shots = field.shape[0]
    points = cells.shape[1]
    vmem = pl.BlockSpec(memory_space=pltpu.VMEM)
    return pl.pallas_call(
        inject_kernel,
        out_shape=(
            jax.ShapeDtypeStruct(field.shape, F32),
            jax.ShapeDtypeStruct((shots * STEPS, points), F32),
        ),
        in_specs=[vmem] * 4,
        out_specs=(vmem, vmem),
        scratch_shapes=[
            pltpu.VMEM((shots * DEPTH, points), BF16),
            pltpu.VMEM((shots * DEPTH, points), BF16),
            pltpu.VMEM((TILE * TILE, shots * DEPTH), F32),
        ],
        compiler_params=pltpu.CompilerParams(vmem_limit_bytes=12 << 20),
        cost_estimate=pl.CostEstimate(flops=4_000_000_000, bytes_accessed=4_000_000, transcendentals=0),
        name="inject",
    )(em, cells, weights, field)


def halo_blocks(now, prev, speed):
    def stacked(xs, ys):
        return jnp.concatenate([now[:, xs, ys], prev[:, xs, ys], speed[None, xs, ys]], 0)

    whole = slice(None)
    head, tail = slice(0, BAND), slice(TILE - BAND, TILE)
    xm = lax.ppermute(stacked(tail, whole), "tx", UP)
    ym = lax.ppermute(stacked(whole, tail), "ty", UP)
    xp = lax.ppermute(stacked(head, whole), "tx", DOWN)
    yp = lax.ppermute(stacked(whole, head), "ty", DOWN)
    cmm = lax.ppermute(ym[:, tail], "tx", UP)
    cpm = lax.ppermute(xp[:, :, tail], "ty", UP)
    cpp = lax.ppermute(yp[:, head], "tx", DOWN)
    cmp = lax.ppermute(xm[:, :, head], "ty", DOWN)
    return xm, xp, ym, yp, cmm, cmp, cpm, cpp


def gathered_green(green):
    other = lax.ppermute(green, "shot", HALF_SWAP)
    mine = jnp.concatenate([green, other], -1)
    theirs = lax.ppermute(mine, "shot", CORE_SWAP)
    blocks = jnp.concatenate([mine, theirs], -1)
    width = blocks.shape[-1]
    me = lax.axis_index("shot")
    half, core = me // 16, me % 2
    source = lax.broadcasted_iota(jnp.int32, (width, width), 0)
    target = lax.broadcasted_iota(jnp.int32, (width, width), 1)
    block = source // 256
    place = (
        (source % 256 // 16) * 64
        + jnp.bitwise_xor(block % 2, half) * 32
        + jnp.bitwise_xor(block // 2, core) * 16
        + source % 16
    )
    order = (place == target).astype(BF16)
    return jnp.einsum("lrc,cd->lrd", blocks, order, preferred_element_type=BF16)


def block(
    wave_now, wave_prev, courant, rec_index, rec_history, green, lag_delay, emit_cells, emit_weights
):
    shots = wave_now.shape[0]
    receivers = rec_index.reshape(-1)
    rows_hot = (
        lax.shift_right_logical(receivers, 7)[:, None] == jnp.arange(TILE * TILE)[None, :]
    ).astype(BF16)
    lanes_hot = (
        jnp.bitwise_and(receivers, DEPTH - 1)[:, None] == jnp.arange(DEPTH)[None, :]
    ).astype(F32)
    halos = halo_blocks(wave_now, wave_prev, courant)
    old_all = spread_rows(rec_history.reshape(shots * HIST, -1))
    wide_green = gathered_green(green)
    field, wave_last, new_here = stencil(wave_now, wave_prev, courant, halos, rows_hot, lanes_hot)
    new_all = spread_rows(new_here)
    partial = columns(lag_delay, old_all, new_all, wide_green)
    partial = lax.all_to_all(partial.reshape(4, 512, 128), "tx", 0, 0, tiled=True)
    partial = jnp.sum(partial, axis=0).reshape(4, 128, 128)
    summed = jnp.sum(lax.all_to_all(partial, "ty", 0, 0, tiled=True), axis=0)
    em = row_exchange(summed.reshape(8, 16, 128))
    wave_out, emission = inject(
        em, emit_cells.reshape(emit_cells.shape[-2:]), emit_weights.reshape(emit_weights.shape[-2:]), field
    )
    return wave_out, wave_last, emission.reshape(shots, STEPS, 1, 1, -1)


def solution(mesh):
    return jax.shard_map(
        block,
        mesh=mesh,
        in_specs=(
            P("shot", "tx", "ty", None),
            P("shot", "tx", "ty", None),
            P("tx", "ty", None),
            P("tx", "ty", None),
            P("shot", None, "tx", "ty", None),
            P(None, ("tx", "ty"), "shot"),
            P(),
            P("tx", "ty", None, None),
            P("tx", "ty", None, None),
        ),
        out_specs=(
            P("shot", "tx", "ty", None),
            P("shot", "tx", "ty", None),
            P("shot", None, "tx", "ty", None),
        ),
        check_vma=False,
    )
```

profile of v0, /device:TPU:2, one launch (start us, length us, event | category | flops | bytes accessed | tf_op | source)
XLA Modules:
  0.0 177.3 jit_solution(6605784580032486698)
XLA Ops:
  0.6 1.5 broadcast_in_dim.30
  2.1 7.1 %all-to-all-start = ((bf16[8,32,512]{2,1,0:T(8,128)(2,1)}), bf16[8,32,512]{2,1,0:T(8,128)(2,1)S(1)}, u32[]{:S(2)}, u32[]{:S(2)}) async-start(bf16[8,32,512]{2,1,0:T(8,128)(2,1)} %broadcast_in_dim.30), calls=%async_computation | async-start | bytes 524288 | tf_op jit(solution)/shard_map/all_to_all | solution.py:34
  10.1 1.4 fusion.70
  11.6 3.4 %collective-permute-start = (f32[9,8,16,128]{3,2,1,0:T(8,128)S(1)}, f32[9,8,16,128]{3,2,1,0:T(8,128)S(1)}, u32[]{:S(2)}, u32[]{:S(2)}) collective-permute-start(f32[9,8,16,128]{3,2,1,0:T(8,128)S(1)} %pad_maximum_fusion.1), channel_id=1, source_target_pairs={{0,4},{4,8},{8,12},{1,5},{5,9},{9,13},{2,6},{6,10},{10,14},{3,7},{... | collective-permute-start | bytes 1769480 | tf_op jit(solution)/shard_map/ppermute | solution.py:265
  15.1 2.5 %collective-permute-start.1 = (f32[9,8,16,128]{3,2,1,0:T(8,128)S(1)}, f32[9,8,16,128]{3,2,1,0:T(8,128)S(1)}, u32[]{:S(2)}, u32[]{:S(2)}) collective-permute-start(f32[9,8,16,128]{3,2,1,0:T(8,128)S(1)} %pad_maximum_fusion.2), channel_id=1, source_target_pairs={{4,0},{8,4},{12,8},{5,1},{9,5},{13,9},{6,2},{10,6},{14,10},{7,3},{... | collective-permute-start | bytes 1769480 | tf_op jit(solution)/shard_map/ppermute | solution.py:267
  17.6 10.9 %collective-permute-start.8 = (bf16[2,512,256]{2,1,0:T(8,128)(2,1)S(1)}, bf16[2,512,256]{2,1,0:T(8,128)(2,1)S(1)}, u32[]{:S(2)}, u32[]{:S(2)}) collective-permute-start(bf16[2,512,256]{2,1,0:T(8,128)(2,1)S(1)} %copy-done.10), channel_id=1, source_target_pairs={{0,256},{16,272},{32,288},{48,304},{64,320},{80,336},{96,352},{112... | collective-permute-start | bytes 1572872 | tf_op jit(solution)/shard_map/ppermute | solution.py:277
  28.7 3.4 %collective-permute-start.2 = (f32[9,16,8,128]{3,2,1,0:T(8,128)S(1)}, f32[9,16,8,128]{3,2,1,0:T(8,128)S(1)}, u32[]{:S(2)}, u32[]{:S(2)}) collective-permute-start(f32[9,16,8,128]{3,2,1,0:T(8,128)S(1)} %pad_maximum_fusion.3), channel_id=1, source_target_pairs={{0,1},{1,2},{2,3},{4,5},{5,6},{6,7},{8,9},{9,10},{10,11},{12,13},{... | collective-permute-start | bytes 1769480 | tf_op jit(solution)/shard_map/ppermute | solution.py:266
  32.2 1.3 collective-permute-start.3
  33.5 18.4 %collective-permute-done.8 = bf16[2,512,256]{2,1,0:T(8,128)(2,1)S(1)} collective-permute-done((bf16[2,512,256]{2,1,0:T(8,128)(2,1)S(1)}, bf16[2,512,256]{2,1,0:T(8,128)(2,1)S(1)}, u32[]{:S(2)}, u32[]{:S(2)}) %collective-permute-start.8) | collective-permute-done | bytes 524320 | tf_op jit(solution)/shard_map/ppermute | solution.py:277
  53.1 1.9 %collective-permute-start.9 = (bf16[2,512,512]{2,1,0:T(8,128)(2,1)}, bf16[2,512,512]{2,1,0:T(8,128)(2,1)}, u32[]{:S(2)}, u32[]{:S(2)}) collective-permute-start(bf16[2,512,512]{2,1,0:T(8,128)(2,1)} %pad_maximum_fusion), channel_id=1, source_target_pairs={{0,16},{16,0},{32,48},{48,32},{64,80},{80,64},{96,112},{112,96},{1... | collective-permute-start | bytes 3145736 | tf_op jit(solution)/shard_map/ppermute | solution.py:279
  55.2 7.5 %collective-permute-done.2.ym = f32[9,16,8,128]{3,2,1,0:T(8,128)S(1)} collective-permute-done((f32[9,16,8,128]{3,2,1,0:T(8,128)S(1)}, f32[9,16,8,128]{3,2,1,0:T(8,128)S(1)}, u32[]{:S(2)}, u32[]{:S(2)}) %collective-permute-start.2) | collective-permute-done | bytes 589856 | tf_op jit(solution)/shard_map/ppermute | solution.py:266
  63.4 3.4 %collective-permute-start.4 = (f32[9,8,8,128]{3,2,1,0:T(8,128)}, f32[9,8,8,128]{3,2,1,0:T(8,128)}, u32[]{:S(2)}, u32[]{:S(2)}) collective-permute-start(f32[9,8,8,128]{3,2,1,0:T(8,128)} %slice.64), channel_id=1, source_target_pairs={{0,4},{4,8},{8,12},{1,5},{5,9},{9,13},{2,6},{6,10},{10,14},{3,7},{... | collective-permute-start | bytes 884744 | tf_op jit(solution)/shard_map/ppermute | solution.py:269
  69.6 5.7 %collective-permute-start.6 = (f32[9,8,8,128]{3,2,1,0:T(8,128)}, f32[9,8,8,128]{3,2,1,0:T(8,128)}, u32[]{:S(2)}, u32[]{:S(2)}) collective-permute-start(f32[9,8,8,128]{3,2,1,0:T(8,128)} %slice.66), channel_id=1, source_target_pairs={{0,1},{1,2},{2,3},{4,5},{5,6},{6,7},{8,9},{9,10},{10,11},{12,13},{... | collective-permute-start | bytes 884744 | tf_op jit(solution)/shard_map/ppermute | solution.py:270
  76.9 3.2 %collective-permute-start.7 = (f32[9,8,8,128]{3,2,1,0:T(8,128)}, f32[9,8,8,128]{3,2,1,0:T(8,128)}, u32[]{:S(2)}, u32[]{:S(2)}) collective-permute-start(f32[9,8,8,128]{3,2,1,0:T(8,128)} %slice.67), channel_id=1, source_target_pairs={{4,0},{8,4},{12,8},{5,1},{9,5},{13,9},{6,2},{10,6},{14,10},{7,3},{... | collective-permute-start | bytes 884744 | tf_op jit(solution)/shard_map/ppermute | solution.py:271
  80.3 6.1 %collective-permute-done.7.cpp = f32[9,8,8,128]{3,2,1,0:T(8,128)} collective-permute-done((f32[9,8,8,128]{3,2,1,0:T(8,128)}, f32[9,8,8,128]{3,2,1,0:T(8,128)}, u32[]{:S(2)}, u32[]{:S(2)}) %collective-permute-start.7) | collective-permute-done | bytes 294944 | tf_op jit(solution)/shard_map/ppermute | solution.py:271
  87.5 25.4 %stencil.1 = (f32[4,16,16,128]{3,2,1,0:T(8,128)S(1)}, f32[4,16,16,128]{3,2,1,0:T(8,128)}, bf16[32,512]{1,0:T(8,128)(2,1)S(1)}) custom-call(f32[4,16,16,128]{3,2,1,0:T(8,128)S(1)} %copy-done, f32[4,16,16,128]{3,2,1,0:T(8,128)S(1)} %copy-done.1, f32[16,16,128]{2,1,0:T(8,128)S(1)} %copy-done.2, f32[9,8,16,128]{3,2,1,0:T(8,128)S(1)} %collective-permute-done.xm, ...), custom_call_target="tpu_custom_call" | custom-call | flops 2000000000 | bytes 12000000 | tf_op jit(solution)/shard_map/stencil/pallas_call | solution.py:128
  114.5 6.9 %all-to-all-start.1 = ((bf16[8,32,512]{2,1,0:T(8,128)(2,1)}), bf16[8,32,512]{2,1,0:T(8,128)(2,1)S(1)}, u32[]{:S(2)}, u32[]{:S(2)}) async-start(bf16[8,32,512]{2,1,0:T(8,128)(2,1)} %broadcast_in_dim.35), calls=%async_computation.1 | async-start | bytes 524288 | tf_op jit(solution)/shard_map/all_to_all | solution.py:34
  121.4 4.6 %fusion.18.green = bf16[2,512,1024]{2,1,0:T(8,128)(2,1)S(1)} fusion(bf16[2,512,512]{2,1,0:T(8,128)(2,1)} %collective-permute-done.9, bf16[2,512,256]{2,1,0:T(8,128)(2,1)} %copy-done.11, bf16[2,512,256]{2,1,0:T(8,128)(2,1)} %param.14, s32[1024]{0:T(1024)S(1)} %get-tuple-element.38, s32[1024]{0:T(1024)S(1)} %get-tuple-element.39, s32[]{:T(128)S(6)} %select_n.44, ...), kind=kOutput, calls=%fused_computation.33 | convolution fusion | flops 2202009600 | bytes 4221960 | tf_op jit(solution)/shard_map/lrc,cd->lrd/dot_general | solution.py:294
  126.0 5.8 %all-to-all-done.1.new = bf16[8,32,512]{2,1,0:T(8,128)(2,1)S(1)} async-done(((bf16[8,32,512]{2,1,0:T(8,128)(2,1)}), bf16[8,32,512]{2,1,0:T(8,128)(2,1)S(1)}, u32[]{:S(2)}, u32[]{:S(2)}) %all-to-all-start.1) | async-done | bytes 262176 | tf_op jit(solution)/shard_map/all_to_all | solution.py:34
  131.9 1.8 %columns.1 = f32[16,128,128]{2,1,0:T(8,128)S(1)} custom-call(s32[2]{0:T(128)S(1)} %copy-done.7, bf16[8,32,512]{2,1,0:T(8,128)(2,1)S(1)} %all-to-all-done.old, bf16[8,32,512]{2,1,0:T(8,128)(2,1)S(1)} %all-to-all-done.1.new, bf16[2,512,1024]{2,1,0:T(8,128)(2,1)S(1)} %fusion.18.green), custom_call_target="tpu_custom_call" | custom-call | flops 1000000000 | bytes 4000000 | tf_op jit(solution)/shard_map/columns/pallas_call | solution.py:184
  133.7 14.5 %all_to_all.25 = f32[4,512,128]{2,1,0:T(8,128)S(1)} all-to-all(f32[4,512,128]{2,1,0:T(8,128)S(1)} %bitcast.20), channel_id=1, replica_groups=mesh['shot'=32,'tx'=4,'ty'=4] {'tx'}, dimensions={0} | all-to-all | bytes 2097152 | tf_op jit(solution)/shard_map/all_to_all | solution.py:314
  148.3 12.6 %all_to_all.26 = f32[4,128,128]{2,1,0:T(8,128)S(1)} all-to-all(f32[4,128,128]{2,1,0:T(8,128)S(1)} %bitcast.24), channel_id=1, replica_groups=mesh['shot'=32,'tx'=4,'ty'=4] {'ty'}, dimensions={0} | all-to-all | bytes 524288 | tf_op jit(solution)/shard_map/all_to_all | solution.py:316
  160.9 10.8 %all_to_all.27.em = f32[8,16,128]{2,1,0:T(8,128)S(1)} all-to-all(f32[8,16,128]{2,1,0:T(8,128)S(1)} %bitcast.25), channel_id=1, replica_groups={{0,32,64,96,128,160,192,224},{16,48,80,112,144,176,208,240},{256,288,32..., dimensions={0} | all-to-all | bytes 131072 | tf_op jit(solution)/shard_map/all_to_all | solution.py:34
  171.7 4.9 %inject.1 = (f32[4,16,16,128]{3,2,1,0:T(8,128)}, f32[32,512]{1,0:T(8,128)S(1)}) custom-call(f32[8,16,128]{2,1,0:T(8,128)S(1)} %all_to_all.27.em, s32[8,512]{1,0:T(8,128)S(1)} %bitcast.22, f32[8,512]{1,0:T(8,128)S(1)} %bitcast.23, f32[4,16,16,128]{3,2,1,0:T(8,128)S(1)} %copy-done.9), custom_call_target="tpu_custom_call" | custom-call | flops 4000000000 | bytes 4000000 | tf_op jit(solution)/shard_map/inject/pallas_call | solution.py:240
  (59 shorter events, 11.1 us)
Async XLA Ops:
  2.1 111.6 %all-to-all-start = ((bf16[8,32,512]{2,1,0:T(8,128)(2,1)}), bf16[8,32,512]{2,1,0:T(8,128)(2,1)S(1)}, u32[]{:S(2)}, u32[]{:S(2)}) async-start(bf16[8,32,512]{2,1,0:T(8,128)(2,1)} %broadcast_in_dim.30), calls=%async_computation | async-start | bytes 524288 | tf_op jit(solution)/shard_map/all_to_all | solution.py:34
  10.1 7.4 %copy-start.10 = (bf16[2,512,256]{2,1,0:T(8,128)(2,1)S(1)}, bf16[2,512,256]{2,1,0:T(8,128)(2,1)}, u32[]{:S(2)}) copy-start(bf16[2,512,256]{2,1,0:T(8,128)(2,1)} %param.14) | copy-start | bytes 1572868
  10.1 18.4 %copy-start.2 = (f32[16,16,128]{2,1,0:T(8,128)S(1)}, f32[16,16,128]{2,1,0:T(8,128)}, u32[]{:S(2)}) copy-start(f32[16,16,128]{2,1,0:T(8,128)} %speed_in.1) | copy-start | bytes 393220
  10.1 18.4 %copy-start = (f32[4,16,16,128]{3,2,1,0:T(8,128)S(1)}, f32[4,16,16,128]{3,2,1,0:T(8,128)}, u32[]{:S(2)}) copy-start(f32[4,16,16,128]{3,2,1,0:T(8,128)} %now.1) | copy-start | bytes 1572868
  10.1 18.4 %copy-start.1 = (f32[4,16,16,128]{3,2,1,0:T(8,128)S(1)}, f32[4,16,16,128]{3,2,1,0:T(8,128)}, u32[]{:S(2)}) copy-start(f32[4,16,16,128]{3,2,1,0:T(8,128)} %prev.1) | copy-start | bytes 1572868
  11.6 55.2 %collective-permute-start = (f32[9,8,16,128]{3,2,1,0:T(8,128)S(1)}, f32[9,8,16,128]{3,2,1,0:T(8,128)S(1)}, u32[]{:S(2)}, u32[]{:S(2)}) collective-permute-start(f32[9,8,16,128]{3,2,1,0:T(8,128)S(1)} %pad_maximum_fusion.1), channel_id=1, source_target_pairs={{0,4},{4,8},{8,12},{1,5},{5,9},{9,13},{2,6},{6,10},{10,14},{3,7},{... | collective-permute-start | bytes 1769480 | tf_op jit(solution)/shard_map/ppermute | solution.py:265
  15.1 53.8 %collective-permute-start.1 = (f32[9,8,16,128]{3,2,1,0:T(8,128)S(1)}, f32[9,8,16,128]{3,2,1,0:T(8,128)S(1)}, u32[]{:S(2)}, u32[]{:S(2)}) collective-permute-start(f32[9,8,16,128]{3,2,1,0:T(8,128)S(1)} %pad_maximum_fusion.2), channel_id=1, source_target_pairs={{4,0},{8,4},{12,8},{5,1},{9,5},{13,9},{6,2},{10,6},{14,10},{7,3},{... | collective-permute-start | bytes 1769480 | tf_op jit(solution)/shard_map/ppermute | solution.py:267
  17.6 34.4 %collective-permute-start.8 = (bf16[2,512,256]{2,1,0:T(8,128)(2,1)S(1)}, bf16[2,512,256]{2,1,0:T(8,128)(2,1)S(1)}, u32[]{:S(2)}, u32[]{:S(2)}) collective-permute-start(bf16[2,512,256]{2,1,0:T(8,128)(2,1)S(1)} %copy-done.10), channel_id=1, source_target_pairs={{0,256},{16,272},{32,288},{48,304},{64,320},{80,336},{96,352},{112... | collective-permute-start | bytes 1572872 | tf_op jit(solution)/shard_map/ppermute | solution.py:277
  28.6 26.4 %copy-start.12 = (s32[1,1,512]{2,1,0:T(1,128)S(1)}, s32[1,1,512]{2,1,0:T(1,128)}, u32[]{:S(2)}) copy-start(s32[1,1,512]{2,1,0:T(1,128)} %param.12) | copy-start | bytes 6148
  28.7 34.0 %collective-permute-start.2 = (f32[9,16,8,128]{3,2,1,0:T(8,128)S(1)}, f32[9,16,8,128]{3,2,1,0:T(8,128)S(1)}, u32[]{:S(2)}, u32[]{:S(2)}) collective-permute-start(f32[9,16,8,128]{3,2,1,0:T(8,128)S(1)} %pad_maximum_fusion.3), channel_id=1, source_target_pairs={{0,1},{1,2},{2,3},{4,5},{5,6},{6,7},{8,9},{9,10},{10,11},{12,13},{... | collective-permute-start | bytes 1769480 | tf_op jit(solution)/shard_map/ppermute | solution.py:266
  32.2 43.2 %collective-permute-start.3 = (f32[9,16,8,128]{3,2,1,0:T(8,128)S(1)}, f32[9,16,8,128]{3,2,1,0:T(8,128)S(1)}, u32[]{:S(2)}, u32[]{:S(2)}) collective-permute-start(f32[9,16,8,128]{3,2,1,0:T(8,128)S(1)} %pad_maximum_fusion.4), channel_id=1, source_target_pairs={{1,0},{2,1},{3,2},{5,4},{6,5},{7,6},{9,8},{10,9},{11,10},{13,12},{... | collective-permute-start | bytes 1769480 | tf_op jit(solution)/shard_map/ppermute | solution.py:268
  52.0 24.1 %copy-start.11 = (bf16[2,512,256]{2,1,0:T(8,128)(2,1)}, bf16[2,512,256]{2,1,0:T(8,128)(2,1)S(1)}, u32[]{:S(2)}) copy-start(bf16[2,512,256]{2,1,0:T(8,128)(2,1)S(1)} %collective-permute-done.8) | copy-start | bytes 1572868
  53.1 68.3 %collective-permute-start.9 = (bf16[2,512,512]{2,1,0:T(8,128)(2,1)}, bf16[2,512,512]{2,1,0:T(8,128)(2,1)}, u32[]{:S(2)}, u32[]{:S(2)}) collective-permute-start(bf16[2,512,512]{2,1,0:T(8,128)(2,1)} %pad_maximum_fusion), channel_id=1, source_target_pairs={{0,16},{16,0},{32,48},{48,32},{64,80},{80,64},{96,112},{112,96},{1... | collective-permute-start | bytes 3145736 | tf_op jit(solution)/shard_map/ppermute | solution.py:279
  63.4 16.8 %collective-permute-start.4 = (f32[9,8,8,128]{3,2,1,0:T(8,128)}, f32[9,8,8,128]{3,2,1,0:T(8,128)}, u32[]{:S(2)}, u32[]{:S(2)}) collective-permute-start(f32[9,8,8,128]{3,2,1,0:T(8,128)} %slice.64), channel_id=1, source_target_pairs={{0,4},{4,8},{8,12},{1,5},{5,9},{9,13},{2,6},{6,10},{10,14},{3,7},{... | collective-permute-start | bytes 884744 | tf_op jit(solution)/shard_map/ppermute | solution.py:269
  67.5 12.7 %collective-permute-start.5 = (f32[9,8,8,128]{3,2,1,0:T(8,128)}, f32[9,8,8,128]{3,2,1,0:T(8,128)}, u32[]{:S(2)}, u32[]{:S(2)}) collective-permute-start(f32[9,8,8,128]{3,2,1,0:T(8,128)} %slice.65), channel_id=1, source_target_pairs={{1,0},{2,1},{3,2},{5,4},{6,5},{7,6},{9,8},{10,9},{11,10},{13,12},{... | collective-permute-start | bytes 884744 | tf_op jit(solution)/shard_map/ppermute | solution.py:272
  69.6 10.7 %collective-permute-start.6 = (f32[9,8,8,128]{3,2,1,0:T(8,128)}, f32[9,8,8,128]{3,2,1,0:T(8,128)}, u32[]{:S(2)}, u32[]{:S(2)}) collective-permute-start(f32[9,8,8,128]{3,2,1,0:T(8,128)} %slice.66), channel_id=1, source_target_pairs={{0,1},{1,2},{2,3},{4,5},{5,6},{6,7},{8,9},{9,10},{10,11},{12,13},{... | collective-permute-start | bytes 884744 | tf_op jit(solution)/shard_map/ppermute | solution.py:270
  76.1 0.8 copy-start.3
  76.9 9.5 %collective-permute-start.7 = (f32[9,8,8,128]{3,2,1,0:T(8,128)}, f32[9,8,8,128]{3,2,1,0:T(8,128)}, u32[]{:S(2)}, u32[]{:S(2)}) collective-permute-start(f32[9,8,8,128]{3,2,1,0:T(8,128)} %slice.67), channel_id=1, source_target_pairs={{4,0},{8,4},{12,8},{5,1},{9,5},{13,9},{6,2},{10,6},{14,10},{7,3},{... | collective-permute-start | bytes 884744 | tf_op jit(solution)/shard_map/ppermute | solution.py:271
  86.4 1.1 copy-start.4
  114.5 17.4 %all-to-all-start.1 = ((bf16[8,32,512]{2,1,0:T(8,128)(2,1)}), bf16[8,32,512]{2,1,0:T(8,128)(2,1)S(1)}, u32[]{:S(2)}, u32[]{:S(2)}) async-start(bf16[8,32,512]{2,1,0:T(8,128)(2,1)} %broadcast_in_dim.35), calls=%async_computation.1 | async-start | bytes 524288 | tf_op jit(solution)/shard_map/all_to_all | solution.py:34
  121.4 10.5 %copy-start.7 = (s32[2]{0:T(128)S(1)}, s32[2]{0:T(128)}, u32[]{:S(2)}) copy-start(s32[2]{0:T(128)} %delay.1) | copy-start | bytes 28
  133.7 38.0 %copy-start.5 = (s32[1,1,8,512]{3,2,1,0:T(8,128)S(1)}, s32[1,1,8,512]{3,2,1,0:T(8,128)}, u32[]{:S(2)}) copy-start(s32[1,1,8,512]{3,2,1,0:T(8,128)} %param.16) | copy-start | bytes 49156
  133.7 38.0 %copy-start.6 = (f32[1,1,8,512]{3,2,1,0:T(8,128)S(1)}, f32[1,1,8,512]{3,2,1,0:T(8,128)}, u32[]{:S(2)}) copy-start(f32[1,1,8,512]{3,2,1,0:T(8,128)} %param.17) | copy-start | bytes 49156
  133.7 38.0 %copy-start.9 = (f32[4,16,16,128]{3,2,1,0:T(8,128)S(1)}, f32[4,16,16,128]{3,2,1,0:T(8,128)}, u32[]{:S(2)}) copy-start(f32[4,16,16,128]{3,2,1,0:T(8,128)} %copy-done.8) | copy-start | bytes 1572868
  (1 other events, 0.8 us)
where the time goes:
time: 178 us; the launch traced here: 177 us
  starting transfers between devices  51 us (29%)
  waiting for transfers between devices  37.9 us (21%)
  blocking collectives  37.9 us (21%)
  Pallas kernels  32.1 us (18%)
  local copies, waits for them, and re-layouts  11 us (6%)
  matrix products  4.63 us (3%)
    pallas_call x1, Pallas kernels, stencil(): pl.pallas_call(stencil_kernel, out_shape=(jax.ShapeDtypeStruct(now.shape,...  25.4 us
    ppermute x1, waiting for transfers between devices, gathered_green(): other = lax.ppermute(green, 'shot', HALF_SWAP)  18.4 us
    all_to_all x1, blocking collectives, block(): lax.all_to_all(partial.reshape(4, 512, 128), 'tx', 0, 0, tiled=True)  14.5 us
    all_to_all x2, starting transfers between devices, row_exchange(): lax.all_to_all(x, 'shot', split_axis=0, concat_axis=0, tiled=True, axis_i...  14 us
    all_to_all x1, blocking collectives, block(): summed = jnp.sum(lax.all_to_all(partial, 'ty', 0, 0, tiled=True), axis=0)  12.6 us
    ppermute x1, starting transfers between devices, gathered_green(): other = lax.ppermute(green, 'shot', HALF_SWAP)  10.9 us
    all_to_all x1, blocking collectives, row_exchange(): lax.all_to_all(x, 'shot', split_axis=0, concat_axis=0, tiled=True, axis_i...  10.8 us
    ppermute x1, waiting for transfers between devices, halo_blocks(): ym = lax.ppermute(stacked(whole, tail), 'ty', UP)  7.48 us
  transfers between devices with their start and end apart: 12, of which 4 were waited for; matrix products, arithmetic and copies ran while one was open for 7% of the time, Pallas kernels for 14%

commit v1 on v0

--- a/solution.py
+++ b/solution.py
@@ -24,8 +24,12 @@
 
 SHOT_COORDS = [(h, r, c) for h in range(2) for r in range(8) for c in range(2)]
 CORE_SWAP = [(shot_id(h, r, c), shot_id(h, r, 1 - c)) for h, r, c in SHOT_COORDS]
-HALF_SWAP = [(shot_id(h, r, c), shot_id(1 - h, r, c)) for h, r, c in SHOT_COORDS]
-ROW_GROUPS = [[shot_id(h, r, c) for r in range(8)] for h in range(2) for c in range(2)]
+PAIR_SWAP = [(shot_id(h, r, c), shot_id(h, r ^ 1, c)) for h, r, c in SHOT_COORDS]
+ROW_GROUPS = [
+    [shot_id(h, 2 * k + odd, c) for h in range(2) for k in range(4)]
+    for odd in range(2)
+    for c in range(2)
+]
 UP = [(i, i + 1) for i in range(3)]
 DOWN = [(i + 1, i) for i in range(3)]
 
@@ -79,7 +83,7 @@
     for step in range(1, STEPS + 1):
         src, dst = bufs[(step - 1) % 2], bufs[step % 2]
         if step < STEPS:
-            start, count = PAD, WIDE
+            start, count = (PAD, WIDE) if step < 4 else (PAD + 4, WIDE - 8)
         else:
             start, count = PAD + BAND, TILE
         lane = lanes[:count]
@@ -99,7 +103,7 @@
                 )
             return carry
 
-        lax.fori_loop(step, WIDE - step, body, 0)
+        lax.fori_loop(step, WIDE - step, body, 0, unroll=4)
         if step < STEPS:
             field = jnp.concatenate(
                 [dst[s, mid, ymid, :].reshape(TILE * TILE, DEPTH).astype(BF16) for s in range(shots)],
@@ -196,17 +200,10 @@
     shots = field.shape[0]
     points = cells.shape[1]
     lane = lax.broadcasted_iota(jnp.int32, (16, 128), 1)
-    for sh in range(2):
-        for tile in range(4):
-            z = tile // 2
-            block = None
-            for i in range(4):
-                piece = em[(tile % 2) * 4 + i]
-                shift = (i * 32 - sh * 64 - z * 32) % 128
-                if shift:
-                    piece = pltpu.roll(piece, shift, 1)
-                block = piece if block is None else jnp.where(lane >= i * 32, piece, block)
-            emission[pl.ds(sh * 16, 16), pl.ds(tile * 128, 128)] = block
+    for tile in range(4):
+        even, odd = em[2 * tile], em[2 * tile + 1]
+        emission[pl.ds(0, 16), pl.ds(tile * 128, 128)] = jnp.where(lane < 64, even, pltpu.roll(odd, 64, 1))
+        emission[pl.ds(16, 16), pl.ds(tile * 128, 128)] = jnp.where(lane < 64, pltpu.roll(even, 64, 1), odd)
 
     acc[...] = jnp.zeros_like(acc)
     row_iota = lax.broadcasted_iota(jnp.int32, (TILE * TILE, points), 0)
@@ -256,16 +253,41 @@
     )(em, cells, weights, field)
 
 
+def pack_kernel(now, prev, speed, xtail, ytail, xhead, yhead):
+    shots = now.shape[0]
+    head, tail = slice(0, BAND), slice(TILE - BAND, TILE)
+    for out, xs, ys in (
+        (xtail, tail, slice(None)), (ytail, slice(None), tail),
+        (xhead, head, slice(None)), (yhead, slice(None), head),
+    ):
+        out[pl.ds(0, shots)] = now[:, xs, ys]
+        out[pl.ds(shots, shots)] = prev[:, xs, ys]
+        out[2 * shots] = speed[xs, ys]
+
+
+def packed(now, prev, speed):
+    fields = 2 * now.shape[0] + 1
+    vmem = pl.BlockSpec(memory_space=pltpu.VMEM)
+    across = jax.ShapeDtypeStruct((fields, BAND, TILE, DEPTH), F32)
+    along = jax.ShapeDtypeStruct((fields, TILE, BAND, DEPTH), F32)
+    return pl.pallas_call(
+        pack_kernel,
+        out_shape=(across, along, across, along),
+        in_specs=[vmem] * 3,
+        out_specs=(vmem,) * 4,
+        compiler_params=pltpu.CompilerParams(vmem_limit_bytes=8 << 20),
+        cost_estimate=pl.CostEstimate(flops=0, bytes_accessed=4_000_000, transcendentals=0),
+        name="pack",
+    )(now, prev, speed)
+
+
 def halo_blocks(now, prev, speed):
-    def stacked(xs, ys):
-        return jnp.concatenate([now[:, xs, ys], prev[:, xs, ys], speed[None, xs, ys]], 0)
-
-    whole = slice(None)
+    xtail, ytail, xhead, yhead = packed(now, prev, speed)
     head, tail = slice(0, BAND), slice(TILE - BAND, TILE)
-    xm = lax.ppermute(stacked(tail, whole), "tx", UP)
-    ym = lax.ppermute(stacked(whole, tail), "ty", UP)
-    xp = lax.ppermute(stacked(head, whole), "tx", DOWN)
-    yp = lax.ppermute(stacked(whole, head), "ty", DOWN)
+    xm = lax.ppermute(xtail, "tx", UP)
+    ym = lax.ppermute(ytail, "ty", UP)
+    xp = lax.ppermute(xhead, "tx", DOWN)
+    yp = lax.ppermute(yhead, "ty", DOWN)
     cmm = lax.ppermute(ym[:, tail], "tx", UP)
     cpm = lax.ppermute(xp[:, :, tail], "ty", UP)
     cpp = lax.ppermute(yp[:, head], "tx", DOWN)
@@ -274,19 +296,19 @@
 
 
 def gathered_green(green):
-    other = lax.ppermute(green, "shot", HALF_SWAP)
+    other = lax.ppermute(green, "shot", PAIR_SWAP)
     mine = jnp.concatenate([green, other], -1)
     theirs = lax.ppermute(mine, "shot", CORE_SWAP)
     blocks = jnp.concatenate([mine, theirs], -1)
     width = blocks.shape[-1]
     me = lax.axis_index("shot")
-    half, core = me // 16, me % 2
+    odd, core = me // 2 % 2, me % 2
     source = lax.broadcasted_iota(jnp.int32, (width, width), 0)
     target = lax.broadcasted_iota(jnp.int32, (width, width), 1)
     block = source // 256
     place = (
         (source % 256 // 16) * 64
-        + jnp.bitwise_xor(block % 2, half) * 32
+        + jnp.bitwise_xor(block % 2, odd) * 32
         + jnp.bitwise_xor(block // 2, core) * 16
         + source % 16
     )

time: 178 us -> 160 us (0.90)
  the two profiles are of different devices: /device:TPU:2 before, /device:TPU:8 now
where the time goes in v1:
time: 160 us; the launch traced here: 159 us
  starting transfers between devices  52.7 us (33%)
  blocking collectives  40.2 us (25%)
  waiting for transfers between devices  24.8 us (16%)
  Pallas kernels  21.6 us (14%)
  local copies, waits for them, and re-layouts  11.6 us (7%)
  matrix products  4.62 us (3%)
  other arithmetic  2.71 us (2%)
    all_to_all x2, starting transfers between devices, row_exchange(): lax.all_to_all(x, 'shot', split_axis=0, concat_axis=0, tiled=True, axis_i...  20.5 us
    all_to_all x1, blocking collectives, row_exchange(): lax.all_to_all(x, 'shot', split_axis=0, concat_axis=0, tiled=True, axis_i...  15.3 us
    pallas_call x1, Pallas kernels, stencil(): pl.pallas_call(stencil_kernel, out_shape=(jax.ShapeDtypeStruct(now.shape,...  14.8 us
    all_to_all x1, blocking collectives, block(): lax.all_to_all(partial.reshape(4, 512, 128), 'tx', 0, 0, tiled=True)  14.1 us
    all_to_all x1, blocking collectives, block(): summed = jnp.sum(lax.all_to_all(partial, 'ty', 0, 0, tiled=True), axis=0)  10.8 us
    all_to_all x2, waiting for transfers between devices, row_exchange(): lax.all_to_all(x, 'shot', split_axis=0, concat_axis=0, tiled=True, axis_i...  9.91 us
    ppermute x1, starting transfers between devices, gathered_green(): other = lax.ppermute(green, 'shot', PAIR_SWAP)  7.71 us
    ppermute x1, waiting for transfers between devices, halo_blocks(): ym = lax.ppermute(ytail, 'ty', UP)  7.19 us
  transfers between devices with their start and end apart: 12, of which 4 were waited for; matrix products, arithmetic and copies ran while one was open for 8% of the time, Pallas kernels for 9%

profile of v1, /device:TPU:8, one launch (start us, length us, event | category | flops | bytes accessed | tf_op | source)
XLA Modules:
  0.0 159.2 jit_solution(8583710181927866836)
XLA Ops:
  0.6 7.7 %collective-permute-start.8 = (bf16[2,512,256]{2,1,0:T(8,128)(2,1)}, bf16[2,512,256]{2,1,0:T(8,128)(2,1)}, u32[]{:S(2)}, u32[]{:S(2)}) collective-permute-start(bf16[2,512,256]{2,1,0:T(8,128)(2,1)} %param.14), channel_id=1, source_target_pairs={{0,32},{16,48},{32,0},{48,16},{64,96},{80,112},{96,64},{112,80},{1... | collective-permute-start | bytes 1572872 | tf_op jit(solution)/shard_map/ppermute | solution.py:299
  8.4 1.5 broadcast_in_dim.7
  9.9 10.2 %all-to-all-start = ((bf16[8,32,512]{2,1,0:T(8,128)(2,1)}), bf16[8,32,512]{2,1,0:T(8,128)(2,1)S(1)}, u32[]{:S(2)}, u32[]{:S(2)}) async-start(bf16[8,32,512]{2,1,0:T(8,128)(2,1)} %broadcast_in_dim.7), calls=%async_computation | async-start | bytes 524288 | tf_op jit(solution)/shard_map/all_to_all | solution.py:38
  23.2 3.4 %collective-permute-start = (f32[9,8,16,128]{3,2,1,0:T(8,128)S(1)}, f32[9,8,16,128]{3,2,1,0:T(8,128)S(1)}, u32[]{:S(2)}, u32[]{:S(2)}) collective-permute-start(f32[9,8,16,128]{3,2,1,0:T(8,128)S(1)} %get-tuple-element.12), channel_id=1, source_target_pairs={{0,4},{4,8},{8,12},{1,5},{5,9},{9,13},{2,6},{6,10},{10,14},{3,7},{... | collective-permute-start | bytes 1769480 | tf_op jit(solution)/shard_map/ppermute | solution.py:287
  26.6 1.3 collective-permute-start.1
  27.9 3.4 %collective-permute-start.2 = (f32[9,16,8,128]{3,2,1,0:T(8,128)S(1)}, f32[9,16,8,128]{3,2,1,0:T(8,128)S(1)}, u32[]{:S(2)}, u32[]{:S(2)}) collective-permute-start(f32[9,16,8,128]{3,2,1,0:T(8,128)S(1)} %get-tuple-element.14), channel_id=1, source_target_pairs={{0,1},{1,2},{2,3},{4,5},{5,6},{6,7},{8,9},{9,10},{10,11},{12,13},{... | collective-permute-start | bytes 1769480 | tf_op jit(solution)/shard_map/ppermute | solution.py:288
  31.4 1.3 collective-permute-start.3
  32.7 2.3 %pad_maximum_fusion = bf16[2,512,512]{2,1,0:T(8,128)(2,1)} fusion(bf16[2,512,256]{2,1,0:T(8,128)(2,1)} %collective-permute-done.8, bf16[2,512,256]{2,1,0:T(8,128)(2,1)} %param.14), kind=kLoop, calls=%fused_computation.60 | loop fusion | flops 2097152 | bytes 2097152 | tf_op jit(solution)/shard_map/concatenate | solution.py:300
  35.1 1.9 %collective-permute-start.9 = (bf16[2,512,512]{2,1,0:T(8,128)(2,1)}, bf16[2,512,512]{2,1,0:T(8,128)(2,1)}, u32[]{:S(2)}, u32[]{:S(2)}) collective-permute-start(bf16[2,512,512]{2,1,0:T(8,128)(2,1)} %pad_maximum_fusion), channel_id=1, source_target_pairs={{0,16},{16,0},{32,48},{48,32},{64,80},{80,64},{96,112},{112,96},{1... | collective-permute-start | bytes 3145736 | tf_op jit(solution)/shard_map/ppermute | solution.py:301
  37.2 7.2 %collective-permute-done.2.ym = f32[9,16,8,128]{3,2,1,0:T(8,128)S(1)} collective-permute-done((f32[9,16,8,128]{3,2,1,0:T(8,128)S(1)}, f32[9,16,8,128]{3,2,1,0:T(8,128)S(1)}, u32[]{:S(2)}, u32[]{:S(2)}) %collective-permute-start.2) | collective-permute-done | bytes 589856 | tf_op jit(solution)/shard_map/ppermute | solution.py:288
  45.1 4.9 %collective-permute-start.4 = (f32[9,8,8,128]{3,2,1,0:T(8,128)}, f32[9,8,8,128]{3,2,1,0:T(8,128)}, u32[]{:S(2)}, u32[]{:S(2)}) collective-permute-start(f32[9,8,8,128]{3,2,1,0:T(8,128)} %slice.16), channel_id=1, source_target_pairs={{0,4},{4,8},{8,12},{1,5},{5,9},{9,13},{2,6},{6,10},{10,14},{3,7},{... | collective-permute-start | bytes 884744 | tf_op jit(solution)/shard_map/ppermute | solution.py:291
  50.7 1.3 collective-permute-start.5
  52.8 5.7 %collective-permute-start.6 = (f32[9,8,8,128]{3,2,1,0:T(8,128)}, f32[9,8,8,128]{3,2,1,0:T(8,128)}, u32[]{:S(2)}, u32[]{:S(2)}) collective-permute-start(f32[9,8,8,128]{3,2,1,0:T(8,128)} %slice.18), channel_id=1, source_target_pairs={{0,1},{1,2},{2,3},{4,5},{5,6},{6,7},{8,9},{9,10},{10,11},{12,13},{... | collective-permute-start | bytes 884744 | tf_op jit(solution)/shard_map/ppermute | solution.py:292
  60.1 1.3 collective-permute-start.7
  62.9 6.4 %collective-permute-done.7.cpp = f32[9,8,8,128]{3,2,1,0:T(8,128)} collective-permute-done((f32[9,8,8,128]{3,2,1,0:T(8,128)}, f32[9,8,8,128]{3,2,1,0:T(8,128)}, u32[]{:S(2)}, u32[]{:S(2)}) %collective-permute-start.7) | collective-permute-done | bytes 294944 | tf_op jit(solution)/shard_map/ppermute | solution.py:293
  70.3 14.8 %stencil.1 = (f32[4,16,16,128]{3,2,1,0:T(8,128)S(1)}, f32[4,16,16,128]{3,2,1,0:T(8,128)}, bf16[32,512]{1,0:T(8,128)(2,1)S(1)}) custom-call(f32[4,16,16,128]{3,2,1,0:T(8,128)S(1)} %copy-done.1, f32[4,16,16,128]{3,2,1,0:T(8,128)S(1)} %copy-done.3, f32[16,16,128]{2,1,0:T(8,128)S(1)} %copy-done.7, f32[9,8,16,128]{3,2,1,0:T(8,128)S(1)} %collective-permute-done.xm, ...), custom_call_target="tpu_custom_call" | custom-call | flops 2000000000 | bytes 12000000 | tf_op jit(solution)/shard_map/stencil/pallas_call | solution.py:132
  86.7 10.3 %all-to-all-start.1 = ((bf16[8,32,512]{2,1,0:T(8,128)(2,1)}), bf16[8,32,512]{2,1,0:T(8,128)(2,1)S(1)}, u32[]{:S(2)}, u32[]{:S(2)}) async-start(bf16[8,32,512]{2,1,0:T(8,128)(2,1)} %broadcast_in_dim.8), calls=%async_computation.1 | async-start | bytes 524288 | tf_op jit(solution)/shard_map/all_to_all | solution.py:38
  96.9 4.6 %fusion.18.green = bf16[2,512,1024]{2,1,0:T(8,128)(2,1)S(1)} fusion(bf16[2,512,512]{2,1,0:T(8,128)(2,1)} %collective-permute-done.9, bf16[2,512,256]{2,1,0:T(8,128)(2,1)} %collective-permute-done.8, bf16[2,512,256]{2,1,0:T(8,128)(2,1)} %param.14, s32[1024]{0:T(1024)S(1)} %get-tuple-element.30, s32[1024]{0:T(1024)S(1)} %get-tuple-element.31, ...), kind=kOutput, calls=%fused_computation.33 | convolution fusion | flops 2202009600 | bytes 4221960 | tf_op jit(solution)/shard_map/lrc,cd->lrd/dot_general | solution.py:316
  101.6 9.9 %all-to-all-done.1.new = bf16[8,32,512]{2,1,0:T(8,128)(2,1)S(1)} async-done(((bf16[8,32,512]{2,1,0:T(8,128)(2,1)}), bf16[8,32,512]{2,1,0:T(8,128)(2,1)S(1)}, u32[]{:S(2)}, u32[]{:S(2)}) %all-to-all-start.1) | async-done | bytes 262176 | tf_op jit(solution)/shard_map/all_to_all | solution.py:38
  111.5 1.8 %columns.1 = f32[16,128,128]{2,1,0:T(8,128)S(1)} custom-call(s32[2]{0:T(128)S(1)} %copy-done.10, bf16[8,32,512]{2,1,0:T(8,128)(2,1)S(1)} %all-to-all-done.old, bf16[8,32,512]{2,1,0:T(8,128)(2,1)S(1)} %all-to-all-done.1.new, bf16[2,512,1024]{2,1,0:T(8,128)(2,1)S(1)} %fusion.18.green), custom_call_target="tpu_custom_call" | custom-call | flops 1000000000 | bytes 4000000 | tf_op jit(solution)/shard_map/columns/pallas_call | solution.py:188
  113.3 14.1 %all_to_all.25 = f32[4,512,128]{2,1,0:T(8,128)S(1)} all-to-all(f32[4,512,128]{2,1,0:T(8,128)S(1)} %bitcast.12), channel_id=1, replica_groups=mesh['shot'=32,'tx'=4,'ty'=4] {'tx'}, dimensions={0} | all-to-all | bytes 2097152 | tf_op jit(solution)/shard_map/all_to_all | solution.py:336
  127.5 10.8 %all_to_all.26 = f32[4,128,128]{2,1,0:T(8,128)S(1)} all-to-all(f32[4,128,128]{2,1,0:T(8,128)S(1)} %bitcast.16), channel_id=1, replica_groups=mesh['shot'=32,'tx'=4,'ty'=4] {'ty'}, dimensions={0} | all-to-all | bytes 524288 | tf_op jit(solution)/shard_map/all_to_all | solution.py:338
  138.3 15.3 %all_to_all.27.em = f32[8,16,128]{2,1,0:T(8,128)S(1)} all-to-all(f32[8,16,128]{2,1,0:T(8,128)S(1)} %bitcast.17), channel_id=1, replica_groups={{0,64,128,192,256,320,384,448},{16,80,144,208,272,336,400,464},{32,96,1..., dimensions={0} | all-to-all | bytes 131072 | tf_op jit(solution)/shard_map/all_to_all | solution.py:38
  153.6 4.9 %inject.1 = (f32[4,16,16,128]{3,2,1,0:T(8,128)}, f32[32,512]{1,0:T(8,128)S(1)}) custom-call(f32[8,16,128]{2,1,0:T(8,128)S(1)} %all_to_all.27.em, s32[8,512]{1,0:T(8,128)S(1)} %bitcast.14, f32[8,512]{1,0:T(8,128)S(1)} %bitcast.15, f32[4,16,16,128]{3,2,1,0:T(8,128)S(1)} %copy-done.12), custom_call_target="tpu_custom_call" | custom-call | flops 4000000000 | bytes 4000000 | tf_op jit(solution)/shard_map/inject/pallas_call | solution.py:237
  (54 shorter events, 11.9 us)
Async XLA Ops:
  0.6 36.4 %copy-start.13 = (s32[1,1,512]{2,1,0:T(1,128)S(1)}, s32[1,1,512]{2,1,0:T(1,128)}, u32[]{:S(2)}) copy-start(s32[1,1,512]{2,1,0:T(1,128)} %param.12) | copy-start | bytes 6148
  0.6 32.1 %collective-permute-start.8 = (bf16[2,512,256]{2,1,0:T(8,128)(2,1)}, bf16[2,512,256]{2,1,0:T(8,128)(2,1)}, u32[]{:S(2)}, u32[]{:S(2)}) collective-permute-start(bf16[2,512,256]{2,1,0:T(8,128)(2,1)} %param.14), channel_id=1, source_target_pairs={{0,32},{16,48},{32,0},{48,16},{64,96},{80,112},{96,64},{112,80},{1... | collective-permute-start | bytes 1572872 | tf_op jit(solution)/shard_map/ppermute | solution.py:299
  9.9 76.1 %all-to-all-start = ((bf16[8,32,512]{2,1,0:T(8,128)(2,1)}), bf16[8,32,512]{2,1,0:T(8,128)(2,1)S(1)}, u32[]{:S(2)}, u32[]{:S(2)}) async-start(bf16[8,32,512]{2,1,0:T(8,128)(2,1)} %broadcast_in_dim.7), calls=%async_computation | async-start | bytes 524288 | tf_op jit(solution)/shard_map/all_to_all | solution.py:38
  20.1 1.0 copy-start
  21.1 1.0 copy-start.2
  22.1 0.9 copy-start.6
  23.2 26.8 %collective-permute-start = (f32[9,8,16,128]{3,2,1,0:T(8,128)S(1)}, f32[9,8,16,128]{3,2,1,0:T(8,128)S(1)}, u32[]{:S(2)}, u32[]{:S(2)}) collective-permute-start(f32[9,8,16,128]{3,2,1,0:T(8,128)S(1)} %get-tuple-element.12), channel_id=1, source_target_pairs={{0,4},{4,8},{8,12},{1,5},{5,9},{9,13},{2,6},{6,10},{10,14},{3,7},{... | collective-permute-start | bytes 1769480 | tf_op jit(solution)/shard_map/ppermute | solution.py:287
  26.6 25.4 %collective-permute-start.1 = (f32[9,8,16,128]{3,2,1,0:T(8,128)S(1)}, f32[9,8,16,128]{3,2,1,0:T(8,128)S(1)}, u32[]{:S(2)}, u32[]{:S(2)}) collective-permute-start(f32[9,8,16,128]{3,2,1,0:T(8,128)S(1)} %get-tuple-element.13), channel_id=1, source_target_pairs={{4,0},{8,4},{12,8},{5,1},{9,5},{13,9},{6,2},{10,6},{14,10},{7,3},{... | collective-permute-start | bytes 1769480 | tf_op jit(solution)/shard_map/ppermute | solution.py:289
  27.9 16.4 %collective-permute-start.2 = (f32[9,16,8,128]{3,2,1,0:T(8,128)S(1)}, f32[9,16,8,128]{3,2,1,0:T(8,128)S(1)}, u32[]{:S(2)}, u32[]{:S(2)}) collective-permute-start(f32[9,16,8,128]{3,2,1,0:T(8,128)S(1)} %get-tuple-element.14), channel_id=1, source_target_pairs={{0,1},{1,2},{2,3},{4,5},{5,6},{6,7},{8,9},{9,10},{10,11},{12,13},{... | collective-permute-start | bytes 1769480 | tf_op jit(solution)/shard_map/ppermute | solution.py:288
  31.4 27.2 %collective-permute-start.3 = (f32[9,16,8,128]{3,2,1,0:T(8,128)S(1)}, f32[9,16,8,128]{3,2,1,0:T(8,128)S(1)}, u32[]{:S(2)}, u32[]{:S(2)}) collective-permute-start(f32[9,16,8,128]{3,2,1,0:T(8,128)S(1)} %get-tuple-element.15), channel_id=1, source_target_pairs={{1,0},{2,1},{3,2},{5,4},{6,5},{7,6},{9,8},{10,9},{11,10},{13,12},{... | collective-permute-start | bytes 1769480 | tf_op jit(solution)/shard_map/ppermute | solution.py:290
  32.7 36.5 %copy-start.1 = (f32[4,16,16,128]{3,2,1,0:T(8,128)S(1)}, f32[4,16,16,128]{3,2,1,0:T(8,128)}, u32[]{:S(2)}) copy-start(f32[4,16,16,128]{3,2,1,0:T(8,128)} %now.3) | copy-start | bytes 1572868
  32.7 36.5 %copy-start.3 = (f32[4,16,16,128]{3,2,1,0:T(8,128)S(1)}, f32[4,16,16,128]{3,2,1,0:T(8,128)}, u32[]{:S(2)}) copy-start(f32[4,16,16,128]{3,2,1,0:T(8,128)} %prev.3) | copy-start | bytes 1572868
  32.7 36.5 %copy-start.7 = (f32[16,16,128]{2,1,0:T(8,128)S(1)}, f32[16,16,128]{2,1,0:T(8,128)}, u32[]{:S(2)}) copy-start(f32[16,16,128]{2,1,0:T(8,128)} %speed_in.1) | copy-start | bytes 393220
  35.1 61.9 %collective-permute-start.9 = (bf16[2,512,512]{2,1,0:T(8,128)(2,1)}, bf16[2,512,512]{2,1,0:T(8,128)(2,1)}, u32[]{:S(2)}, u32[]{:S(2)}) collective-permute-start(bf16[2,512,512]{2,1,0:T(8,128)(2,1)} %pad_maximum_fusion), channel_id=1, source_target_pairs={{0,16},{16,0},{32,48},{48,32},{64,80},{80,64},{96,112},{112,96},{1... | collective-permute-start | bytes 3145736 | tf_op jit(solution)/shard_map/ppermute | solution.py:301
  45.1 16.5 %collective-permute-start.4 = (f32[9,8,8,128]{3,2,1,0:T(8,128)}, f32[9,8,8,128]{3,2,1,0:T(8,128)}, u32[]{:S(2)}, u32[]{:S(2)}) collective-permute-start(f32[9,8,8,128]{3,2,1,0:T(8,128)} %slice.16), channel_id=1, source_target_pairs={{0,4},{4,8},{8,12},{1,5},{5,9},{9,13},{2,6},{6,10},{10,14},{3,7},{... | collective-permute-start | bytes 884744 | tf_op jit(solution)/shard_map/ppermute | solution.py:291
  50.7 10.8 %collective-permute-start.5 = (f32[9,8,8,128]{3,2,1,0:T(8,128)}, f32[9,8,8,128]{3,2,1,0:T(8,128)}, u32[]{:S(2)}, u32[]{:S(2)}) collective-permute-start(f32[9,8,8,128]{3,2,1,0:T(8,128)} %slice.17), channel_id=1, source_target_pairs={{1,0},{2,1},{3,2},{5,4},{6,5},{7,6},{9,8},{10,9},{11,10},{13,12},{... | collective-permute-start | bytes 884744 | tf_op jit(solution)/shard_map/ppermute | solution.py:294
  52.8 10.1 %collective-permute-start.6 = (f32[9,8,8,128]{3,2,1,0:T(8,128)}, f32[9,8,8,128]{3,2,1,0:T(8,128)}, u32[]{:S(2)}, u32[]{:S(2)}) collective-permute-start(f32[9,8,8,128]{3,2,1,0:T(8,128)} %slice.18), channel_id=1, source_target_pairs={{0,1},{1,2},{2,3},{4,5},{5,6},{6,7},{8,9},{9,10},{10,11},{12,13},{... | collective-permute-start | bytes 884744 | tf_op jit(solution)/shard_map/ppermute | solution.py:292
  60.1 9.2 %collective-permute-start.7 = (f32[9,8,8,128]{3,2,1,0:T(8,128)}, f32[9,8,8,128]{3,2,1,0:T(8,128)}, u32[]{:S(2)}, u32[]{:S(2)}) collective-permute-start(f32[9,8,8,128]{3,2,1,0:T(8,128)} %slice.19), channel_id=1, source_target_pairs={{4,0},{8,4},{12,8},{5,1},{9,5},{13,9},{6,2},{10,6},{14,10},{7,3},{... | collective-permute-start | bytes 884744 | tf_op jit(solution)/shard_map/ppermute | solution.py:293
  69.3 1.1 copy-start.5
  86.7 24.8 %all-to-all-start.1 = ((bf16[8,32,512]{2,1,0:T(8,128)(2,1)}), bf16[8,32,512]{2,1,0:T(8,128)(2,1)S(1)}, u32[]{:S(2)}, u32[]{:S(2)}) async-start(bf16[8,32,512]{2,1,0:T(8,128)(2,1)} %broadcast_in_dim.8), calls=%async_computation.1 | async-start | bytes 524288 | tf_op jit(solution)/shard_map/all_to_all | solution.py:38
  96.9 14.6 %copy-start.10 = (s32[2]{0:T(128)S(1)}, s32[2]{0:T(128)}, u32[]{:S(2)}) copy-start(s32[2]{0:T(128)} %delay.1) | copy-start | bytes 28
  113.3 40.4 %copy-start.8 = (s32[1,1,8,512]{3,2,1,0:T(8,128)S(1)}, s32[1,1,8,512]{3,2,1,0:T(8,128)}, u32[]{:S(2)}) copy-start(s32[1,1,8,512]{3,2,1,0:T(8,128)} %param.16) | copy-start | bytes 49156
  113.3 40.3 %copy-start.9 = (f32[1,1,8,512]{3,2,1,0:T(8,128)S(1)}, f32[1,1,8,512]{3,2,1,0:T(8,128)}, u32[]{:S(2)}) copy-start(f32[1,1,8,512]{3,2,1,0:T(8,128)} %param.17) | copy-start | bytes 49156
  113.3 40.3 %copy-start.12 = (f32[4,16,16,128]{3,2,1,0:T(8,128)S(1)}, f32[4,16,16,128]{3,2,1,0:T(8,128)}, u32[]{:S(2)}) copy-start(f32[4,16,16,128]{3,2,1,0:T(8,128)} %copy-done.11) | copy-start | bytes 1572868
  (2 other events, 1.6 us)

commit v2 on v1

--- a/solution.py
+++ b/solution.py
@@ -24,6 +24,7 @@
 
 SHOT_COORDS = [(h, r, c) for h in range(2) for r in range(8) for c in range(2)]
 CORE_SWAP = [(shot_id(h, r, c), shot_id(h, r, 1 - c)) for h, r, c in SHOT_COORDS]
+DIAG_SWAP = [(shot_id(h, r, c), shot_id(h, r ^ 1, 1 - c)) for h, r, c in SHOT_COORDS]
 PAIR_SWAP = [(shot_id(h, r, c), shot_id(h, r ^ 1, c)) for h, r, c in SHOT_COORDS]
 ROW_GROUPS = [
     [shot_id(h, 2 * k + odd, c) for h in range(2) for k in range(4)]
@@ -34,6 +35,10 @@
 DOWN = [(i + 1, i) for i in range(3)]
 
 
+def in_hbm(*arrays):
+    return tuple(pltpu.with_memory_space_constraint(x, pltpu.HBM) for x in arrays)
+
+
 def row_exchange(x):
     return lax.all_to_all(
         x, "shot", split_axis=0, concat_axis=0, tiled=True, axis_index_groups=ROW_GROUPS
@@ -45,7 +50,7 @@
 
 
 def stencil_kernel(
-    now, prev, speed_in, xm, xp, ym, yp, cmm, cmp, cpm, cpp, rows_hot, lanes_hot,
+    now, prev, speed_in, xm, xp, ym, yp, cmm, cmp, cpm, cpp, rows_hot, lanes_hot, history,
     next_out, last_out, rec_out, cur, prv, spd, sems, out_sems,
 ):
     shots = now.shape[0]
@@ -114,7 +119,8 @@
             picked = (picked * mask).astype(BF16)
             sel = (sel_row == (sel_col // DEPTH) * STEPS + (step - 1)).astype(F32).astype(BF16)
             records = records + lax.dot_general(sel, picked, NT, preferred_element_type=F32)
-    rec_out[...] = records.astype(BF16)
+    rec_out[pl.ds(0, shots * HIST), :] = history[...]
+    rec_out[pl.ds(shots * HIST, shots * STEPS), :] = records.astype(BF16)
     out_next = pltpu.make_async_copy(bufs[STEPS % 2].at[:, mid, ymid], next_out, out_sems.at[0])
     out_last = pltpu.make_async_copy(bufs[(STEPS - 1) % 2].at[:, mid, ymid], last_out, out_sems.at[1])
     out_next.start()
@@ -123,21 +129,22 @@
     out_last.wait()
 
 
-def stencil(now, prev, speed, halos, rows_hot, lanes_hot):
+def stencil(now, prev, speed, halos, rows_hot, lanes_hot, history):
     shots = now.shape[0]
     points = rows_hot.shape[0]
     anywhere = pl.BlockSpec(memory_space=pl.ANY)
     vmem = pl.BlockSpec(memory_space=pltpu.VMEM)
+    hbm = pl.BlockSpec(memory_space=pltpu.HBM)
     wide = (shots, WIDE, WIDE + 2 * PAD, DEPTH)
     return pl.pallas_call(
         stencil_kernel,
         out_shape=(
             jax.ShapeDtypeStruct(now.shape, F32),
             jax.ShapeDtypeStruct(now.shape, F32),
-            jax.ShapeDtypeStruct((shots * STEPS, points), BF16),
+            jax.ShapeDtypeStruct((shots * (HIST + STEPS), points), BF16),
         ),
-        in_specs=[anywhere] * 11 + [vmem] * 2,
-        out_specs=(anywhere, anywhere, vmem),
+        in_specs=[hbm] * 3 + [anywhere] * 8 + [vmem] * 3,
+        out_specs=(hbm, hbm, vmem),
         scratch_shapes=[
             pltpu.VMEM(wide, F32),
             pltpu.VMEM(wide, F32),
@@ -148,11 +155,12 @@
         compiler_params=pltpu.CompilerParams(vmem_limit_bytes=16 << 20),
         cost_estimate=pl.CostEstimate(flops=2_000_000_000, bytes_accessed=12_000_000, transcendentals=0),
         name="stencil",
-    )(now, prev, speed, *halos, rows_hot, lanes_hot)
-
-
-def columns_kernel(delay, old, new, green, out):
-    groups, rows, _ = old.shape
+    )(*in_hbm(now, prev, speed), *halos, rows_hot, lanes_hot, history)
+
+
+def columns_kernel(delay, records, green, out):
+    groups, rows, _ = records.shape
+    rows = rows // 2
     half = rows // 2
     lags = green.shape[0]
     width = green.shape[2]
@@ -160,7 +168,7 @@
     sel_col = lax.broadcasted_iota(jnp.int32, (half, 2 * rows), 1)
     col_shot = (sel_col % rows) // STEPS
     col_time = (sel_col // rows) * HIST + sel_col % STEPS
-    both = [jnp.concatenate([old[g], new[g]], axis=0) for g in range(groups)]
+    both = [records[g] for g in range(groups)]
     parts = []
     for h in range(2):
         row_shot = sel_row // STEPS + h * (half // STEPS)
@@ -183,20 +191,20 @@
         out[2 * m + 1] = jnp.where(lane < 64, pltpu.roll(a, 64, 1), b)
 
 
-def columns(delay, old, new, green):
+def columns(delay, records, green):
     vmem = pl.BlockSpec(memory_space=pltpu.VMEM)
     return pl.pallas_call(
         columns_kernel,
         out_shape=jax.ShapeDtypeStruct((16, 128, 128), F32),
-        in_specs=[pl.BlockSpec(memory_space=pltpu.SMEM), vmem, vmem, vmem],
+        in_specs=[pl.BlockSpec(memory_space=pltpu.SMEM), vmem, vmem],
         out_specs=vmem,
         compiler_params=pltpu.CompilerParams(vmem_limit_bytes=12 << 20),
         cost_estimate=pl.CostEstimate(flops=1_000_000_000, bytes_accessed=4_000_000, transcendentals=0),
         name="columns",
-    )(delay, old, new, green)
-
-
-def inject_kernel(em, cells, weights, field, wave_out, emission, rhs_high, rhs_low, acc):
+    )(delay, records, green)
+
+
+def inject_kernel(em, cells, weights, field, wave_out, emission_out, rhs_high, rhs_low, acc, emission):
     shots = field.shape[0]
     points = cells.shape[1]
     lane = lax.broadcasted_iota(jnp.int32, (16, 128), 1)
@@ -226,6 +234,8 @@
         return carry
 
     lax.fori_loop(0, cells.shape[0], body, 0)
+    for row in range(shots * STEPS):
+        emission_out[row] = emission[pl.ds(row, 1), :]
     for s in range(shots):
         wave_out[s] = field[s] + acc[:, s * DEPTH : (s + 1) * DEPTH].reshape(TILE, TILE, DEPTH)
 
@@ -238,7 +248,7 @@
         inject_kernel,
         out_shape=(
             jax.ShapeDtypeStruct(field.shape, F32),
-            jax.ShapeDtypeStruct((shots * STEPS, points), F32),
+            jax.ShapeDtypeStruct((shots * STEPS, 1, points), F32),
         ),
         in_specs=[vmem] * 4,
         out_specs=(vmem, vmem),
@@ -246,6 +256,7 @@
             pltpu.VMEM((shots * DEPTH, points), BF16),
             pltpu.VMEM((shots * DEPTH, points), BF16),
             pltpu.VMEM((TILE * TILE, shots * DEPTH), F32),
+            pltpu.VMEM((shots * STEPS, points), F32),
         ],
         compiler_params=pltpu.CompilerParams(vmem_limit_bytes=12 << 20),
         cost_estimate=pl.CostEstimate(flops=4_000_000_000, bytes_accessed=4_000_000, transcendentals=0),
@@ -253,16 +264,22 @@
     )(em, cells, weights, field)
 
 
-def pack_kernel(now, prev, speed, xtail, ytail, xhead, yhead):
+def pack_kernel(now, prev, speed, xtail, ytail, xhead, yhead, field, sems):
     shots = now.shape[0]
+    copies = [
+        pltpu.make_async_copy(now, field.at[pl.ds(0, shots)], sems.at[0]),
+        pltpu.make_async_copy(prev, field.at[pl.ds(shots, shots)], sems.at[1]),
+        pltpu.make_async_copy(speed, field.at[2 * shots], sems.at[2]),
+    ]
+    for copy in copies:
+        copy.start()
+    for copy in copies:
+        copy.wait()
     head, tail = slice(0, BAND), slice(TILE - BAND, TILE)
-    for out, xs, ys in (
-        (xtail, tail, slice(None)), (ytail, slice(None), tail),
-        (xhead, head, slice(None)), (yhead, slice(None), head),
-    ):
-        out[pl.ds(0, shots)] = now[:, xs, ys]
-        out[pl.ds(shots, shots)] = prev[:, xs, ys]
-        out[2 * shots] = speed[xs, ys]
+    xtail[...] = field[:, tail]
+    ytail[...] = field[:, :, tail]
+    xhead[...] = field[:, head]
+    yhead[...] = field[:, :, head]
 
 
 def packed(now, prev, speed):
@@ -273,12 +290,16 @@
     return pl.pallas_call(
         pack_kernel,
         out_shape=(across, along, across, along),
-        in_specs=[vmem] * 3,
+        in_specs=[pl.BlockSpec(memory_space=pltpu.HBM)] * 3,
         out_specs=(vmem,) * 4,
+        scratch_shapes=[
+            pltpu.VMEM((fields, TILE, TILE, DEPTH), F32),
+            pltpu.SemaphoreType.DMA((3,)),
+        ],
         compiler_params=pltpu.CompilerParams(vmem_limit_bytes=8 << 20),
         cost_estimate=pl.CostEstimate(flops=0, bytes_accessed=4_000_000, transcendentals=0),
         name="pack",
-    )(now, prev, speed)
+    )(*in_hbm(now, prev, speed))
 
 
 def halo_blocks(now, prev, speed):
@@ -295,25 +316,62 @@
     return xm, xp, ym, yp, cmm, cmp, cpm, cpp
 
 
+def order_kernel(place, own_in, pair_in, core_in, diag_in, out, own, pair, core, diag, sems):
+    copies = [
+        pltpu.make_async_copy(src, dst, sems.at[i])
+        for i, (src, dst) in enumerate(
+            ((own_in, own), (pair_in, pair), (core_in, core), (diag_in, diag))
+        )
+    ]
+    for copy in copies:
+        copy.start()
+    for copy in copies:
+        copy.wait()
+    lags, _, width = own.shape
+    source = lax.broadcasted_iota(jnp.int32, (256, 512), 0)
+    target = lax.broadcasted_iota(jnp.int32, (256, 512), 1)
+    local = source % 128
+    other_row = source // 128
+    for lag in range(lags):
+        for m in range(width // 128):
+            cut = pl.ds(m * 128, 128)
+            total = None
+            for other_core, (a, b) in enumerate(((own, pair), (core, diag))):
+                spot = (
+                    (local // 16) * 64
+                    + jnp.bitwise_xor(other_row, place[0]) * 32
+                    + jnp.bitwise_xor(other_core, place[1]) * 16
+                    + local % 16
+                )
+                hot = (spot == target).astype(F32).astype(BF16)
+                both = jnp.concatenate([a[lag, :, cut], b[lag, :, cut]], axis=1)
+                term = jnp.dot(both, hot, preferred_element_type=F32)
+                total = term if total is None else total + term
+            out[lag, :, pl.ds(m * 512, 512)] = total.astype(BF16)
+
+
 def gathered_green(green):
-    other = lax.ppermute(green, "shot", PAIR_SWAP)
-    mine = jnp.concatenate([green, other], -1)
-    theirs = lax.ppermute(mine, "shot", CORE_SWAP)
-    blocks = jnp.concatenate([mine, theirs], -1)
-    width = blocks.shape[-1]
+    def moved(pairs):
+        return lax.ppermute(green, "shot", pairs)
+
+    core = moved(CORE_SWAP)
+    pair = moved(PAIR_SWAP)
+    diag = moved(DIAG_SWAP)
     me = lax.axis_index("shot")
-    odd, core = me // 2 % 2, me % 2
-    source = lax.broadcasted_iota(jnp.int32, (width, width), 0)
-    target = lax.broadcasted_iota(jnp.int32, (width, width), 1)
-    block = source // 256
-    place = (
-        (source % 256 // 16) * 64
-        + jnp.bitwise_xor(block % 2, odd) * 32
-        + jnp.bitwise_xor(block // 2, core) * 16
-        + source % 16
-    )
-    order = (place == target).astype(BF16)
-    return jnp.einsum("lrc,cd->lrd", blocks, order, preferred_element_type=BF16)
+    place = jnp.stack([me // 2 % 2, me % 2]).astype(jnp.int32)
+    lags, points, width = green.shape
+    vmem = pl.BlockSpec(memory_space=pltpu.VMEM)
+    return pl.pallas_call(
+        order_kernel,
+        out_shape=jax.ShapeDtypeStruct((lags, points, 4 * width), BF16),
+        in_specs=[pl.BlockSpec(memory_space=pltpu.SMEM)]
+        + [pl.BlockSpec(memory_space=pltpu.HBM)] * 4,
+        out_specs=vmem,
+        scratch_shapes=[pltpu.VMEM(green.shape, BF16)] * 4 + [pltpu.SemaphoreType.DMA((4,))],
+        compiler_params=pltpu.CompilerParams(vmem_limit_bytes=12 << 20),
+        cost_estimate=pl.CostEstimate(flops=1_000_000_000, bytes_accessed=4_000_000, transcendentals=0),
+        name="order",
+    )(place, *in_hbm(green, pair, core, diag))
 
 
 def block(
@@ -328,11 +386,12 @@
         jnp.bitwise_and(receivers, DEPTH - 1)[:, None] == jnp.arange(DEPTH)[None, :]
     ).astype(F32)
     halos = halo_blocks(wave_now, wave_prev, courant)
-    old_all = spread_rows(rec_history.reshape(shots * HIST, -1))
     wide_green = gathered_green(green)
-    field, wave_last, new_here = stencil(wave_now, wave_prev, courant, halos, rows_hot, lanes_hot)
-    new_all = spread_rows(new_here)
-    partial = columns(lag_delay, old_all, new_all, wide_green)
+    field, wave_last, records = stencil(
+        wave_now, wave_prev, courant, halos, rows_hot, lanes_hot, rec_history.reshape(shots * HIST, -1)
+    )
+    records = spread_rows(records)
+    partial = columns(lag_delay, records, wide_green)
     partial = lax.all_to_all(partial.reshape(4, 512, 128), "tx", 0, 0, tiled=True)
     partial = jnp.sum(partial, axis=0).reshape(4, 128, 128)
     summed = jnp.sum(lax.all_to_all(partial, "ty", 0, 0, tiled=True), axis=0)

time: 160 us -> 166 us (1.038)
  blocking collectives: 40.2 us -> 56.4 us
  waiting for transfers between devices: 24.8 us -> 37.2 us
  starting transfers between devices: 52.7 us -> 41.3 us
  local copies, waits for them, and re-layouts: 11.6 us -> 2.56 us
  matrix products: 4.62 us -> 0 us
  Pallas kernels: 21.6 us -> 26 us
    ppermute x2 -> x3, waiting for transfers between devices: 0.01 us -> 21.5 us  [moved(): return lax.ppermute(green, 'shot', pairs)]
    all_to_all x2 -> x1, waiting for transfers between devices: 9.91 us -> 0.01 us  [row_exchange(): lax.all_to_all(x, 'shot', split_axis=0, concat_axis=0, tiled=True, axis_i...]
    all_to_all x1, blocking collectives: 15.3 us -> 24.2 us  [row_exchange(): lax.all_to_all(x, 'shot', split_axis=0, concat_axis=0, tiled=True, axis_i...]
    all_to_all x2 -> x1, starting transfers between devices: 20.5 us -> 12.9 us  [row_exchange(): lax.all_to_all(x, 'shot', split_axis=0, concat_axis=0, tiled=True, axis_i...]
    all_to_all x1, blocking collectives: 14.1 us -> 19.4 us  [block(): lax.all_to_all(partial.reshape(4, 512, 128), 'tx', 0, 0, tiled=True)]
    unnamed x29 -> x14, local copies, waits for them, and re-layouts: 6.39 us -> 1.64 us
    dot_general x1 -> x0, matrix products: 4.62 us -> none  [gathered_green(): return jnp.einsum('lrc,cd->lrd', blocks, order, preferred_element_type=BF16)]
    pallas_call x0 -> x1, Pallas kernels: none -> 3.41 us  [gathered_green(): pl.pallas_call(order_kernel, out_shape=jax.ShapeDtypeStruct((lags, points...]
  transfers between devices with their start and end apart: 12 -> 12, of which waited for: 4 -> 8; matrix products, arithmetic and copies ran while one was open for 8% -> 1% of each run, Pallas kernels for 9% -> 2%
where the time goes in v2:
time: 166 us
  blocking collectives  56.4 us (34%)
  starting transfers between devices  41.3 us (25%)
  waiting for transfers between devices  37.2 us (22%)
  Pallas kernels  26 us (16%)
  local copies, waits for them, and re-layouts  2.56 us (2%)
    all_to_all x1, blocking collectives, row_exchange(): lax.all_to_all(x, 'shot', split_axis=0, concat_axis=0, tiled=True, axis_i...  24.2 us
    ppermute x3, waiting for transfers between devices, moved(): return lax.ppermute(green, 'shot', pairs)  21.5 us
    all_to_all x1, blocking collectives, block(): lax.all_to_all(partial.reshape(4, 512, 128), 'tx', 0, 0, tiled=True)  19.4 us
    pallas_call x1, Pallas kernels, stencil(): pl.pallas_call(stencil_kernel, out_shape=(jax.ShapeDtypeStruct(now.shape,...  14.5 us
    all_to_all x1, starting transfers between devices, row_exchange(): lax.all_to_all(x, 'shot', split_axis=0, concat_axis=0, tiled=True, axis_i...  12.9 us
    all_to_all x1, blocking collectives, block(): summed = jnp.sum(lax.all_to_all(partial, 'ty', 0, 0, tiled=True), axis=0)  12.8 us
    ppermute x3, starting transfers between devices, moved(): return lax.ppermute(green, 'shot', pairs)  7.87 us
    ppermute x1, waiting for transfers between devices, halo_blocks(): ym = lax.ppermute(ytail, 'ty', UP)  5.8 us
  transfers between devices with their start and end apart: 12, of which 8 were waited for; matrix products, arithmetic and copies ran while one was open for 1% of the time, Pallas kernels for 2%

profile of v2, /device:TPU:8, one launch (start us, length us, event | category | flops | bytes accessed | tf_op | source)
XLA Modules:
  0.0 165.5 jit_solution(5632780427500088853)
XLA Ops:
  0.6 1.4 pack.1
  2.1 4.3 %collective-permute-start.2 = (f32[9,16,8,128]{3,2,1,0:T(8,128)S(1)}, f32[9,16,8,128]{3,2,1,0:T(8,128)S(1)}, u32[]{:S(2)}, u32[]{:S(2)}) collective-permute-start(f32[9,16,8,128]{3,2,1,0:T(8,128)S(1)} %get-tuple-element.14), channel_id=1, source_target_pairs={{0,1},{1,2},{2,3},{4,5},{5,6},{6,7},{8,9},{9,10},{10,11},{12,13},{... | collective-permute-start | bytes 1769480 | tf_op jit(solution)/shard_map/ppermute | solution.py:309
  6.4 3.4 %collective-permute-start = (f32[9,8,16,128]{3,2,1,0:T(8,128)S(1)}, f32[9,8,16,128]{3,2,1,0:T(8,128)S(1)}, u32[]{:S(2)}, u32[]{:S(2)}) collective-permute-start(f32[9,8,16,128]{3,2,1,0:T(8,128)S(1)} %get-tuple-element.12), channel_id=1, source_target_pairs={{0,4},{4,8},{8,12},{1,5},{5,9},{9,13},{2,6},{6,10},{10,14},{3,7},{... | collective-permute-start | bytes 1769480 | tf_op jit(solution)/shard_map/ppermute | solution.py:308
  9.8 1.3 collective-permute-start.1
  11.1 1.3 collective-permute-start.3
  13.1 5.8 %collective-permute-done.2.ym = f32[9,16,8,128]{3,2,1,0:T(8,128)S(1)} collective-permute-done((f32[9,16,8,128]{3,2,1,0:T(8,128)S(1)}, f32[9,16,8,128]{3,2,1,0:T(8,128)S(1)}, u32[]{:S(2)}, u32[]{:S(2)}) %collective-permute-start.2) | collective-permute-done | bytes 589856 | tf_op jit(solution)/shard_map/ppermute | solution.py:309
  18.9 3.4 %collective-permute-start.4 = (f32[9,8,8,128]{3,2,1,0:T(8,128)S(1)}, f32[9,8,8,128]{3,2,1,0:T(8,128)S(1)}, u32[]{:S(2)}, u32[]{:S(2)}) collective-permute-start(f32[9,8,8,128]{3,2,1,0:T(8,128)S(1)} %slice.16), channel_id=1, source_target_pairs={{0,4},{4,8},{8,12},{1,5},{5,9},{9,13},{2,6},{6,10},{10,14},{3,7},{... | collective-permute-start | bytes 884744 | tf_op jit(solution)/shard_map/ppermute | solution.py:312
  24.0 2.2 %collective-permute-done.1.xp = f32[9,8,16,128]{3,2,1,0:T(8,128)S(1)} collective-permute-done((f32[9,8,16,128]{3,2,1,0:T(8,128)S(1)}, f32[9,8,16,128]{3,2,1,0:T(8,128)S(1)}, u32[]{:S(2)}, u32[]{:S(2)}) %collective-permute-start.1) | collective-permute-done | bytes 589856 | tf_op jit(solution)/shard_map/ppermute | solution.py:310
  26.2 4.3 %collective-permute-start.6 = (f32[9,8,8,128]{3,2,1,0:T(8,128)S(1)}, f32[9,8,8,128]{3,2,1,0:T(8,128)S(1)}, u32[]{:S(2)}, u32[]{:S(2)}) collective-permute-start(f32[9,8,8,128]{3,2,1,0:T(8,128)S(1)} %slice.18), channel_id=1, source_target_pairs={{0,1},{1,2},{2,3},{4,5},{5,6},{6,7},{8,9},{9,10},{10,11},{12,13},{... | collective-permute-start | bytes 884744 | tf_op jit(solution)/shard_map/ppermute | solution.py:313
  32.1 2.3 %collective-permute-done.5.cmp = f32[9,8,8,128]{3,2,1,0:T(8,128)S(1)} collective-permute-done((f32[9,8,8,128]{3,2,1,0:T(8,128)S(1)}, f32[9,8,8,128]{3,2,1,0:T(8,128)S(1)}, u32[]{:S(2)}, u32[]{:S(2)}) %collective-permute-start.5) | collective-permute-done | bytes 294944 | tf_op jit(solution)/shard_map/ppermute | solution.py:315
  35.3 4.2 %collective-permute-done.7.cpp = f32[9,8,8,128]{3,2,1,0:T(8,128)S(1)} collective-permute-done((f32[9,8,8,128]{3,2,1,0:T(8,128)S(1)}, f32[9,8,8,128]{3,2,1,0:T(8,128)S(1)}, u32[]{:S(2)}, u32[]{:S(2)}) %collective-permute-start.7) | collective-permute-done | bytes 294944 | tf_op jit(solution)/shard_map/ppermute | solution.py:314
  39.5 14.5 %stencil.1 = (f32[4,16,16,128]{3,2,1,0:T(8,128)S(1)}, f32[4,16,16,128]{3,2,1,0:T(8,128)}, bf16[64,512]{1,0:T(8,128)(2,1)S(1)}) custom-call(f32[4,16,16,128]{3,2,1,0:T(8,128)} %now.3, f32[4,16,16,128]{3,2,1,0:T(8,128)} %prev.3, f32[16,16,128]{2,1,0:T(8,128)} %speed_in.1, f32[9,8,16,128]{3,2,1,0:T(8,128)S(1)} %collective-permute-done.xm, ...), custom_call_target="tpu_custom_call" | custom-call | flops 2000000000 | bytes 12000000 | tf_op jit(solution)/shard_map/stencil/pallas_call | solution.py:139
  54.9 12.9 %all-to-all-start = ((bf16[8,64,512]{2,1,0:T(8,128)(2,1)}), bf16[8,64,512]{2,1,0:T(8,128)(2,1)S(1)}, u32[]{:S(2)}, u32[]{:S(2)}) async-start(bf16[8,64,512]{2,1,0:T(8,128)(2,1)} %broadcast_in_dim.2), calls=%async_computation | async-start | bytes 1048576 | tf_op jit(solution)/shard_map/all_to_all | solution.py:43
  67.7 3.3 %collective-permute-start.8 = (bf16[2,512,256]{2,1,0:T(8,128)(2,1)S(1)}, bf16[2,512,256]{2,1,0:T(8,128)(2,1)S(1)}, u32[]{:S(2)}, u32[]{:S(2)}) collective-permute-start(bf16[2,512,256]{2,1,0:T(8,128)(2,1)S(1)} %copy-done.4), channel_id=1, source_target_pairs={{0,32},{16,48},{32,0},{48,16},{64,96},{80,112},{96,64},{112,80},{1... | collective-permute-start | bytes 1572872 | tf_op jit(solution)/shard_map/ppermute | solution.py:355
  71.0 1.9 %collective-permute-start.9 = (bf16[2,512,256]{2,1,0:T(8,128)(2,1)S(1)}, bf16[2,512,256]{2,1,0:T(8,128)(2,1)S(1)}, u32[]{:S(2)}, u32[]{:S(2)}) collective-permute-start(bf16[2,512,256]{2,1,0:T(8,128)(2,1)S(1)} %copy-done.4), channel_id=1, source_target_pairs={{0,16},{16,0},{32,48},{48,32},{64,80},{80,64},{96,112},{112,96},{1... | collective-permute-start | bytes 1572872 | tf_op jit(solution)/shard_map/ppermute | solution.py:355
  72.9 2.7 %collective-permute-start.10 = (bf16[2,512,256]{2,1,0:T(8,128)(2,1)S(1)}, bf16[2,512,256]{2,1,0:T(8,128)(2,1)}, u32[]{:S(2)}, u32[]{:S(2)}) collective-permute-start(bf16[2,512,256]{2,1,0:T(8,128)(2,1)S(1)} %copy-done.4), channel_id=1, source_target_pairs={{0,48},{16,32},{32,16},{48,0},{64,112},{80,96},{96,80},{112,64},{1... | collective-permute-start | bytes 1572872 | tf_op jit(solution)/shard_map/ppermute | solution.py:355
  75.7 16.3 %collective-permute-done.8.pair_in = bf16[2,512,256]{2,1,0:T(8,128)(2,1)S(1)} collective-permute-done((bf16[2,512,256]{2,1,0:T(8,128)(2,1)S(1)}, bf16[2,512,256]{2,1,0:T(8,128)(2,1)S(1)}, u32[]{:S(2)}, u32[]{:S(2)}) %collective-permute-start.8) | collective-permute-done | bytes 524320 | tf_op jit(solution)/shard_map/ppermute | solution.py:355
  93.6 5.3 %collective-permute-done.10.diag_in = bf16[2,512,256]{2,1,0:T(8,128)(2,1)} collective-permute-done((bf16[2,512,256]{2,1,0:T(8,128)(2,1)S(1)}, bf16[2,512,256]{2,1,0:T(8,128)(2,1)}, u32[]{:S(2)}, u32[]{:S(2)}) %collective-permute-start.10) | collective-permute-done | bytes 524320 | tf_op jit(solution)/shard_map/ppermute | solution.py:355
  98.9 3.4 %order.1.green = bf16[2,512,1024]{2,1,0:T(8,128)(2,1)S(1)} custom-call(s32[2]{0:T(128)S(1)} %pad_add_fusion.place, bf16[2,512,256]{2,1,0:T(8,128)(2,1)} %own_in.1, bf16[2,512,256]{2,1,0:T(8,128)(2,1)} %copy-done.5, bf16[2,512,256]{2,1,0:T(8,128)(2,1)} %copy-done.6, bf16[2,512,256]{2,1,0:T(8,128)(2,1)} %collective-permute-done.10.diag_in), custom_call_target="tpu_custom_call" | custom-call | flops 1000000000 | bytes 4000000 | tf_op jit(solution)/shard_map/order/pallas_call | solution.py:364
  102.3 1.8 %columns.1 = f32[16,128,128]{2,1,0:T(8,128)S(1)} custom-call(s32[2]{0:T(128)S(1)} %copy-done.3, bf16[8,64,512]{2,1,0:T(8,128)(2,1)S(1)} %all-to-all-done.records, bf16[2,512,1024]{2,1,0:T(8,128)(2,1)S(1)} %order.1.green), custom_call_target="tpu_custom_call" | custom-call | flops 1000000000 | bytes 4000000 | tf_op jit(solution)/shard_map/columns/pallas_call | solution.py:196
  104.1 19.4 %all_to_all.20 = f32[4,512,128]{2,1,0:T(8,128)S(1)} all-to-all(f32[4,512,128]{2,1,0:T(8,128)S(1)} %bitcast.13), channel_id=1, replica_groups=mesh['shot'=32,'tx'=4,'ty'=4] {'tx'}, dimensions={0} | all-to-all | bytes 2097152 | tf_op jit(solution)/shard_map/all_to_all | solution.py:395
  123.5 12.8 %all_to_all.21 = f32[4,128,128]{2,1,0:T(8,128)S(1)} all-to-all(f32[4,128,128]{2,1,0:T(8,128)S(1)} %bitcast.17), channel_id=1, replica_groups=mesh['shot'=32,'tx'=4,'ty'=4] {'ty'}, dimensions={0} | all-to-all | bytes 524288 | tf_op jit(solution)/shard_map/all_to_all | solution.py:397
  136.4 24.2 %all_to_all.22.em = f32[8,16,128]{2,1,0:T(8,128)S(1)} all-to-all(f32[8,16,128]{2,1,0:T(8,128)S(1)} %bitcast.18), channel_id=1, replica_groups={{0,64,128,192,256,320,384,448},{16,80,144,208,272,336,400,464},{32,96,1..., dimensions={0} | all-to-all | bytes 131072 | tf_op jit(solution)/shard_map/all_to_all | solution.py:43
  160.6 4.9 %inject.1 = (f32[4,16,16,128]{3,2,1,0:T(8,128)}, f32[32,1,512]{2,1,0:T(1,128)}) custom-call(f32[8,16,128]{2,1,0:T(8,128)S(1)} %all_to_all.22.em, s32[8,512]{1,0:T(8,128)S(1)} %bitcast.15, f32[8,512]{1,0:T(8,128)S(1)} %bitcast.16, f32[4,16,16,128]{3,2,1,0:T(8,128)S(1)} %get-tuple-element.17.field), custom_call_target="tpu_custom_call" | custom-call | flops 4000000000 | bytes 4000000 | tf_op jit(solution)/shard_map/inject/pallas_call | solution.py:247
  (33 shorter events, 7.5 us)
Async XLA Ops:
  0.6 38.9 %copy-start = (bf16[4,8,1,1,512]{4,1,3,2,0:T(8,128)(2,1)S(1)}, bf16[4,8,1,1,512]{4,1,3,2,0:T(8,128)(2,1)}, u32[]{:S(2)}) copy-start(bf16[4,8,1,1,512]{4,1,3,2,0:T(8,128)(2,1)} %param.13) | copy-start | bytes 98308
  2.1 16.9 %collective-permute-start.2 = (f32[9,16,8,128]{3,2,1,0:T(8,128)S(1)}, f32[9,16,8,128]{3,2,1,0:T(8,128)S(1)}, u32[]{:S(2)}, u32[]{:S(2)}) collective-permute-start(f32[9,16,8,128]{3,2,1,0:T(8,128)S(1)} %get-tuple-element.14), channel_id=1, source_target_pairs={{0,1},{1,2},{2,3},{4,5},{5,6},{6,7},{8,9},{9,10},{10,11},{12,13},{... | collective-permute-start | bytes 1769480 | tf_op jit(solution)/shard_map/ppermute | solution.py:309
  6.4 16.3 %collective-permute-start = (f32[9,8,16,128]{3,2,1,0:T(8,128)S(1)}, f32[9,8,16,128]{3,2,1,0:T(8,128)S(1)}, u32[]{:S(2)}, u32[]{:S(2)}) collective-permute-start(f32[9,8,16,128]{3,2,1,0:T(8,128)S(1)} %get-tuple-element.12), channel_id=1, source_target_pairs={{0,4},{4,8},{8,12},{1,5},{5,9},{9,13},{2,6},{6,10},{10,14},{3,7},{... | collective-permute-start | bytes 1769480 | tf_op jit(solution)/shard_map/ppermute | solution.py:308
  9.8 16.4 %collective-permute-start.1 = (f32[9,8,16,128]{3,2,1,0:T(8,128)S(1)}, f32[9,8,16,128]{3,2,1,0:T(8,128)S(1)}, u32[]{:S(2)}, u32[]{:S(2)}) collective-permute-start(f32[9,8,16,128]{3,2,1,0:T(8,128)S(1)} %get-tuple-element.13), channel_id=1, source_target_pairs={{4,0},{8,4},{12,8},{5,1},{9,5},{13,9},{6,2},{10,6},{14,10},{7,3},{... | collective-permute-start | bytes 1769480 | tf_op jit(solution)/shard_map/ppermute | solution.py:310
  11.1 19.4 %collective-permute-start.3 = (f32[9,16,8,128]{3,2,1,0:T(8,128)S(1)}, f32[9,16,8,128]{3,2,1,0:T(8,128)S(1)}, u32[]{:S(2)}, u32[]{:S(2)}) collective-permute-start(f32[9,16,8,128]{3,2,1,0:T(8,128)S(1)} %get-tuple-element.15), channel_id=1, source_target_pairs={{1,0},{2,1},{3,2},{5,4},{6,5},{7,6},{9,8},{10,9},{11,10},{13,12},{... | collective-permute-start | bytes 1769480 | tf_op jit(solution)/shard_map/ppermute | solution.py:311
  18.9 13.2 %collective-permute-start.4 = (f32[9,8,8,128]{3,2,1,0:T(8,128)S(1)}, f32[9,8,8,128]{3,2,1,0:T(8,128)S(1)}, u32[]{:S(2)}, u32[]{:S(2)}) collective-permute-start(f32[9,8,8,128]{3,2,1,0:T(8,128)S(1)} %slice.16), channel_id=1, source_target_pairs={{0,4},{4,8},{8,12},{1,5},{5,9},{9,13},{2,6},{6,10},{10,14},{3,7},{... | collective-permute-start | bytes 884744 | tf_op jit(solution)/shard_map/ppermute | solution.py:312
  22.7 11.7 %collective-permute-start.5 = (f32[9,8,8,128]{3,2,1,0:T(8,128)S(1)}, f32[9,8,8,128]{3,2,1,0:T(8,128)S(1)}, u32[]{:S(2)}, u32[]{:S(2)}) collective-permute-start(f32[9,8,8,128]{3,2,1,0:T(8,128)S(1)} %slice.17), channel_id=1, source_target_pairs={{1,0},{2,1},{3,2},{5,4},{6,5},{7,6},{9,8},{10,9},{11,10},{13,12},{... | collective-permute-start | bytes 884744 | tf_op jit(solution)/shard_map/ppermute | solution.py:315
  26.2 9.1 %collective-permute-start.6 = (f32[9,8,8,128]{3,2,1,0:T(8,128)S(1)}, f32[9,8,8,128]{3,2,1,0:T(8,128)S(1)}, u32[]{:S(2)}, u32[]{:S(2)}) collective-permute-start(f32[9,8,8,128]{3,2,1,0:T(8,128)S(1)} %slice.18), channel_id=1, source_target_pairs={{0,1},{1,2},{2,3},{4,5},{5,6},{6,7},{8,9},{9,10},{10,11},{12,13},{... | collective-permute-start | bytes 884744 | tf_op jit(solution)/shard_map/ppermute | solution.py:313
  30.5 8.9 %collective-permute-start.7 = (f32[9,8,8,128]{3,2,1,0:T(8,128)S(1)}, f32[9,8,8,128]{3,2,1,0:T(8,128)S(1)}, u32[]{:S(2)}, u32[]{:S(2)}) collective-permute-start(f32[9,8,8,128]{3,2,1,0:T(8,128)S(1)} %slice.19), channel_id=1, source_target_pairs={{4,0},{8,4},{12,8},{5,1},{9,5},{13,9},{6,2},{10,6},{14,10},{7,3},{... | collective-permute-start | bytes 884744 | tf_op jit(solution)/shard_map/ppermute | solution.py:314
  39.5 28.2 %copy-start.4 = (bf16[2,512,256]{2,1,0:T(8,128)(2,1)S(1)}, bf16[2,512,256]{2,1,0:T(8,128)(2,1)}, u32[]{:S(2)}) copy-start(bf16[2,512,256]{2,1,0:T(8,128)(2,1)} %own_in.1) | copy-start | bytes 1572868
  54.9 47.4 %all-to-all-start = ((bf16[8,64,512]{2,1,0:T(8,128)(2,1)}), bf16[8,64,512]{2,1,0:T(8,128)(2,1)S(1)}, u32[]{:S(2)}, u32[]{:S(2)}) async-start(bf16[8,64,512]{2,1,0:T(8,128)(2,1)} %broadcast_in_dim.2), calls=%async_computation | async-start | bytes 1048576 | tf_op jit(solution)/shard_map/all_to_all | solution.py:43
  67.7 24.3 %collective-permute-start.8 = (bf16[2,512,256]{2,1,0:T(8,128)(2,1)S(1)}, bf16[2,512,256]{2,1,0:T(8,128)(2,1)S(1)}, u32[]{:S(2)}, u32[]{:S(2)}) collective-permute-start(bf16[2,512,256]{2,1,0:T(8,128)(2,1)S(1)} %copy-done.4), channel_id=1, source_target_pairs={{0,32},{16,48},{32,0},{48,16},{64,96},{80,112},{96,64},{112,80},{1... | collective-permute-start | bytes 1572872 | tf_op jit(solution)/shard_map/ppermute | solution.py:355
  71.0 21.0 %collective-permute-start.9 = (bf16[2,512,256]{2,1,0:T(8,128)(2,1)S(1)}, bf16[2,512,256]{2,1,0:T(8,128)(2,1)S(1)}, u32[]{:S(2)}, u32[]{:S(2)}) collective-permute-start(bf16[2,512,256]{2,1,0:T(8,128)(2,1)S(1)} %copy-done.4), channel_id=1, source_target_pairs={{0,16},{16,0},{32,48},{48,32},{64,80},{80,64},{96,112},{112,96},{1... | collective-permute-start | bytes 1572872 | tf_op jit(solution)/shard_map/ppermute | solution.py:355
  72.9 25.9 %collective-permute-start.10 = (bf16[2,512,256]{2,1,0:T(8,128)(2,1)S(1)}, bf16[2,512,256]{2,1,0:T(8,128)(2,1)}, u32[]{:S(2)}, u32[]{:S(2)}) collective-permute-start(bf16[2,512,256]{2,1,0:T(8,128)(2,1)S(1)} %copy-done.4), channel_id=1, source_target_pairs={{0,48},{16,32},{32,16},{48,0},{64,112},{80,96},{96,80},{112,64},{1... | collective-permute-start | bytes 1572872 | tf_op jit(solution)/shard_map/ppermute | solution.py:355
  75.7 26.6 %copy-start.3 = (s32[2]{0:T(128)S(1)}, s32[2]{0:T(128)}, u32[]{:S(2)}) copy-start(s32[2]{0:T(128)} %delay.1) | copy-start | bytes 28
  92.0 0.8 copy-start.5
  92.8 0.8 copy-start.6
  104.1 56.5 %copy-start.1 = (s32[1,1,8,512]{3,2,1,0:T(8,128)S(1)}, s32[1,1,8,512]{3,2,1,0:T(8,128)}, u32[]{:S(2)}) copy-start(s32[1,1,8,512]{3,2,1,0:T(8,128)} %param.16) | copy-start | bytes 49156
  104.1 56.5 %copy-start.2 = (f32[1,1,8,512]{3,2,1,0:T(8,128)S(1)}, f32[1,1,8,512]{3,2,1,0:T(8,128)}, u32[]{:S(2)}) copy-start(f32[1,1,8,512]{3,2,1,0:T(8,128)} %param.17) | copy-start | bytes 49156

commit v3 on v2

--- a/solution.py
+++ b/solution.py
@@ -24,13 +24,21 @@
 
 SHOT_COORDS = [(h, r, c) for h in range(2) for r in range(8) for c in range(2)]
 CORE_SWAP = [(shot_id(h, r, c), shot_id(h, r, 1 - c)) for h, r, c in SHOT_COORDS]
-DIAG_SWAP = [(shot_id(h, r, c), shot_id(h, r ^ 1, 1 - c)) for h, r, c in SHOT_COORDS]
 PAIR_SWAP = [(shot_id(h, r, c), shot_id(h, r ^ 1, c)) for h, r, c in SHOT_COORDS]
 ROW_GROUPS = [
     [shot_id(h, 2 * k + odd, c) for h in range(2) for k in range(4)]
     for odd in range(2)
     for c in range(2)
 ]
+COLUMN_GROUPS = [
+    [shot_id(h, 2 * k + odd, c) for k in range(4)]
+    for h in range(2)
+    for odd in range(2)
+    for c in range(2)
+]
+RING_GROUPS = [
+    [shot_id(h, r, c) * 4 + b for h in range(2) for b in range(4)] for r in range(8) for c in range(2)
+]
 UP = [(i, i + 1) for i in range(3)]
 DOWN = [(i + 1, i) for i in range(3)]
 
@@ -43,10 +51,6 @@
     return lax.all_to_all(
         x, "shot", split_axis=0, concat_axis=0, tiled=True, axis_index_groups=ROW_GROUPS
     )
-
-
-def spread_rows(x):
-    return row_exchange(jnp.broadcast_to(x[None], (8, *x.shape)))
 
 
 def stencil_kernel(
@@ -119,8 +123,10 @@
             picked = (picked * mask).astype(BF16)
             sel = (sel_row == (sel_col // DEPTH) * STEPS + (step - 1)).astype(F32).astype(BF16)
             records = records + lax.dot_general(sel, picked, NT, preferred_element_type=F32)
-    rec_out[pl.ds(0, shots * HIST), :] = history[...]
-    rec_out[pl.ds(shots * HIST, shots * STEPS), :] = records.astype(BF16)
+    records = records.astype(BF16)
+    for group in range(rec_out.shape[0]):
+        rec_out[group, pl.ds(0, shots * HIST), :] = history[...]
+        rec_out[group, pl.ds(shots * HIST, shots * STEPS), :] = records
     out_next = pltpu.make_async_copy(bufs[STEPS % 2].at[:, mid, ymid], next_out, out_sems.at[0])
     out_last = pltpu.make_async_copy(bufs[(STEPS - 1) % 2].at[:, mid, ymid], last_out, out_sems.at[1])
     out_next.start()
@@ -141,7 +147,7 @@
         out_shape=(
             jax.ShapeDtypeStruct(now.shape, F32),
             jax.ShapeDtypeStruct(now.shape, F32),
-            jax.ShapeDtypeStruct((shots * (HIST + STEPS), points), BF16),
+            jax.ShapeDtypeStruct((8, shots * (HIST + STEPS), points), BF16),
         ),
         in_specs=[hbm] * 3 + [anywhere] * 8 + [vmem] * 3,
         out_specs=(hbm, hbm, vmem),
@@ -209,7 +215,7 @@
     points = cells.shape[1]
     lane = lax.broadcasted_iota(jnp.int32, (16, 128), 1)
     for tile in range(4):
-        even, odd = em[2 * tile], em[2 * tile + 1]
+        even, odd = em[2 * tile % 4, tile // 2], em[2 * tile % 4 + 1, tile // 2]
         emission[pl.ds(0, 16), pl.ds(tile * 128, 128)] = jnp.where(lane < 64, even, pltpu.roll(odd, 64, 1))
         emission[pl.ds(16, 16), pl.ds(tile * 128, 128)] = jnp.where(lane < 64, pltpu.roll(even, 64, 1), odd)
 
@@ -351,12 +357,12 @@
 
 
 def gathered_green(green):
-    def moved(pairs):
-        return lax.ppermute(green, "shot", pairs)
-
-    core = moved(CORE_SWAP)
-    pair = moved(PAIR_SWAP)
-    diag = moved(DIAG_SWAP)
+    def moved(block, pairs):
+        return lax.ppermute(block, "shot", pairs)
+
+    pair = moved(green, PAIR_SWAP)
+    core = moved(green, CORE_SWAP)
+    diag = moved(pair, CORE_SWAP)
     me = lax.axis_index("shot")
     place = jnp.stack([me // 2 % 2, me % 2]).astype(jnp.int32)
     lags, points, width = green.shape
@@ -390,12 +396,19 @@
     field, wave_last, records = stencil(
         wave_now, wave_prev, courant, halos, rows_hot, lanes_hot, rec_history.reshape(shots * HIST, -1)
     )
-    records = spread_rows(records)
+    records = row_exchange(records)
     partial = columns(lag_delay, records, wide_green)
     partial = lax.all_to_all(partial.reshape(4, 512, 128), "tx", 0, 0, tiled=True)
-    partial = jnp.sum(partial, axis=0).reshape(4, 128, 128)
-    summed = jnp.sum(lax.all_to_all(partial, "ty", 0, 0, tiled=True), axis=0)
-    em = row_exchange(summed.reshape(8, 16, 128))
+    partial = jnp.sum(partial, axis=0).reshape(4, 2, 64, 128)
+    partial = jnp.swapaxes(partial, 0, 1).reshape(8, 64, 128)
+    partial = lax.all_to_all(
+        partial, ("shot", "ty"), 0, 0, tiled=True, axis_index_groups=RING_GROUPS
+    )
+    summed = jnp.sum(partial.reshape(2, 4, 64, 128), axis=1)
+    summed = jnp.swapaxes(summed.reshape(2, 4, 16, 128), 0, 1)
+    em = lax.all_to_all(
+        summed, "shot", 0, 0, tiled=True, axis_index_groups=COLUMN_GROUPS
+    )
     wave_out, emission = inject(
         em, emit_cells.reshape(emit_cells.shape[-2:]), emit_weights.reshape(emit_weights.shape[-2:]), field
     )

time: 166 us -> 138 us (0.83)
  waiting for transfers between devices: 37.2 us -> 23 us
  blocking collectives: 56.4 us -> 43.9 us
    ppermute x3, waiting for transfers between devices: 21.5 us -> 0.71 us  [moved(): return lax.ppermute(block, 'shot', pairs)]
    all_to_all x1, waiting for transfers between devices: 0.01 us -> 9.24 us  [row_exchange(): lax.all_to_all(x, 'shot', split_axis=0, concat_axis=0, tiled=True, axis_i...]
    all_to_all x2, blocking collectives: 37 us -> 29.1 us  [the longest x1 15.3 us: block(): lax.all_to_all(summed, 'shot', 0, 0, tiled=True, axis_index_groups=COLUMN...]
    all_to_all x1, blocking collectives: 19.4 us -> 14.8 us  [block(): lax.all_to_all(partial.reshape(4, 512, 128), 'tx', 0, 0, tiled=True)]
    ppermute x1, waiting for transfers between devices: 5.8 us -> 3.18 us  [halo_blocks(): ym = lax.ppermute(ytail, 'ty', UP)]
  transfers between devices with their start and end apart: 12 -> 12, of which waited for: 8 -> 8; matrix products, arithmetic and copies ran while one was open for 1% -> 1% of each run, Pallas kernels for 2% -> 14%
where the time goes in v3:
time: 138 us; the launch traced here: 137 us
  blocking collectives  43.9 us (32%)
  starting transfers between devices  40.4 us (29%)
  Pallas kernels  26.8 us (19%)
  waiting for transfers between devices  23 us (17%)
    pallas_call x1, Pallas kernels, stencil(): pl.pallas_call(stencil_kernel, out_shape=(jax.ShapeDtypeStruct(now.shape,...  15.3 us
    all_to_all x1, blocking collectives, block(): lax.all_to_all(summed, 'shot', 0, 0, tiled=True, axis_index_groups=COLUMN...  15.3 us
    all_to_all x1, blocking collectives, block(): lax.all_to_all(partial.reshape(4, 512, 128), 'tx', 0, 0, tiled=True)  14.8 us
    all_to_all x1, blocking collectives, block(): lax.all_to_all(partial, ('shot', 'ty'), 0, 0, tiled=True, axis_index_grou...  13.8 us
    all_to_all x1, starting transfers between devices, row_exchange(): lax.all_to_all(x, 'shot', split_axis=0, concat_axis=0, tiled=True, axis_i...  12.9 us
    all_to_all x1, waiting for transfers between devices, row_exchange(): lax.all_to_all(x, 'shot', split_axis=0, concat_axis=0, tiled=True, axis_i...  9.24 us
    ppermute x3, starting transfers between devices, moved(): return lax.ppermute(block, 'shot', pairs)  6.94 us
    pallas_call x1, Pallas kernels, inject(): pl.pallas_call(inject_kernel, out_shape=(jax.ShapeDtypeStruct(field.shape...  4.91 us
  transfers between devices with their start and end apart: 12, of which 8 were waited for; matrix products, arithmetic and copies ran while one was open for 1% of the time, Pallas kernels for 14%

profile of v3, /device:TPU:8, one launch (start us, length us, event | category | flops | bytes accessed | tf_op | source)
XLA Modules:
  0.0 137.1 jit_solution(8425913658660133414)
XLA Ops:
  0.6 1.4 %pack.1 = (f32[9,8,16,128]{3,2,1,0:T(8,128)S(1)}, f32[9,16,8,128]{3,2,1,0:T(8,128)S(1)}, f32[9,8,16,128]{3,2,1,0:T(8,128)S(1)}, f32[9,16,8,128]{3,2,1,0:T(8,128)S(1)}) custom-call(f32[4,16,16,128]{3,2,1,0:T(8,128)} %now.3, f32[4,16,16,128]{3,2,1,0:T(8,128)} %prev.3, f32[16,16,128]{2,1,0:T(8,128)} %speed_in.1), custom_call_target="tpu_custom_call" | custom-call | bytes 4000000 | tf_op jit(solution)/shard_map/pack/pallas_call | solution.py:296
  2.1 4.3 %collective-permute-start.2 = (f32[9,16,8,128]{3,2,1,0:T(8,128)S(1)}, f32[9,16,8,128]{3,2,1,0:T(8,128)S(1)}, u32[]{:S(2)}, u32[]{:S(2)}) collective-permute-start(f32[9,16,8,128]{3,2,1,0:T(8,128)S(1)} %get-tuple-element.14), channel_id=1, source_target_pairs={{0,1},{1,2},{2,3},{4,5},{5,6},{6,7},{8,9},{9,10},{10,11},{12,13},{... | collective-permute-start | bytes 1769480 | tf_op jit(solution)/shard_map/ppermute | solution.py:315
  6.4 3.4 %collective-permute-start = (f32[9,8,16,128]{3,2,1,0:T(8,128)S(1)}, f32[9,8,16,128]{3,2,1,0:T(8,128)S(1)}, u32[]{:S(2)}, u32[]{:S(2)}) collective-permute-start(f32[9,8,16,128]{3,2,1,0:T(8,128)S(1)} %get-tuple-element.12), channel_id=1, source_target_pairs={{0,4},{4,8},{8,12},{1,5},{5,9},{9,13},{2,6},{6,10},{10,14},{3,7},{... | collective-permute-start | bytes 1769480 | tf_op jit(solution)/shard_map/ppermute | solution.py:314
  9.8 1.3 collective-permute-start.1
  11.1 1.3 collective-permute-start.3
  12.4 2.6 %collective-permute-start.8 = (bf16[2,512,256]{2,1,0:T(8,128)(2,1)}, bf16[2,512,256]{2,1,0:T(8,128)(2,1)S(1)}, u32[]{:S(2)}, u32[]{:S(2)}) collective-permute-start(bf16[2,512,256]{2,1,0:T(8,128)(2,1)} %own_in.1), channel_id=1, source_target_pairs={{0,32},{16,48},{32,0},{48,16},{64,96},{80,112},{96,64},{112,80},{1... | collective-permute-start | bytes 1572872 | tf_op jit(solution)/shard_map/ppermute | solution.py:361
  15.7 3.2 %collective-permute-done.2.ym = f32[9,16,8,128]{3,2,1,0:T(8,128)S(1)} collective-permute-done((f32[9,16,8,128]{3,2,1,0:T(8,128)S(1)}, f32[9,16,8,128]{3,2,1,0:T(8,128)S(1)}, u32[]{:S(2)}, u32[]{:S(2)}) %collective-permute-start.2) | collective-permute-done | bytes 589856 | tf_op jit(solution)/shard_map/ppermute | solution.py:315
  18.9 3.4 %collective-permute-start.4 = (f32[9,8,8,128]{3,2,1,0:T(8,128)S(1)}, f32[9,8,8,128]{3,2,1,0:T(8,128)S(1)}, u32[]{:S(2)}, u32[]{:S(2)}) collective-permute-start(f32[9,8,8,128]{3,2,1,0:T(8,128)S(1)} %slice.16), channel_id=1, source_target_pairs={{0,4},{4,8},{8,12},{1,5},{5,9},{9,13},{2,6},{6,10},{10,14},{3,7},{... | collective-permute-start | bytes 884744 | tf_op jit(solution)/shard_map/ppermute | solution.py:318
  22.7 1.3 collective-permute-start.5
  24.0 2.2 %collective-permute-done.1.xp = f32[9,8,16,128]{3,2,1,0:T(8,128)S(1)} collective-permute-done((f32[9,8,16,128]{3,2,1,0:T(8,128)S(1)}, f32[9,8,16,128]{3,2,1,0:T(8,128)S(1)}, u32[]{:S(2)}, u32[]{:S(2)}) %collective-permute-start.1) | collective-permute-done | bytes 589856 | tf_op jit(solution)/shard_map/ppermute | solution.py:316
  26.2 4.3 %collective-permute-start.6 = (f32[9,8,8,128]{3,2,1,0:T(8,128)S(1)}, f32[9,8,8,128]{3,2,1,0:T(8,128)S(1)}, u32[]{:S(2)}, u32[]{:S(2)}) collective-permute-start(f32[9,8,8,128]{3,2,1,0:T(8,128)S(1)} %slice.18), channel_id=1, source_target_pairs={{0,1},{1,2},{2,3},{4,5},{5,6},{6,7},{8,9},{9,10},{10,11},{12,13},{... | collective-permute-start | bytes 884744 | tf_op jit(solution)/shard_map/ppermute | solution.py:319
  32.1 2.3 %collective-permute-done.5.cmp = f32[9,8,8,128]{3,2,1,0:T(8,128)S(1)} collective-permute-done((f32[9,8,8,128]{3,2,1,0:T(8,128)S(1)}, f32[9,8,8,128]{3,2,1,0:T(8,128)S(1)}, u32[]{:S(2)}, u32[]{:S(2)}) %collective-permute-start.5) | collective-permute-done | bytes 294944 | tf_op jit(solution)/shard_map/ppermute | solution.py:321
  35.3 4.2 %collective-permute-done.7.cpp = f32[9,8,8,128]{3,2,1,0:T(8,128)S(1)} collective-permute-done((f32[9,8,8,128]{3,2,1,0:T(8,128)S(1)}, f32[9,8,8,128]{3,2,1,0:T(8,128)S(1)}, u32[]{:S(2)}, u32[]{:S(2)}) %collective-permute-start.7) | collective-permute-done | bytes 294944 | tf_op jit(solution)/shard_map/ppermute | solution.py:320
  39.5 15.3 %stencil.1 = (f32[4,16,16,128]{3,2,1,0:T(8,128)S(1)}, f32[4,16,16,128]{3,2,1,0:T(8,128)}, bf16[8,64,512]{2,1,0:T(8,128)(2,1)}) custom-call(f32[4,16,16,128]{3,2,1,0:T(8,128)} %now.3, f32[4,16,16,128]{3,2,1,0:T(8,128)} %prev.3, f32[16,16,128]{2,1,0:T(8,128)} %speed_in.1, f32[9,8,16,128]{3,2,1,0:T(8,128)S(1)} %collective-permute-done.xm, ...), custom_call_target="tpu_custom_call" | custom-call | flops 2000000000 | bytes 12000000 | tf_op jit(solution)/shard_map/stencil/pallas_call | solution.py:145
  54.8 12.9 %all-to-all-start = ((bf16[8,64,512]{2,1,0:T(8,128)(2,1)}), bf16[8,64,512]{2,1,0:T(8,128)(2,1)S(1)}, u32[]{:S(2)}, u32[]{:S(2)}) async-start(bf16[8,64,512]{2,1,0:T(8,128)(2,1)} %get-tuple-element.16), calls=%async_computation | async-start | bytes 1048576 | tf_op jit(solution)/shard_map/all_to_all | solution.py:51
  67.7 1.9 %collective-permute-start.9 = (bf16[2,512,256]{2,1,0:T(8,128)(2,1)S(1)}, bf16[2,512,256]{2,1,0:T(8,128)(2,1)S(1)}, u32[]{:S(2)}, u32[]{:S(2)}) collective-permute-start(bf16[2,512,256]{2,1,0:T(8,128)(2,1)S(1)} %copy-done.4), channel_id=1, source_target_pairs={{0,16},{16,0},{32,48},{48,32},{64,80},{80,64},{96,112},{112,96},{1... | collective-permute-start | bytes 1572872 | tf_op jit(solution)/shard_map/ppermute | solution.py:361
  69.7 2.4 %collective-permute-start.10 = (bf16[2,512,256]{2,1,0:T(8,128)(2,1)S(1)}, bf16[2,512,256]{2,1,0:T(8,128)(2,1)}, u32[]{:S(2)}, u32[]{:S(2)}) collective-permute-start(bf16[2,512,256]{2,1,0:T(8,128)(2,1)S(1)} %collective-permute-done.8.pair_in), channel_id=1, source_target_pairs={{0,16},{16,0},{32,48},{48,32},{64,80},{80,64},{96,112},{112,96},{1... | collective-permute-start | bytes 1572872 | tf_op jit(solution)/shard_map/ppermute | solution.py:361
  73.7 3.4 %order.1.green = bf16[2,512,1024]{2,1,0:T(8,128)(2,1)S(1)} custom-call(s32[2]{0:T(128)S(1)} %pad_add_fusion.place, bf16[2,512,256]{2,1,0:T(8,128)(2,1)} %own_in.1, bf16[2,512,256]{2,1,0:T(8,128)(2,1)} %copy-done.5, bf16[2,512,256]{2,1,0:T(8,128)(2,1)} %copy-done.6, bf16[2,512,256]{2,1,0:T(8,128)(2,1)} %collective-permute-done.10.diag_in), custom_call_target="tpu_custom_call" | custom-call | flops 1000000000 | bytes 4000000 | tf_op jit(solution)/shard_map/order/pallas_call | solution.py:370
  77.1 9.2 %all-to-all-done.records = bf16[8,64,512]{2,1,0:T(8,128)(2,1)S(1)} async-done(((bf16[8,64,512]{2,1,0:T(8,128)(2,1)}), bf16[8,64,512]{2,1,0:T(8,128)(2,1)S(1)}, u32[]{:S(2)}, u32[]{:S(2)}) %all-to-all-start) | async-done | bytes 524320 | tf_op jit(solution)/shard_map/all_to_all | solution.py:51
  86.4 1.8 %columns.1 = f32[16,128,128]{2,1,0:T(8,128)S(1)} custom-call(s32[2]{0:T(128)S(1)} %copy-done.3, bf16[8,64,512]{2,1,0:T(8,128)(2,1)S(1)} %all-to-all-done.records, bf16[2,512,1024]{2,1,0:T(8,128)(2,1)S(1)} %order.1.green), custom_call_target="tpu_custom_call" | custom-call | flops 1000000000 | bytes 4000000 | tf_op jit(solution)/shard_map/columns/pallas_call | solution.py:202
  88.2 14.8 %all_to_all.20 = f32[4,512,128]{2,1,0:T(8,128)S(1)} all-to-all(f32[4,512,128]{2,1,0:T(8,128)S(1)} %bitcast.21), channel_id=1, replica_groups=mesh['shot'=32,'tx'=4,'ty'=4] {'tx'}, dimensions={0} | all-to-all | bytes 2097152 | tf_op jit(solution)/shard_map/all_to_all | solution.py:401
  103.1 13.8 %all_to_all.21 = f32[8,64,128]{2,1,0:T(8,128)S(1)} all-to-all(f32[8,64,128]{2,1,0:T(8,128)S(1)} %bitcast.26), channel_id=1, replica_groups={{0,1,2,3,256,257,258,259},{16,17,18,19,272,273,274,275},{32,33,34,35,28..., dimensions={0} | all-to-all | bytes 524288 | tf_op jit(solution)/shard_map/all_to_all | solution.py:404
  116.9 15.3 %all_to_all.22.em = f32[4,2,16,128]{3,2,1,0:T(8,128)S(1)} all-to-all(f32[4,2,16,128]{3,2,1,0:T(8,128)S(1)} %bitcast.28), channel_id=1, replica_groups={{0,64,128,192},{16,80,144,208},{32,96,160,224},{48,112,176,240},{256,32..., dimensions={0} | all-to-all | bytes 131072 | tf_op jit(solution)/shard_map/all_to_all | solution.py:409
  132.2 4.9 %inject.1 = (f32[4,16,16,128]{3,2,1,0:T(8,128)}, f32[32,1,512]{2,1,0:T(1,128)}) custom-call(f32[4,2,16,128]{3,2,1,0:T(8,128)S(1)} %all_to_all.22.em, s32[8,512]{1,0:T(8,128)S(1)} %bitcast.23, f32[8,512]{1,0:T(8,128)S(1)} %bitcast.24, f32[4,16,16,128]{3,2,1,0:T(8,128)S(1)} %get-tuple-element.17.field), custom_call_target="tpu_custom_call" | custom-call | flops 4000000000 | bytes 4000000 | tf_op jit(solution)/shard_map/inject/pallas_call | solution.py:253
  (34 shorter events, 5.3 us)
Async XLA Ops:
  0.6 38.9 %copy-start = (bf16[4,8,1,1,512]{4,1,3,2,0:T(8,128)(2,1)S(1)}, bf16[4,8,1,1,512]{4,1,3,2,0:T(8,128)(2,1)}, u32[]{:S(2)}) copy-start(bf16[4,8,1,1,512]{4,1,3,2,0:T(8,128)(2,1)} %param.13) | copy-start | bytes 98308
  2.1 16.9 %collective-permute-start.2 = (f32[9,16,8,128]{3,2,1,0:T(8,128)S(1)}, f32[9,16,8,128]{3,2,1,0:T(8,128)S(1)}, u32[]{:S(2)}, u32[]{:S(2)}) collective-permute-start(f32[9,16,8,128]{3,2,1,0:T(8,128)S(1)} %get-tuple-element.14), channel_id=1, source_target_pairs={{0,1},{1,2},{2,3},{4,5},{5,6},{6,7},{8,9},{9,10},{10,11},{12,13},{... | collective-permute-start | bytes 1769480 | tf_op jit(solution)/shard_map/ppermute | solution.py:315
  6.4 16.3 %collective-permute-start = (f32[9,8,16,128]{3,2,1,0:T(8,128)S(1)}, f32[9,8,16,128]{3,2,1,0:T(8,128)S(1)}, u32[]{:S(2)}, u32[]{:S(2)}) collective-permute-start(f32[9,8,16,128]{3,2,1,0:T(8,128)S(1)} %get-tuple-element.12), channel_id=1, source_target_pairs={{0,4},{4,8},{8,12},{1,5},{5,9},{9,13},{2,6},{6,10},{10,14},{3,7},{... | collective-permute-start | bytes 1769480 | tf_op jit(solution)/shard_map/ppermute | solution.py:314
  9.8 16.4 %collective-permute-start.1 = (f32[9,8,16,128]{3,2,1,0:T(8,128)S(1)}, f32[9,8,16,128]{3,2,1,0:T(8,128)S(1)}, u32[]{:S(2)}, u32[]{:S(2)}) collective-permute-start(f32[9,8,16,128]{3,2,1,0:T(8,128)S(1)} %get-tuple-element.13), channel_id=1, source_target_pairs={{4,0},{8,4},{12,8},{5,1},{9,5},{13,9},{6,2},{10,6},{14,10},{7,3},{... | collective-permute-start | bytes 1769480 | tf_op jit(solution)/shard_map/ppermute | solution.py:316
  11.1 19.4 %collective-permute-start.3 = (f32[9,16,8,128]{3,2,1,0:T(8,128)S(1)}, f32[9,16,8,128]{3,2,1,0:T(8,128)S(1)}, u32[]{:S(2)}, u32[]{:S(2)}) collective-permute-start(f32[9,16,8,128]{3,2,1,0:T(8,128)S(1)} %get-tuple-element.15), channel_id=1, source_target_pairs={{1,0},{2,1},{3,2},{5,4},{6,5},{7,6},{9,8},{10,9},{11,10},{13,12},{... | collective-permute-start | bytes 1769480 | tf_op jit(solution)/shard_map/ppermute | solution.py:317
  12.4 57.2 %collective-permute-start.8 = (bf16[2,512,256]{2,1,0:T(8,128)(2,1)}, bf16[2,512,256]{2,1,0:T(8,128)(2,1)S(1)}, u32[]{:S(2)}, u32[]{:S(2)}) collective-permute-start(bf16[2,512,256]{2,1,0:T(8,128)(2,1)} %own_in.1), channel_id=1, source_target_pairs={{0,32},{16,48},{32,0},{48,16},{64,96},{80,112},{96,64},{112,80},{1... | collective-permute-start | bytes 1572872 | tf_op jit(solution)/shard_map/ppermute | solution.py:361
  18.9 13.2 %collective-permute-start.4 = (f32[9,8,8,128]{3,2,1,0:T(8,128)S(1)}, f32[9,8,8,128]{3,2,1,0:T(8,128)S(1)}, u32[]{:S(2)}, u32[]{:S(2)}) collective-permute-start(f32[9,8,8,128]{3,2,1,0:T(8,128)S(1)} %slice.16), channel_id=1, source_target_pairs={{0,4},{4,8},{8,12},{1,5},{5,9},{9,13},{2,6},{6,10},{10,14},{3,7},{... | collective-permute-start | bytes 884744 | tf_op jit(solution)/shard_map/ppermute | solution.py:318
  22.7 11.7 %collective-permute-start.5 = (f32[9,8,8,128]{3,2,1,0:T(8,128)S(1)}, f32[9,8,8,128]{3,2,1,0:T(8,128)S(1)}, u32[]{:S(2)}, u32[]{:S(2)}) collective-permute-start(f32[9,8,8,128]{3,2,1,0:T(8,128)S(1)} %slice.17), channel_id=1, source_target_pairs={{1,0},{2,1},{3,2},{5,4},{6,5},{7,6},{9,8},{10,9},{11,10},{13,12},{... | collective-permute-start | bytes 884744 | tf_op jit(solution)/shard_map/ppermute | solution.py:321
  26.2 9.1 %collective-permute-start.6 = (f32[9,8,8,128]{3,2,1,0:T(8,128)S(1)}, f32[9,8,8,128]{3,2,1,0:T(8,128)S(1)}, u32[]{:S(2)}, u32[]{:S(2)}) collective-permute-start(f32[9,8,8,128]{3,2,1,0:T(8,128)S(1)} %slice.18), channel_id=1, source_target_pairs={{0,1},{1,2},{2,3},{4,5},{5,6},{6,7},{8,9},{9,10},{10,11},{12,13},{... | collective-permute-start | bytes 884744 | tf_op jit(solution)/shard_map/ppermute | solution.py:319
  30.5 8.9 %collective-permute-start.7 = (f32[9,8,8,128]{3,2,1,0:T(8,128)S(1)}, f32[9,8,8,128]{3,2,1,0:T(8,128)S(1)}, u32[]{:S(2)}, u32[]{:S(2)}) collective-permute-start(f32[9,8,8,128]{3,2,1,0:T(8,128)S(1)} %slice.19), channel_id=1, source_target_pairs={{4,0},{8,4},{12,8},{5,1},{9,5},{13,9},{6,2},{10,6},{14,10},{7,3},{... | collective-permute-start | bytes 884744 | tf_op jit(solution)/shard_map/ppermute | solution.py:320
  39.5 28.2 %copy-start.4 = (bf16[2,512,256]{2,1,0:T(8,128)(2,1)S(1)}, bf16[2,512,256]{2,1,0:T(8,128)(2,1)}, u32[]{:S(2)}) copy-start(bf16[2,512,256]{2,1,0:T(8,128)(2,1)} %own_in.1) | copy-start | bytes 1572868
  54.8 31.5 %all-to-all-start = ((bf16[8,64,512]{2,1,0:T(8,128)(2,1)}), bf16[8,64,512]{2,1,0:T(8,128)(2,1)S(1)}, u32[]{:S(2)}, u32[]{:S(2)}) async-start(bf16[8,64,512]{2,1,0:T(8,128)(2,1)} %get-tuple-element.16), calls=%async_computation | async-start | bytes 1048576 | tf_op jit(solution)/shard_map/all_to_all | solution.py:51
  67.7 4.5 %collective-permute-start.9 = (bf16[2,512,256]{2,1,0:T(8,128)(2,1)S(1)}, bf16[2,512,256]{2,1,0:T(8,128)(2,1)S(1)}, u32[]{:S(2)}, u32[]{:S(2)}) collective-permute-start(bf16[2,512,256]{2,1,0:T(8,128)(2,1)S(1)} %copy-done.4), channel_id=1, source_target_pairs={{0,16},{16,0},{32,48},{48,32},{64,80},{80,64},{96,112},{112,96},{1... | collective-permute-start | bytes 1572872 | tf_op jit(solution)/shard_map/ppermute | solution.py:361
  69.6 2.5 %copy-start.5 = (bf16[2,512,256]{2,1,0:T(8,128)(2,1)}, bf16[2,512,256]{2,1,0:T(8,128)(2,1)S(1)}, u32[]{:S(2)}) copy-start(bf16[2,512,256]{2,1,0:T(8,128)(2,1)S(1)} %collective-permute-done.8.pair_in) | copy-start | bytes 1572868
  69.7 4.1 %collective-permute-start.10 = (bf16[2,512,256]{2,1,0:T(8,128)(2,1)S(1)}, bf16[2,512,256]{2,1,0:T(8,128)(2,1)}, u32[]{:S(2)}, u32[]{:S(2)}) collective-permute-start(bf16[2,512,256]{2,1,0:T(8,128)(2,1)S(1)} %collective-permute-done.8.pair_in), channel_id=1, source_target_pairs={{0,16},{16,0},{32,48},{48,32},{64,80},{80,64},{96,112},{112,96},{1... | collective-permute-start | bytes 1572872 | tf_op jit(solution)/shard_map/ppermute | solution.py:361
  72.2 14.2 %copy-start.3 = (s32[2]{0:T(128)S(1)}, s32[2]{0:T(128)}, u32[]{:S(2)}) copy-start(s32[2]{0:T(128)} %delay.1) | copy-start | bytes 28
  72.2 0.8 copy-start.6
  88.2 44.0 %copy-start.1 = (s32[1,1,8,512]{3,2,1,0:T(8,128)S(1)}, s32[1,1,8,512]{3,2,1,0:T(8,128)}, u32[]{:S(2)}) copy-start(s32[1,1,8,512]{3,2,1,0:T(8,128)} %param.16) | copy-start | bytes 49156
  88.2 44.0 %copy-start.2 = (f32[1,1,8,512]{3,2,1,0:T(8,128)S(1)}, f32[1,1,8,512]{3,2,1,0:T(8,128)}, u32[]{:S(2)}) copy-start(f32[1,1,8,512]{3,2,1,0:T(8,128)} %param.17) | copy-start | bytes 49156

commit v4 on v3

--- a/solution.py
+++ b/solution.py
@@ -53,118 +53,187 @@
     )
 
 
+LOW = slice(0, BAND)
+MID = slice(BAND, BAND + TILE)
+HIGH = slice(BAND + TILE, WIDE)
+YLOW = slice(PAD, PAD + BAND)
+YMID = slice(PAD + BAND, PAD + BAND + TILE)
+YHIGH = slice(PAD + BAND + TILE, PAD + WIDE)
+NEAR = slice(BAND - 1, BAND + TILE + 1)
+YNEAR = slice(PAD, PAD + WIDE)
+HBM = pl.BlockSpec(memory_space=pltpu.HBM)
+ANY = pl.BlockSpec(memory_space=pl.ANY)
+VMEM = pl.BlockSpec(memory_space=pltpu.VMEM)
+
+
+def band_copies(blocks, cur, prv, spd, sems):
+    shots = cur.shape[0]
+    copies = []
+    for block, xs, ys in blocks:
+        for src, dst in (
+            (block.at[pl.ds(0, shots)], cur.at[:, xs, ys]),
+            (block.at[pl.ds(shots, shots)], prv.at[:, xs, ys]),
+            (block.at[2 * shots], spd.at[xs, ys]),
+        ):
+            copies.append(pltpu.make_async_copy(src, dst, sems.at[len(copies)]))
+    return copies
+
+
+def run(copies):
+    for copy in copies:
+        copy.start()
+    for copy in copies:
+        copy.wait()
+
+
+def assemble_kernel(now, prev, speed, xm, xp, ym, yp, cur, prv, spd, own_sems, sems):
+    own = [
+        pltpu.make_async_copy(now, cur.at[:, MID, YMID], own_sems.at[0]),
+        pltpu.make_async_copy(prev, prv.at[:, MID, YMID], own_sems.at[1]),
+        pltpu.make_async_copy(speed, spd.at[MID, YMID], own_sems.at[2]),
+    ]
+    blocks = ((xm, LOW, YMID), (xp, HIGH, YMID), (ym, MID, YLOW), (yp, MID, YHIGH))
+    run(own + band_copies(blocks, cur, prv, spd, sems))
+
+
+def assemble(now, prev, speed, halos):
+    shots = now.shape[0]
+    wide = (shots, WIDE, WIDE + 2 * PAD, DEPTH)
+    return pl.pallas_call(
+        assemble_kernel,
+        out_shape=(
+            jax.ShapeDtypeStruct(wide, F32),
+            jax.ShapeDtypeStruct(wide, F32),
+            jax.ShapeDtypeStruct(wide[1:], F32),
+        ),
+        in_specs=[HBM] * 3 + [ANY] * 4,
+        out_specs=(VMEM,) * 3,
+        scratch_shapes=[pltpu.SemaphoreType.DMA((3,)), pltpu.SemaphoreType.DMA((12,))],
+        compiler_params=pltpu.CompilerParams(vmem_limit_bytes=10 << 20),
+        cost_estimate=pl.CostEstimate(flops=0, bytes_accessed=8_000_000, transcendentals=0),
+        name="assemble",
+    )(*in_hbm(now, prev, speed), *halos)
+
+
+def advance(src, dst, spd, rows, start, count, shift=0, base=0):
+    lane = lax.broadcasted_iota(jnp.int32, (count, DEPTH), 1)
+
+    def body(x, carry):
+        at, cells = x - shift, pl.ds(start - base, count)
+        speed = spd[at, cells, :]
+        centre = 2.0 - 6.0 * speed
+        for s in range(src.shape[0]):
+            u = src[s, x, pl.ds(start, count), :]
+            total = src[s, x - 1, pl.ds(start, count), :] + src[s, x + 1, pl.ds(start, count), :]
+            total = total + src[s, x, pl.ds(start - 1, count), :]
+            total = total + src[s, x, pl.ds(start + 1, count), :]
+            total = total + jnp.where(lane > 0, pltpu.roll(u, 1, 1), 0.0)
+            total = total + jnp.where(lane < DEPTH - 1, pltpu.roll(u, DEPTH - 1, 1), 0.0)
+            dst[s, at, cells, :] = centre * u - dst[s, at, cells, :] + speed * total
+        return carry
+
+    lax.fori_loop(*rows, body, 0, unroll=4)
+
+
 def stencil_kernel(
-    now, prev, speed_in, xm, xp, ym, yp, cmm, cmp, cpm, cpp, rows_hot, lanes_hot, history,
-    next_out, last_out, rec_out, cur, prv, spd, sems, out_sems,
+    cur_in, prv_in, spd_in, cmm, cmp, cpm, cpp, rows_hot, lanes_hot, history,
+    rec_out, near_out, before_out, cur, prv, spd, rec, sems, out_sems,
 ):
-    shots = now.shape[0]
-    low = slice(0, BAND)
-    mid = slice(BAND, BAND + TILE)
-    high = slice(BAND + TILE, WIDE)
-    ylow = slice(PAD, PAD + BAND)
-    ymid = slice(PAD + BAND, PAD + BAND + TILE)
-    yhigh = slice(PAD + BAND + TILE, PAD + WIDE)
-    copies = []
-
-    def add(src, dst):
-        copies.append(pltpu.make_async_copy(src, dst, sems.at[len(copies)]))
-
-    add(now, cur.at[:, mid, ymid])
-    add(prev, prv.at[:, mid, ymid])
-    add(speed_in, spd.at[mid, ymid])
-    for block, xs, ys in (
-        (xm, low, ymid), (xp, high, ymid), (ym, mid, ylow), (yp, mid, yhigh),
-        (cmm, low, ylow), (cmp, low, yhigh), (cpm, high, ylow), (cpp, high, yhigh),
-    ):
-        add(block.at[pl.ds(0, shots)], cur.at[:, xs, ys])
-        add(block.at[pl.ds(shots, shots)], prv.at[:, xs, ys])
-        add(block.at[2 * shots], spd.at[xs, ys])
-    for copy in copies:
-        copy.start()
-    for copy in copies:
-        copy.wait()
-
+    shots = cur.shape[0]
+    blocks = ((cmm, LOW, YLOW), (cmp, LOW, YHIGH), (cpm, HIGH, YLOW), (cpp, HIGH, YHIGH))
+    run(band_copies(blocks, cur, prv, spd, sems))
     bufs = (cur, prv)
-    lanes = lax.broadcasted_iota(jnp.int32, (WIDE, DEPTH), 1)
     sel_row = lax.broadcasted_iota(jnp.int32, (shots * STEPS, shots * DEPTH), 0)
     sel_col = lax.broadcasted_iota(jnp.int32, (shots * STEPS, shots * DEPTH), 1)
+    mask = jnp.concatenate([lanes_hot[...]] * shots, axis=1)
     records = jnp.zeros((shots * STEPS, rows_hot.shape[0]), F32)
-    for step in range(1, STEPS + 1):
+    for step in range(1, STEPS):
         src, dst = bufs[(step - 1) % 2], bufs[step % 2]
-        if step < STEPS:
-            start, count = (PAD, WIDE) if step < 4 else (PAD + 4, WIDE - 8)
-        else:
-            start, count = PAD + BAND, TILE
-        lane = lanes[:count]
-
-        def body(x, carry, src=src, dst=dst, start=start, count=count, lane=lane):
-            speed = spd[x, pl.ds(start, count), :]
-            centre = 2.0 - 6.0 * speed
-            for s in range(shots):
-                u = src[s, x, pl.ds(start, count), :]
-                total = src[s, x - 1, pl.ds(start, count), :] + src[s, x + 1, pl.ds(start, count), :]
-                total = total + src[s, x, pl.ds(start - 1, count), :]
-                total = total + src[s, x, pl.ds(start + 1, count), :]
-                total = total + jnp.where(lane > 0, pltpu.roll(u, 1, 1), 0.0)
-                total = total + jnp.where(lane < DEPTH - 1, pltpu.roll(u, DEPTH - 1, 1), 0.0)
-                dst[s, x, pl.ds(start, count), :] = (
-                    centre * u - dst[s, x, pl.ds(start, count), :] + speed * total
-                )
-            return carry
-
-        lax.fori_loop(step, WIDE - step, body, 0, unroll=4)
-        if step < STEPS:
-            field = jnp.concatenate(
-                [dst[s, mid, ymid, :].reshape(TILE * TILE, DEPTH).astype(BF16) for s in range(shots)],
-                axis=1,
-            )
-            picked = jnp.dot(rows_hot[...], field, preferred_element_type=F32)
-            mask = jnp.concatenate([lanes_hot[...]] * shots, axis=1)
-            picked = (picked * mask).astype(BF16)
-            sel = (sel_row == (sel_col // DEPTH) * STEPS + (step - 1)).astype(F32).astype(BF16)
-            records = records + lax.dot_general(sel, picked, NT, preferred_element_type=F32)
-    records = records.astype(BF16)
-    for group in range(rec_out.shape[0]):
-        rec_out[group, pl.ds(0, shots * HIST), :] = history[...]
-        rec_out[group, pl.ds(shots * HIST, shots * STEPS), :] = records
-    out_next = pltpu.make_async_copy(bufs[STEPS % 2].at[:, mid, ymid], next_out, out_sems.at[0])
-    out_last = pltpu.make_async_copy(bufs[(STEPS - 1) % 2].at[:, mid, ymid], last_out, out_sems.at[1])
-    out_next.start()
-    out_last.start()
-    out_next.wait()
-    out_last.wait()
-
-
-def stencil(now, prev, speed, halos, rows_hot, lanes_hot, history):
-    shots = now.shape[0]
+        start, count = (PAD, WIDE) if step < 4 else (PAD + 4, WIDE - 8)
+        advance(src, dst, spd, (step, WIDE - step), start, count)
+        field = jnp.concatenate(
+            [dst[s, MID, YMID, :].reshape(TILE * TILE, DEPTH).astype(BF16) for s in range(shots)],
+            axis=1,
+        )
+        picked = jnp.dot(rows_hot[...], field, preferred_element_type=F32)
+        picked = (picked * mask).astype(BF16)
+        sel = (sel_row == (sel_col // DEPTH) * STEPS + (step - 1)).astype(F32).astype(BF16)
+        records = records + lax.dot_general(sel, picked, NT, preferred_element_type=F32)
+    rec[pl.ds(0, shots * HIST), :] = history[...]
+    rec[pl.ds(shots * HIST, shots * STEPS), :] = records.astype(BF16)
+    run(
+        [pltpu.make_async_copy(rec, rec_out.at[g], out_sems.at[g]) for g in range(8)]
+        + [
+            pltpu.make_async_copy(prv.at[:, NEAR, YNEAR], near_out, out_sems.at[8]),
+            pltpu.make_async_copy(cur.at[:, MID, YMID], before_out, out_sems.at[9]),
+        ]
+    )
+
+
+def stencil(cur, prv, spd, corners, rows_hot, lanes_hot, history):
+    shots = cur.shape[0]
     points = rows_hot.shape[0]
-    anywhere = pl.BlockSpec(memory_space=pl.ANY)
-    vmem = pl.BlockSpec(memory_space=pltpu.VMEM)
-    hbm = pl.BlockSpec(memory_space=pltpu.HBM)
-    wide = (shots, WIDE, WIDE + 2 * PAD, DEPTH)
     return pl.pallas_call(
         stencil_kernel,
         out_shape=(
-            jax.ShapeDtypeStruct(now.shape, F32),
-            jax.ShapeDtypeStruct(now.shape, F32),
             jax.ShapeDtypeStruct((8, shots * (HIST + STEPS), points), BF16),
+            jax.ShapeDtypeStruct((shots, TILE + 2, WIDE, DEPTH), F32),
+            jax.ShapeDtypeStruct((shots, TILE, TILE, DEPTH), F32),
+            jax.ShapeDtypeStruct(cur.shape, F32),
+            jax.ShapeDtypeStruct(cur.shape, F32),
+            jax.ShapeDtypeStruct(spd.shape, F32),
         ),
-        in_specs=[hbm] * 3 + [anywhere] * 8 + [vmem] * 3,
-        out_specs=(hbm, hbm, vmem),
+        in_specs=[VMEM] * 3 + [ANY] * 4 + [VMEM] * 3,
+        out_specs=(HBM,) * 3 + (VMEM,) * 3,
+        input_output_aliases={0: 3, 1: 4, 2: 5},
         scratch_shapes=[
-            pltpu.VMEM(wide, F32),
-            pltpu.VMEM(wide, F32),
-            pltpu.VMEM(wide[1:], F32),
-            pltpu.SemaphoreType.DMA((27,)),
-            pltpu.SemaphoreType.DMA((2,)),
+            pltpu.VMEM((shots * (HIST + STEPS), points), BF16),
+            pltpu.SemaphoreType.DMA((12,)),
+            pltpu.SemaphoreType.DMA((10,)),
         ],
-        compiler_params=pltpu.CompilerParams(vmem_limit_bytes=16 << 20),
+        compiler_params=pltpu.CompilerParams(vmem_limit_bytes=20 << 20),
         cost_estimate=pl.CostEstimate(flops=2_000_000_000, bytes_accessed=12_000_000, transcendentals=0),
         name="stencil",
-    )(*in_hbm(now, prev, speed), *halos, rows_hot, lanes_hot, history)
-
-
-def columns_kernel(delay, records, green, out):
+    )(cur, prv, spd, *corners, rows_hot, lanes_hot, history)
+
+
+def late_kernel(near, before, spd, cells, last, field, rows_hot, lanes_hot):
+    middle = slice(BAND, BAND + TILE)
+    last[...] = near[:, 1 : TILE + 1, middle, :]
+    field[...] = before[...]
+    advance(near, field, spd, (1, TILE + 1), BAND, TILE, shift=1, base=BAND)
+    points = cells.shape[1]
+    row_iota = lax.broadcasted_iota(jnp.int32, (TILE * TILE, points), 0)
+    lane_iota = lax.broadcasted_iota(jnp.int32, (DEPTH, points), 0)
+
+    def body(k, carry):
+        cell = cells[pl.ds(k, 1), :]
+        rows_hot[k] = (row_iota == lax.shift_right_logical(cell, 7)).astype(F32).astype(BF16)
+        lanes_hot[k] = (lane_iota == jnp.bitwise_and(cell, DEPTH - 1)).astype(F32).astype(BF16)
+        return carry
+
+    lax.fori_loop(0, cells.shape[0], body, 0)
+
+
+def late(near, before, speed, cells):
+    corners, points = cells.shape
+    return pl.pallas_call(
+        late_kernel,
+        out_shape=(
+            jax.ShapeDtypeStruct(before.shape, F32),
+            jax.ShapeDtypeStruct(before.shape, F32),
+            jax.ShapeDtypeStruct((corners, TILE * TILE, points), BF16),
+            jax.ShapeDtypeStruct((corners, DEPTH, points), BF16),
+        ),
+        in_specs=[VMEM] * 4,
+        out_specs=(VMEM,) * 4,
+        compiler_params=pltpu.CompilerParams(vmem_limit_bytes=20 << 20),
+        cost_estimate=pl.CostEstimate(flops=200_000_000, bytes_accessed=12_000_000, transcendentals=0),
+        name="late",
+    )(near, before, speed, cells)
+
+
+def columns_kernel(delay, records, green, pieces, out, sems):
     groups, rows, _ = records.shape
     rows = rows // 2
     half = rows // 2
@@ -190,11 +259,17 @@
             total = term if total is None else total + term
         parts.append(total)
     lane = lax.broadcasted_iota(jnp.int32, (groups * half, 128), 1)
+    copies = []
     for m in range(width // 128):
         a = parts[0][:, m * 128 : (m + 1) * 128]
         b = parts[1][:, m * 128 : (m + 1) * 128]
         out[2 * m] = jnp.where(lane < 64, a, pltpu.roll(b, 64, 1))
         out[2 * m + 1] = jnp.where(lane < 64, pltpu.roll(a, 64, 1), b)
+        pair = pl.ds(2 * m, 2)
+        copies.append(pltpu.make_async_copy(out.at[pair], pieces.at[pair], sems.at[m]))
+        copies[-1].start()
+    for copy in copies:
+        copy.wait()
 
 
 def columns(delay, records, green):
@@ -203,16 +278,26 @@
         columns_kernel,
         out_shape=jax.ShapeDtypeStruct((16, 128, 128), F32),
         in_specs=[pl.BlockSpec(memory_space=pltpu.SMEM), vmem, vmem],
-        out_specs=vmem,
+        out_specs=pl.BlockSpec(memory_space=pltpu.HBM),
+        scratch_shapes=[pltpu.VMEM((16, 128, 128), F32), pltpu.SemaphoreType.DMA((8,))],
         compiler_params=pltpu.CompilerParams(vmem_limit_bytes=12 << 20),
         cost_estimate=pl.CostEstimate(flops=1_000_000_000, bytes_accessed=4_000_000, transcendentals=0),
         name="columns",
     )(delay, records, green)
 
 
-def inject_kernel(em, cells, weights, field, wave_out, emission_out, rhs_high, rhs_low, acc, emission):
+def inject_kernel(
+    em, rows_in, lanes_in, weights, field,
+    wave_out, emission_out, rhs_high, rhs_low, acc, emission, rows_hot, lanes_hot, sems,
+):
+    count = weights.shape[0]
+    copies = []
+    for k in range(count):
+        copies.append(pltpu.make_async_copy(rows_in.at[k], rows_hot.at[k], sems.at[k]))
+        copies.append(pltpu.make_async_copy(lanes_in.at[k], lanes_hot.at[k], sems.at[count + k]))
+    for copy in copies:
+        copy.start()
     shots = field.shape[0]
-    points = cells.shape[1]
     lane = lax.broadcasted_iota(jnp.int32, (16, 128), 1)
     for tile in range(4):
         even, odd = em[2 * tile % 4, tile // 2], em[2 * tile % 4 + 1, tile // 2]
@@ -220,54 +305,55 @@
         emission[pl.ds(16, 16), pl.ds(tile * 128, 128)] = jnp.where(lane < 64, pltpu.roll(even, 64, 1), odd)
 
     acc[...] = jnp.zeros_like(acc)
-    row_iota = lax.broadcasted_iota(jnp.int32, (TILE * TILE, points), 0)
-    lane_iota = lax.broadcasted_iota(jnp.int32, (DEPTH, points), 0)
 
     def body(k, carry):
-        cell = cells[pl.ds(k, 1), :]
+        pltpu.make_async_copy(rows_in.at[k], rows_hot.at[k], sems.at[k]).wait()
+        pltpu.make_async_copy(lanes_in.at[k], lanes_hot.at[k], sems.at[count + k]).wait()
         weight = weights[pl.ds(k, 1), :]
-        rows_hot = (row_iota == lax.shift_right_logical(cell, 7)).astype(F32).astype(BF16)
-        lane_hot = lane_iota == jnp.bitwise_and(cell, DEPTH - 1)
+        hot = lanes_hot[k]
         for s in range(shots):
             value = weight * emission[pl.ds(s * STEPS + STEPS - 1, 1), :]
-            top = value.astype(BF16).astype(F32)
-            rest = value - top
-            rhs_high[pl.ds(s * DEPTH, DEPTH), :] = jnp.where(lane_hot, top, 0.0).astype(BF16)
-            rhs_low[pl.ds(s * DEPTH, DEPTH), :] = jnp.where(lane_hot, rest, 0.0).astype(BF16)
+            top = value.astype(BF16)
+            rest = (value - top.astype(F32)).astype(BF16)
+            rhs_high[pl.ds(s * DEPTH, DEPTH), :] = hot * top
+            rhs_low[pl.ds(s * DEPTH, DEPTH), :] = hot * rest
         acc[...] += lax.dot_general(
-            rows_hot, rhs_high[...], NT, preferred_element_type=F32
-        ) + lax.dot_general(rows_hot, rhs_low[...], NT, preferred_element_type=F32)
+            rows_hot[k], rhs_high[...], NT, preferred_element_type=F32
+        ) + lax.dot_general(rows_hot[k], rhs_low[...], NT, preferred_element_type=F32)
         return carry
 
-    lax.fori_loop(0, cells.shape[0], body, 0)
+    lax.fori_loop(0, weights.shape[0], body, 0)
     for row in range(shots * STEPS):
         emission_out[row] = emission[pl.ds(row, 1), :]
     for s in range(shots):
         wave_out[s] = field[s] + acc[:, s * DEPTH : (s + 1) * DEPTH].reshape(TILE, TILE, DEPTH)
 
 
-def inject(em, cells, weights, field):
+def inject(em, rows_hot, lanes_hot, weights, field):
     shots = field.shape[0]
-    points = cells.shape[1]
+    points = weights.shape[1]
     vmem = pl.BlockSpec(memory_space=pltpu.VMEM)
     return pl.pallas_call(
         inject_kernel,
         out_shape=(
-            jax.ShapeDtypeStruct(field.shape, F32),
+            jax.ShapeDtypeStruct((shots, TILE, TILE, DEPTH), F32),
             jax.ShapeDtypeStruct((shots * STEPS, 1, points), F32),
         ),
-        in_specs=[vmem] * 4,
+        in_specs=[vmem] + [pl.BlockSpec(memory_space=pltpu.HBM)] * 2 + [vmem] * 2,
         out_specs=(vmem, vmem),
         scratch_shapes=[
             pltpu.VMEM((shots * DEPTH, points), BF16),
             pltpu.VMEM((shots * DEPTH, points), BF16),
             pltpu.VMEM((TILE * TILE, shots * DEPTH), F32),
             pltpu.VMEM((shots * STEPS, points), F32),
+            pltpu.VMEM(rows_hot.shape, BF16),
+            pltpu.VMEM(lanes_hot.shape, BF16),
+            pltpu.SemaphoreType.DMA((2 * weights.shape[0],)),
         ],
         compiler_params=pltpu.CompilerParams(vmem_limit_bytes=12 << 20),
         cost_estimate=pl.CostEstimate(flops=4_000_000_000, bytes_accessed=4_000_000, transcendentals=0),
         name="inject",
-    )(em, cells, weights, field)
+    )(em, *in_hbm(rows_hot, lanes_hot), weights, field)
 
 
 def pack_kernel(now, prev, speed, xtail, ytail, xhead, yhead, field, sems):
@@ -393,8 +479,12 @@
     ).astype(F32)
     halos = halo_blocks(wave_now, wave_prev, courant)
     wide_green = gathered_green(green)
-    field, wave_last, records = stencil(
-        wave_now, wave_prev, courant, halos, rows_hot, lanes_hot, rec_history.reshape(shots * HIST, -1)
+    band = assemble(wave_now, wave_prev, courant, halos[:4])
+    records, near, before = stencil(
+        *band, halos[4:], rows_hot, lanes_hot, rec_history.reshape(shots * HIST, -1)
+    )[:3]
+    wave_last, field, cell_rows, cell_lanes = late(
+        *in_hbm(near), before, courant, emit_cells.reshape(emit_cells.shape[-2:])
     )
     records = row_exchange(records)
     partial = columns(lag_delay, records, wide_green)
@@ -410,7 +500,7 @@
         summed, "shot", 0, 0, tiled=True, axis_index_groups=COLUMN_GROUPS
     )
     wave_out, emission = inject(
-        em, emit_cells.reshape(emit_cells.shape[-2:]), emit_weights.reshape(emit_weights.shape[-2:]), field
+        em, cell_rows, cell_lanes, emit_weights.reshape(emit_weights.shape[-2:]), field
     )
     return wave_out, wave_last, emission.reshape(shots, STEPS, 1, 1, -1)
 

time: 138 us -> 140 us (1.014)
  blocking collectives: 43.9 us -> 28.8 us
  starting transfers between devices: 40.4 us -> 47.7 us
  Pallas kernels: 26.8 us -> 31.8 us
  local copies, waits for them, and re-layouts: 0.95 us -> 4.91 us
    all_to_all x1 -> x0, blocking collectives: 15.3 us -> none  [block(): lax.all_to_all(summed, 'shot', 0, 0, tiled=True, axis_index_groups=COLUMN...]
    all_to_all x0 -> x1, starting transfers between devices: none -> 7.18 us  [block(): lax.all_to_all(summed, 'shot', 0, 0, tiled=True, axis_index_groups=COLUMN...]
    unnamed x14 -> x22, local copies, waits for them, and re-layouts: 0.85 us -> 4.18 us
    pallas_call x2 -> x4, Pallas kernels: 20.3 us -> 23.2 us  [the longest x1 12.7 us: stencil(): pl.pallas_call(stencil_kernel, out_shape=(jax.ShapeDtypeStruct((8, shots...]
    all_to_all x0 -> x1, waiting for transfers between devices: none -> 2.77 us  [block(): lax.all_to_all(summed, 'shot', 0, 0, tiled=True, axis_index_groups=COLUMN...]
    pallas_call x1, Pallas kernels: 1.77 us -> 3.79 us  [columns(): pl.pallas_call(columns_kernel, out_shape=jax.ShapeDtypeStruct((16, 128, 1...]
  transfers between devices with their start and end apart: 12 -> 13, of which waited for: 8 -> 9; matrix products, arithmetic and copies ran while one was open for 1% -> 1% of each run, Pallas kernels for 14% -> 15%
where the time goes in v4:
time: 140 us
  starting transfers between devices  47.7 us (34%)
  Pallas kernels  31.8 us (23%)
  blocking collectives  28.8 us (21%)
  waiting for transfers between devices  24.4 us (17%)
  local copies, waits for them, and re-layouts  4.91 us (4%)
    all_to_all x1, blocking collectives, block(): lax.all_to_all(partial.reshape(4, 512, 128), 'tx', 0, 0, tiled=True)  15 us
    all_to_all x1, blocking collectives, block(): lax.all_to_all(partial, ('shot', 'ty'), 0, 0, tiled=True, axis_index_grou...  13.8 us
    all_to_all x1, starting transfers between devices, row_exchange(): lax.all_to_all(x, 'shot', split_axis=0, concat_axis=0, tiled=True, axis_i...  13 us
    pallas_call x1, Pallas kernels, stencil(): pl.pallas_call(stencil_kernel, out_shape=(jax.ShapeDtypeStruct((8, shots...  12.7 us
    all_to_all x1, waiting for transfers between devices, row_exchange(): lax.all_to_all(x, 'shot', split_axis=0, concat_axis=0, tiled=True, axis_i...  9.21 us
    all_to_all x1, starting transfers between devices, block(): lax.all_to_all(summed, 'shot', 0, 0, tiled=True, axis_index_groups=COLUMN...  7.18 us
    ppermute x3, starting transfers between devices, moved(): return lax.ppermute(block, 'shot', pairs)  6.94 us
    pallas_call x1, Pallas kernels, inject(): pl.pallas_call(inject_kernel, out_shape=(jax.ShapeDtypeStruct((shots, TIL...  5.92 us
  transfers between devices with their start and end apart: 13, of which 9 were waited for; matrix products, arithmetic and copies ran while one was open for 1% of the time, Pallas kernels for 15%

profile of v4, /device:TPU:8, one launch (start us, length us, event | category | flops | bytes accessed | tf_op | source)
XLA Modules:
  0.0 139.6 jit_solution(14747459784477132882)
XLA Ops:
  0.6 1.4 %pack.1 = (f32[9,8,16,128]{3,2,1,0:T(8,128)S(1)}, f32[9,16,8,128]{3,2,1,0:T(8,128)S(1)}, f32[9,8,16,128]{3,2,1,0:T(8,128)S(1)}, f32[9,16,8,128]{3,2,1,0:T(8,128)S(1)}) custom-call(f32[4,16,16,128]{3,2,1,0:T(8,128)} %now.3, f32[4,16,16,128]{3,2,1,0:T(8,128)} %prev.3, f32[16,16,128]{2,1,0:T(8,128)} %spd.1), custom_call_target="tpu_custom_call" | custom-call | bytes 4000000 | tf_op jit(solution)/shard_map/pack/pallas_call | solution.py:382
  2.0 4.3 %collective-permute-start.2 = (f32[9,16,8,128]{3,2,1,0:T(8,128)S(1)}, f32[9,16,8,128]{3,2,1,0:T(8,128)S(1)}, u32[]{:S(2)}, u32[]{:S(2)}) collective-permute-start(f32[9,16,8,128]{3,2,1,0:T(8,128)S(1)} %get-tuple-element.21), channel_id=1, source_target_pairs={{0,1},{1,2},{2,3},{4,5},{5,6},{6,7},{8,9},{9,10},{10,11},{12,13},{... | collective-permute-start | bytes 1769480 | tf_op jit(solution)/shard_map/ppermute | solution.py:401
  6.4 3.4 %collective-permute-start = (f32[9,8,16,128]{3,2,1,0:T(8,128)S(1)}, f32[9,8,16,128]{3,2,1,0:T(8,128)S(1)}, u32[]{:S(2)}, u32[]{:S(2)}) collective-permute-start(f32[9,8,16,128]{3,2,1,0:T(8,128)S(1)} %get-tuple-element.19), channel_id=1, source_target_pairs={{0,4},{4,8},{8,12},{1,5},{5,9},{9,13},{2,6},{6,10},{10,14},{3,7},{... | collective-permute-start | bytes 1769480 | tf_op jit(solution)/shard_map/ppermute | solution.py:400
  12.4 2.6 %collective-permute-start.8 = (bf16[2,512,256]{2,1,0:T(8,128)(2,1)}, bf16[2,512,256]{2,1,0:T(8,128)(2,1)S(1)}, u32[]{:S(2)}, u32[]{:S(2)}) collective-permute-start(bf16[2,512,256]{2,1,0:T(8,128)(2,1)} %own_in.1), channel_id=1, source_target_pairs={{0,32},{16,48},{32,0},{48,16},{64,96},{80,112},{96,64},{112,80},{1... | collective-permute-start | bytes 1572872 | tf_op jit(solution)/shard_map/ppermute | solution.py:447
  15.7 3.2 %collective-permute-done.2.ym = f32[9,16,8,128]{3,2,1,0:T(8,128)S(1)} collective-permute-done((f32[9,16,8,128]{3,2,1,0:T(8,128)S(1)}, f32[9,16,8,128]{3,2,1,0:T(8,128)S(1)}, u32[]{:S(2)}, u32[]{:S(2)}) %collective-permute-start.2) | collective-permute-done | bytes 589856 | tf_op jit(solution)/shard_map/ppermute | solution.py:401
  18.9 3.4 %collective-permute-start.4 = (f32[9,8,8,128]{3,2,1,0:T(8,128)S(1)}, f32[9,8,8,128]{3,2,1,0:T(8,128)S(1)}, u32[]{:S(2)}, u32[]{:S(2)}) collective-permute-start(f32[9,8,8,128]{3,2,1,0:T(8,128)S(1)} %slice.16), channel_id=1, source_target_pairs={{0,4},{4,8},{8,12},{1,5},{5,9},{9,13},{2,6},{6,10},{10,14},{3,7},{... | collective-permute-start | bytes 884744 | tf_op jit(solution)/shard_map/ppermute | solution.py:404
  24.0 2.2 %collective-permute-done.1.xp = f32[9,8,16,128]{3,2,1,0:T(8,128)S(1)} collective-permute-done((f32[9,8,16,128]{3,2,1,0:T(8,128)S(1)}, f32[9,8,16,128]{3,2,1,0:T(8,128)S(1)}, u32[]{:S(2)}, u32[]{:S(2)}) %collective-permute-start.1) | collective-permute-done | bytes 589856 | tf_op jit(solution)/shard_map/ppermute | solution.py:402
  26.2 4.3 %collective-permute-start.6 = (f32[9,8,8,128]{3,2,1,0:T(8,128)S(1)}, f32[9,8,8,128]{3,2,1,0:T(8,128)S(1)}, u32[]{:S(2)}, u32[]{:S(2)}) collective-permute-start(f32[9,8,8,128]{3,2,1,0:T(8,128)S(1)} %slice.18), channel_id=1, source_target_pairs={{0,1},{1,2},{2,3},{4,5},{5,6},{6,7},{8,9},{9,10},{10,11},{12,13},{... | collective-permute-start | bytes 884744 | tf_op jit(solution)/shard_map/ppermute | solution.py:405
  32.1 1.4 assemble.1
  35.3 4.2 %collective-permute-done.7.cpp = f32[9,8,8,128]{3,2,1,0:T(8,128)S(1)} collective-permute-done((f32[9,8,8,128]{3,2,1,0:T(8,128)S(1)}, f32[9,8,8,128]{3,2,1,0:T(8,128)S(1)}, u32[]{:S(2)}, u32[]{:S(2)}) %collective-permute-start.7) | collective-permute-done | bytes 294944 | tf_op jit(solution)/shard_map/ppermute | solution.py:406
  39.5 12.7 %stencil.1 = (bf16[8,64,512]{2,1,0:T(8,128)(2,1)}, f32[4,18,32,128]{3,2,1,0:T(8,128)S(1)}, f32[4,16,16,128]{3,2,1,0:T(8,128)S(1)}, f32[4,32,48,128]{3,2,1,0:T(8,...) custom-call(f32[4,32,48,128]{3,2,1,0:T(8,128)S(1)} %get-tuple-elemen, ...), custom_call_target="tpu_custom_call", output_to_operand_aliasing={{3}: (0, {}), {4}: (1, {}), {5}: (2, {})} | custom-call | flops 2000000000 | bytes 12000000 | tf_op jit(solution)/shard_map/stencil/pallas_call | solution.py:176
  53.2 13.0 %all-to-all-start = ((bf16[8,64,512]{2,1,0:T(8,128)(2,1)}), bf16[8,64,512]{2,1,0:T(8,128)(2,1)S(1)}, u32[]{:S(2)}, u32[]{:S(2)}) async-start(bf16[8,64,512]{2,1,0:T(8,128)(2,1)} %get-tuple-element.26), calls=%async_computation | async-start | bytes 1048576 | tf_op jit(solution)/shard_map/all_to_all | solution.py:51
  66.2 1.9 %collective-permute-start.9 = (bf16[2,512,256]{2,1,0:T(8,128)(2,1)S(1)}, bf16[2,512,256]{2,1,0:T(8,128)(2,1)S(1)}, u32[]{:S(2)}, u32[]{:S(2)}) collective-permute-start(bf16[2,512,256]{2,1,0:T(8,128)(2,1)S(1)} %copy-done.8), channel_id=1, source_target_pairs={{0,16},{16,0},{32,48},{48,32},{64,80},{80,64},{96,112},{112,96},{1... | collective-permute-start | bytes 1572872 | tf_op jit(solution)/shard_map/ppermute | solution.py:447
  68.1 2.4 %collective-permute-start.10 = (bf16[2,512,256]{2,1,0:T(8,128)(2,1)S(1)}, bf16[2,512,256]{2,1,0:T(8,128)(2,1)}, u32[]{:S(2)}, u32[]{:S(2)}) collective-permute-start(bf16[2,512,256]{2,1,0:T(8,128)(2,1)S(1)} %collective-permute-done.8.pair_in), channel_id=1, source_target_pairs={{0,16},{16,0},{32,48},{48,32},{64,80},{80,64},{96,112},{112,96},{1... | collective-permute-start | bytes 1572872 | tf_op jit(solution)/shard_map/ppermute | solution.py:447
  72.2 3.4 %order.1.green = bf16[2,512,1024]{2,1,0:T(8,128)(2,1)S(1)} custom-call(s32[2]{0:T(128)S(1)} %pad_add_fusion.place, bf16[2,512,256]{2,1,0:T(8,128)(2,1)} %own_in.1, bf16[2,512,256]{2,1,0:T(8,128)(2,1)} %copy-done.9, bf16[2,512,256]{2,1,0:T(8,128)(2,1)} %copy-done.10, bf16[2,512,256]{2,1,0:T(8,128)(2,1)} %collective-permute-done.10.diag_in), custom_call_target="tpu_custom_call" | custom-call | flops 1000000000 | bytes 4000000 | tf_op jit(solution)/shard_map/order/pallas_call | solution.py:456
  75.6 9.2 %all-to-all-done.records = bf16[8,64,512]{2,1,0:T(8,128)(2,1)S(1)} async-done(((bf16[8,64,512]{2,1,0:T(8,128)(2,1)}), bf16[8,64,512]{2,1,0:T(8,128)(2,1)S(1)}, u32[]{:S(2)}, u32[]{:S(2)}) %all-to-all-start) | async-done | bytes 524320 | tf_op jit(solution)/shard_map/all_to_all | solution.py:51
  84.8 3.8 %columns.1 = f32[16,128,128]{2,1,0:T(8,128)S(1)} custom-call(s32[2]{0:T(128)S(1)} %copy-done.7, bf16[8,64,512]{2,1,0:T(8,128)(2,1)S(1)} %all-to-all-done.records, bf16[2,512,1024]{2,1,0:T(8,128)(2,1)S(1)} %order.1.green), custom_call_target="tpu_custom_call" | custom-call | flops 1000000000 | bytes 4000000 | tf_op jit(solution)/shard_map/columns/pallas_call | solution.py:277
  88.7 15.0 %all_to_all.20 = f32[4,512,128]{2,1,0:T(8,128)S(1)} all-to-all(f32[4,512,128]{2,1,0:T(8,128)S(1)} %bitcast.21), channel_id=1, replica_groups=mesh['shot'=32,'tx'=4,'ty'=4] {'tx'}, dimensions={0} | all-to-all | bytes 2097152 | tf_op jit(solution)/shard_map/all_to_all | solution.py:491
  103.7 13.8 %all_to_all.21 = f32[8,64,128]{2,1,0:T(8,128)S(1)} all-to-all(f32[8,64,128]{2,1,0:T(8,128)S(1)} %bitcast.26), channel_id=1, replica_groups={{0,1,2,3,256,257,258,259},{16,17,18,19,272,273,274,275},{32,33,34,35,28..., dimensions={0} | all-to-all | bytes 524288 | tf_op jit(solution)/shard_map/all_to_all | solution.py:494
  118.2 7.2 %all-to-all-start.3 = ((f32[4,2,16,128]{3,2,1,0:T(8,128)}), f32[4,2,16,128]{3,2,1,0:T(8,128)S(1)}, u32[]{:S(2)}, u32[]{:S(2)}) async-start(f32[4,2,16,128]{3,2,1,0:T(8,128)} %bitcast.20), calls=%async_computation.3 | async-start | bytes 131072 | tf_op jit(solution)/shard_map/all_to_all | solution.py:499
  125.4 3.2 %late.1 = (f32[4,16,16,128]{3,2,1,0:T(8,128)}, f32[4,16,16,128]{3,2,1,0:T(8,128)S(1)}, bf16[8,256,512]{2,1,0:T(8,128)(2,1)S(1)}, bf16[8,128,512]{2,1,0:T(8,128)(2,1)S(1)}) custom-call(f32[4,18,32,128]{3,2,1,0:T(8,128)} %copy-done.1, f32[4,16,16,128]{3,2,1,0:T(8,128)S(1)} %get-tuple-element.28.before, f32[16,16,128]{2,1,0:T(8,128)S(1)} %copy-done, ...), custom_call_target="tpu_custom_call" | custom-call | flops 200000000 | bytes 12000000 | tf_op jit(solution)/shard_map/late/pallas_call | solution.py:220
  128.6 1.3 copy-done.4
  130.9 2.8 %all-to-all-done.3.em = f32[4,2,16,128]{3,2,1,0:T(8,128)S(1)} async-done(((f32[4,2,16,128]{3,2,1,0:T(8,128)}), f32[4,2,16,128]{3,2,1,0:T(8,128)S(1)}, u32[]{:S(2)}, u32[]{:S(2)}) %all-to-all-start.3) | async-done | bytes 65568 | tf_op jit(solution)/shard_map/all_to_all | solution.py:499
  133.6 5.9 %inject.1 = (f32[4,16,16,128]{3,2,1,0:T(8,128)}, f32[32,1,512]{2,1,0:T(1,128)}) custom-call(f32[4,2,16,128]{3,2,1,0:T(8,128)S(1)} %all-to-all-done.3.em, bf16[8,256,512]{2,1,0:T(8,128)(2,1)} %copy-done.4, bf16[8,128,512]{2,1,0:T(8,128)(2,1)} %copy-done.5, f32[8,512]{1,0:T(8,128)S(1)} %bitcast.24, f32[4,16,16,128]{3,2,1,0:T(8,128)S(1)} %get-tuple-element.31.field), custom_call_target="tpu_custom_call" | custom-call | flops 4000000000 | bytes 4000000 | tf_op jit(solution)/shard_map/inject/pallas_call | solution.py:336
  (45 shorter events, 12.8 us)
Async XLA Ops:
  2.0 16.9 %collective-permute-start.2 = (f32[9,16,8,128]{3,2,1,0:T(8,128)S(1)}, f32[9,16,8,128]{3,2,1,0:T(8,128)S(1)}, u32[]{:S(2)}, u32[]{:S(2)}) collective-permute-start(f32[9,16,8,128]{3,2,1,0:T(8,128)S(1)} %get-tuple-element.21), channel_id=1, source_target_pairs={{0,1},{1,2},{2,3},{4,5},{5,6},{6,7},{8,9},{9,10},{10,11},{12,13},{... | collective-permute-start | bytes 1769480 | tf_op jit(solution)/shard_map/ppermute | solution.py:401
  6.4 16.3 %collective-permute-start = (f32[9,8,16,128]{3,2,1,0:T(8,128)S(1)}, f32[9,8,16,128]{3,2,1,0:T(8,128)S(1)}, u32[]{:S(2)}, u32[]{:S(2)}) collective-permute-start(f32[9,8,16,128]{3,2,1,0:T(8,128)S(1)} %get-tuple-element.19), channel_id=1, source_target_pairs={{0,4},{4,8},{8,12},{1,5},{5,9},{9,13},{2,6},{6,10},{10,14},{3,7},{... | collective-permute-start | bytes 1769480 | tf_op jit(solution)/shard_map/ppermute | solution.py:400
  9.8 16.4 %collective-permute-start.1 = (f32[9,8,16,128]{3,2,1,0:T(8,128)S(1)}, f32[9,8,16,128]{3,2,1,0:T(8,128)S(1)}, u32[]{:S(2)}, u32[]{:S(2)}) collective-permute-start(f32[9,8,16,128]{3,2,1,0:T(8,128)S(1)} %get-tuple-element.20), channel_id=1, source_target_pairs={{4,0},{8,4},{12,8},{5,1},{9,5},{13,9},{6,2},{10,6},{14,10},{7,3},{... | collective-permute-start | bytes 1769480 | tf_op jit(solution)/shard_map/ppermute | solution.py:402
  11.1 19.4 %collective-permute-start.3 = (f32[9,16,8,128]{3,2,1,0:T(8,128)S(1)}, f32[9,16,8,128]{3,2,1,0:T(8,128)S(1)}, u32[]{:S(2)}, u32[]{:S(2)}) collective-permute-start(f32[9,16,8,128]{3,2,1,0:T(8,128)S(1)} %get-tuple-element.22), channel_id=1, source_target_pairs={{1,0},{2,1},{3,2},{5,4},{6,5},{7,6},{9,8},{10,9},{11,10},{13,12},{... | collective-permute-start | bytes 1769480 | tf_op jit(solution)/shard_map/ppermute | solution.py:403
  12.4 55.7 %collective-permute-start.8 = (bf16[2,512,256]{2,1,0:T(8,128)(2,1)}, bf16[2,512,256]{2,1,0:T(8,128)(2,1)S(1)}, u32[]{:S(2)}, u32[]{:S(2)}) collective-permute-start(bf16[2,512,256]{2,1,0:T(8,128)(2,1)} %own_in.1), channel_id=1, source_target_pairs={{0,32},{16,48},{32,0},{48,16},{64,96},{80,112},{96,64},{112,80},{1... | collective-permute-start | bytes 1572872 | tf_op jit(solution)/shard_map/ppermute | solution.py:447
  15.7 23.8 %copy-start.2 = (bf16[4,8,1,1,512]{4,1,3,2,0:T(8,128)(2,1)S(1)}, bf16[4,8,1,1,512]{4,1,3,2,0:T(8,128)(2,1)}, u32[]{:S(2)}) copy-start(bf16[4,8,1,1,512]{4,1,3,2,0:T(8,128)(2,1)} %param.13) | copy-start | bytes 98308
  18.9 14.6 %collective-permute-start.4 = (f32[9,8,8,128]{3,2,1,0:T(8,128)S(1)}, f32[9,8,8,128]{3,2,1,0:T(8,128)S(1)}, u32[]{:S(2)}, u32[]{:S(2)}) collective-permute-start(f32[9,8,8,128]{3,2,1,0:T(8,128)S(1)} %slice.16), channel_id=1, source_target_pairs={{0,4},{4,8},{8,12},{1,5},{5,9},{9,13},{2,6},{6,10},{10,14},{3,7},{... | collective-permute-start | bytes 884744 | tf_op jit(solution)/shard_map/ppermute | solution.py:404
  22.7 11.7 %collective-permute-start.5 = (f32[9,8,8,128]{3,2,1,0:T(8,128)S(1)}, f32[9,8,8,128]{3,2,1,0:T(8,128)S(1)}, u32[]{:S(2)}, u32[]{:S(2)}) collective-permute-start(f32[9,8,8,128]{3,2,1,0:T(8,128)S(1)} %slice.17), channel_id=1, source_target_pairs={{1,0},{2,1},{3,2},{5,4},{6,5},{7,6},{9,8},{10,9},{11,10},{13,12},{... | collective-permute-start | bytes 884744 | tf_op jit(solution)/shard_map/ppermute | solution.py:407
  26.2 9.1 %collective-permute-start.6 = (f32[9,8,8,128]{3,2,1,0:T(8,128)S(1)}, f32[9,8,8,128]{3,2,1,0:T(8,128)S(1)}, u32[]{:S(2)}, u32[]{:S(2)}) collective-permute-start(f32[9,8,8,128]{3,2,1,0:T(8,128)S(1)} %slice.18), channel_id=1, source_target_pairs={{0,1},{1,2},{2,3},{4,5},{5,6},{6,7},{8,9},{9,10},{10,11},{12,13},{... | collective-permute-start | bytes 884744 | tf_op jit(solution)/shard_map/ppermute | solution.py:405
  30.5 8.9 %collective-permute-start.7 = (f32[9,8,8,128]{3,2,1,0:T(8,128)S(1)}, f32[9,8,8,128]{3,2,1,0:T(8,128)S(1)}, u32[]{:S(2)}, u32[]{:S(2)}) collective-permute-start(f32[9,8,8,128]{3,2,1,0:T(8,128)S(1)} %slice.19), channel_id=1, source_target_pairs={{4,0},{8,4},{12,8},{5,1},{9,5},{13,9},{6,2},{10,6},{14,10},{7,3},{... | collective-permute-start | bytes 884744 | tf_op jit(solution)/shard_map/ppermute | solution.py:406
  39.5 26.7 %copy-start.8 = (bf16[2,512,256]{2,1,0:T(8,128)(2,1)S(1)}, bf16[2,512,256]{2,1,0:T(8,128)(2,1)}, u32[]{:S(2)}) copy-start(bf16[2,512,256]{2,1,0:T(8,128)(2,1)} %own_in.1) | copy-start | bytes 1572868
  52.2 1.1 copy-start.1
  53.2 31.6 %copy-start.7 = (s32[2]{0:T(128)S(1)}, s32[2]{0:T(128)}, u32[]{:S(2)}) copy-start(s32[2]{0:T(128)} %delay.1) | copy-start | bytes 28
  53.2 31.6 %all-to-all-start = ((bf16[8,64,512]{2,1,0:T(8,128)(2,1)}), bf16[8,64,512]{2,1,0:T(8,128)(2,1)S(1)}, u32[]{:S(2)}, u32[]{:S(2)}) async-start(bf16[8,64,512]{2,1,0:T(8,128)(2,1)} %get-tuple-element.26), calls=%async_computation | async-start | bytes 1048576 | tf_op jit(solution)/shard_map/all_to_all | solution.py:51
  66.2 4.5 %collective-permute-start.9 = (bf16[2,512,256]{2,1,0:T(8,128)(2,1)S(1)}, bf16[2,512,256]{2,1,0:T(8,128)(2,1)S(1)}, u32[]{:S(2)}, u32[]{:S(2)}) collective-permute-start(bf16[2,512,256]{2,1,0:T(8,128)(2,1)S(1)} %copy-done.8), channel_id=1, source_target_pairs={{0,16},{16,0},{32,48},{48,32},{64,80},{80,64},{96,112},{112,96},{1... | collective-permute-start | bytes 1572872 | tf_op jit(solution)/shard_map/ppermute | solution.py:447
  68.1 2.5 %copy-start.9 = (bf16[2,512,256]{2,1,0:T(8,128)(2,1)}, bf16[2,512,256]{2,1,0:T(8,128)(2,1)S(1)}, u32[]{:S(2)}) copy-start(bf16[2,512,256]{2,1,0:T(8,128)(2,1)S(1)} %collective-permute-done.8.pair_in) | copy-start | bytes 1572868
  68.1 4.1 %collective-permute-start.10 = (bf16[2,512,256]{2,1,0:T(8,128)(2,1)S(1)}, bf16[2,512,256]{2,1,0:T(8,128)(2,1)}, u32[]{:S(2)}, u32[]{:S(2)}) collective-permute-start(bf16[2,512,256]{2,1,0:T(8,128)(2,1)S(1)} %collective-permute-done.8.pair_in), channel_id=1, source_target_pairs={{0,16},{16,0},{32,48},{48,32},{64,80},{80,64},{96,112},{112,96},{1... | collective-permute-start | bytes 1572872 | tf_op jit(solution)/shard_map/ppermute | solution.py:447
  70.7 0.8 copy-start.10
  88.6 36.7 %copy-start = (f32[16,16,128]{2,1,0:T(8,128)S(1)}, f32[16,16,128]{2,1,0:T(8,128)}, u32[]{:S(2)}) copy-start(f32[16,16,128]{2,1,0:T(8,128)} %spd.1) | copy-start | bytes 393220
  88.7 36.7 %copy-start.3 = (s32[1,1,8,512]{3,2,1,0:T(8,128)S(1)}, s32[1,1,8,512]{3,2,1,0:T(8,128)}, u32[]{:S(2)}) copy-start(s32[1,1,8,512]{3,2,1,0:T(8,128)} %param.16) | copy-start | bytes 49156
  88.7 45.0 %copy-start.6 = (f32[1,1,8,512]{3,2,1,0:T(8,128)S(1)}, f32[1,1,8,512]{3,2,1,0:T(8,128)}, u32[]{:S(2)}) copy-start(f32[1,1,8,512]{3,2,1,0:T(8,128)} %param.17) | copy-start | bytes 49156
  118.2 15.4 %all-to-all-start.3 = ((f32[4,2,16,128]{3,2,1,0:T(8,128)}), f32[4,2,16,128]{3,2,1,0:T(8,128)S(1)}, u32[]{:S(2)}, u32[]{:S(2)}) async-start(f32[4,2,16,128]{3,2,1,0:T(8,128)} %bitcast.20), calls=%async_computation.3 | async-start | bytes 131072 | tf_op jit(solution)/shard_map/all_to_all | solution.py:499
  128.6 1.3 copy-start.4
  129.9 1.0 copy-start.5

commit v5 on v4

--- a/solution.py
+++ b/solution.py
@@ -59,8 +59,6 @@
 YLOW = slice(PAD, PAD + BAND)
 YMID = slice(PAD + BAND, PAD + BAND + TILE)
 YHIGH = slice(PAD + BAND + TILE, PAD + WIDE)
-NEAR = slice(BAND - 1, BAND + TILE + 1)
-YNEAR = slice(PAD, PAD + WIDE)
 HBM = pl.BlockSpec(memory_space=pltpu.HBM)
 ANY = pl.BlockSpec(memory_space=pl.ANY)
 VMEM = pl.BlockSpec(memory_space=pltpu.VMEM)
@@ -115,12 +113,12 @@
     )(*in_hbm(now, prev, speed), *halos)
 
 
-def advance(src, dst, spd, rows, start, count, shift=0, base=0):
+def advance(src, dst, spd, rows, start, count):
     lane = lax.broadcasted_iota(jnp.int32, (count, DEPTH), 1)
 
     def body(x, carry):
-        at, cells = x - shift, pl.ds(start - base, count)
-        speed = spd[at, cells, :]
+        cells = pl.ds(start, count)
+        speed = spd[x, cells, :]
         centre = 2.0 - 6.0 * speed
         for s in range(src.shape[0]):
             u = src[s, x, pl.ds(start, count), :]
@@ -129,15 +127,15 @@
             total = total + src[s, x, pl.ds(start + 1, count), :]
             total = total + jnp.where(lane > 0, pltpu.roll(u, 1, 1), 0.0)
             total = total + jnp.where(lane < DEPTH - 1, pltpu.roll(u, DEPTH - 1, 1), 0.0)
-            dst[s, at, cells, :] = centre * u - dst[s, at, cells, :] + speed * total
+            dst[s, x, cells, :] = centre * u - dst[s, x, cells, :] + speed * total
         return carry
 
-    lax.fori_loop(*rows, body, 0, unroll=4)
+    lax.fori_loop(*rows, body, 0, unroll=8)
 
 
 def stencil_kernel(
     cur_in, prv_in, spd_in, cmm, cmp, cpm, cpp, rows_hot, lanes_hot, history,
-    rec_out, near_out, before_out, cur, prv, spd, rec, sems, out_sems,
+    rec_out, next_out, last_out, cur, prv, spd, rec, sems, out_sems,
 ):
     shots = cur.shape[0]
     blocks = ((cmm, LOW, YLOW), (cmp, LOW, YHIGH), (cpm, HIGH, YLOW), (cpp, HIGH, YHIGH))
@@ -159,15 +157,16 @@
         picked = (picked * mask).astype(BF16)
         sel = (sel_row == (sel_col // DEPTH) * STEPS + (step - 1)).astype(F32).astype(BF16)
         records = records + lax.dot_general(sel, picked, NT, preferred_element_type=F32)
+    last = pltpu.make_async_copy(prv.at[:, MID, YMID], last_out, out_sems.at[8])
+    last.start()
+    advance(prv, cur, spd, (STEPS, WIDE - STEPS), PAD + BAND, TILE)
     rec[pl.ds(0, shots * HIST), :] = history[...]
     rec[pl.ds(shots * HIST, shots * STEPS), :] = records.astype(BF16)
     run(
         [pltpu.make_async_copy(rec, rec_out.at[g], out_sems.at[g]) for g in range(8)]
-        + [
-            pltpu.make_async_copy(prv.at[:, NEAR, YNEAR], near_out, out_sems.at[8]),
-            pltpu.make_async_copy(cur.at[:, MID, YMID], before_out, out_sems.at[9]),
-        ]
-    )
+        + [pltpu.make_async_copy(cur.at[:, MID, YMID], next_out, out_sems.at[9])]
+    )
+    last.wait()
 
 
 def stencil(cur, prv, spd, corners, rows_hot, lanes_hot, history):
@@ -177,7 +176,7 @@
         stencil_kernel,
         out_shape=(
             jax.ShapeDtypeStruct((8, shots * (HIST + STEPS), points), BF16),
-            jax.ShapeDtypeStruct((shots, TILE + 2, WIDE, DEPTH), F32),
+            jax.ShapeDtypeStruct((shots, TILE, TILE, DEPTH), F32),
             jax.ShapeDtypeStruct((shots, TILE, TILE, DEPTH), F32),
             jax.ShapeDtypeStruct(cur.shape, F32),
             jax.ShapeDtypeStruct(cur.shape, F32),
@@ -197,43 +196,7 @@
     )(cur, prv, spd, *corners, rows_hot, lanes_hot, history)
 
 
-def late_kernel(near, before, spd, cells, last, field, rows_hot, lanes_hot):
-    middle = slice(BAND, BAND + TILE)
-    last[...] = near[:, 1 : TILE + 1, middle, :]
-    field[...] = before[...]
-    advance(near, field, spd, (1, TILE + 1), BAND, TILE, shift=1, base=BAND)
-    points = cells.shape[1]
-    row_iota = lax.broadcasted_iota(jnp.int32, (TILE * TILE, points), 0)
-    lane_iota = lax.broadcasted_iota(jnp.int32, (DEPTH, points), 0)
-
-    def body(k, carry):
-        cell = cells[pl.ds(k, 1), :]
-        rows_hot[k] = (row_iota == lax.shift_right_logical(cell, 7)).astype(F32).astype(BF16)
-        lanes_hot[k] = (lane_iota == jnp.bitwise_and(cell, DEPTH - 1)).astype(F32).astype(BF16)
-        return carry
-
-    lax.fori_loop(0, cells.shape[0], body, 0)
-
-
-def late(near, before, speed, cells):
-    corners, points = cells.shape
-    return pl.pallas_call(
-        late_kernel,
-        out_shape=(
-            jax.ShapeDtypeStruct(before.shape, F32),
-            jax.ShapeDtypeStruct(before.shape, F32),
-            jax.ShapeDtypeStruct((corners, TILE * TILE, points), BF16),
-            jax.ShapeDtypeStruct((corners, DEPTH, points), BF16),
-        ),
-        in_specs=[VMEM] * 4,
-        out_specs=(VMEM,) * 4,
-        compiler_params=pltpu.CompilerParams(vmem_limit_bytes=20 << 20),
-        cost_estimate=pl.CostEstimate(flops=200_000_000, bytes_accessed=12_000_000, transcendentals=0),
-        name="late",
-    )(near, before, speed, cells)
-
-
-def columns_kernel(delay, records, green, pieces, out, sems):
+def columns_kernel(delay, records, green, out):
     groups, rows, _ = records.shape
     rows = rows // 2
     half = rows // 2
@@ -259,17 +222,11 @@
             total = term if total is None else total + term
         parts.append(total)
     lane = lax.broadcasted_iota(jnp.int32, (groups * half, 128), 1)
-    copies = []
     for m in range(width // 128):
         a = parts[0][:, m * 128 : (m + 1) * 128]
         b = parts[1][:, m * 128 : (m + 1) * 128]
         out[2 * m] = jnp.where(lane < 64, a, pltpu.roll(b, 64, 1))
         out[2 * m + 1] = jnp.where(lane < 64, pltpu.roll(a, 64, 1), b)
-        pair = pl.ds(2 * m, 2)
-        copies.append(pltpu.make_async_copy(out.at[pair], pieces.at[pair], sems.at[m]))
-        copies[-1].start()
-    for copy in copies:
-        copy.wait()
 
 
 def columns(delay, records, green):
@@ -278,26 +235,16 @@
         columns_kernel,
         out_shape=jax.ShapeDtypeStruct((16, 128, 128), F32),
         in_specs=[pl.BlockSpec(memory_space=pltpu.SMEM), vmem, vmem],
-        out_specs=pl.BlockSpec(memory_space=pltpu.HBM),
-        scratch_shapes=[pltpu.VMEM((16, 128, 128), F32), pltpu.SemaphoreType.DMA((8,))],
+        out_specs=vmem,
         compiler_params=pltpu.CompilerParams(vmem_limit_bytes=12 << 20),
         cost_estimate=pl.CostEstimate(flops=1_000_000_000, bytes_accessed=4_000_000, transcendentals=0),
         name="columns",
     )(delay, records, green)
 
 
-def inject_kernel(
-    em, rows_in, lanes_in, weights, field,
-    wave_out, emission_out, rhs_high, rhs_low, acc, emission, rows_hot, lanes_hot, sems,
-):
-    count = weights.shape[0]
-    copies = []
-    for k in range(count):
-        copies.append(pltpu.make_async_copy(rows_in.at[k], rows_hot.at[k], sems.at[k]))
-        copies.append(pltpu.make_async_copy(lanes_in.at[k], lanes_hot.at[k], sems.at[count + k]))
-    for copy in copies:
-        copy.start()
+def inject_kernel(em, cells, weights, field, wave_out, emission_out, rhs_high, rhs_low, acc, emission):
     shots = field.shape[0]
+    points = cells.shape[1]
     lane = lax.broadcasted_iota(jnp.int32, (16, 128), 1)
     for tile in range(4):
         even, odd = em[2 * tile % 4, tile // 2], em[2 * tile % 4 + 1, tile // 2]
@@ -305,73 +252,70 @@
         emission[pl.ds(16, 16), pl.ds(tile * 128, 128)] = jnp.where(lane < 64, pltpu.roll(even, 64, 1), odd)
 
     acc[...] = jnp.zeros_like(acc)
+    row_iota = lax.broadcasted_iota(jnp.int32, (TILE * TILE, points), 0)
+    lane_iota = lax.broadcasted_iota(jnp.int32, (DEPTH, points), 0)
 
     def body(k, carry):
-        pltpu.make_async_copy(rows_in.at[k], rows_hot.at[k], sems.at[k]).wait()
-        pltpu.make_async_copy(lanes_in.at[k], lanes_hot.at[k], sems.at[count + k]).wait()
+        cell = cells[pl.ds(k, 1), :]
         weight = weights[pl.ds(k, 1), :]
-        hot = lanes_hot[k]
+        rows_hot = (row_iota == lax.shift_right_logical(cell, 7)).astype(F32).astype(BF16)
+        lane_hot = lane_iota == jnp.bitwise_and(cell, DEPTH - 1)
         for s in range(shots):
             value = weight * emission[pl.ds(s * STEPS + STEPS - 1, 1), :]
-            top = value.astype(BF16)
-            rest = (value - top.astype(F32)).astype(BF16)
-            rhs_high[pl.ds(s * DEPTH, DEPTH), :] = hot * top
-            rhs_low[pl.ds(s * DEPTH, DEPTH), :] = hot * rest
+            top = value.astype(BF16).astype(F32)
+            rest = value - top
+            rhs_high[pl.ds(s * DEPTH, DEPTH), :] = jnp.where(lane_hot, top, 0.0).astype(BF16)
+            rhs_low[pl.ds(s * DEPTH, DEPTH), :] = jnp.where(lane_hot, rest, 0.0).astype(BF16)
         acc[...] += lax.dot_general(
-            rows_hot[k], rhs_high[...], NT, preferred_element_type=F32
-        ) + lax.dot_general(rows_hot[k], rhs_low[...], NT, preferred_element_type=F32)
+            rows_hot, rhs_high[...], NT, preferred_element_type=F32
+        ) + lax.dot_general(rows_hot, rhs_low[...], NT, preferred_element_type=F32)
         return carry
 
-    lax.fori_loop(0, weights.shape[0], body, 0)
+    lax.fori_loop(0, cells.shape[0], body, 0, unroll=4)
     for row in range(shots * STEPS):
         emission_out[row] = emission[pl.ds(row, 1), :]
     for s in range(shots):
         wave_out[s] = field[s] + acc[:, s * DEPTH : (s + 1) * DEPTH].reshape(TILE, TILE, DEPTH)
 
 
-def inject(em, rows_hot, lanes_hot, weights, field):
+def inject(em, cells, weights, field):
     shots = field.shape[0]
-    points = weights.shape[1]
+    points = cells.shape[1]
     vmem = pl.BlockSpec(memory_space=pltpu.VMEM)
     return pl.pallas_call(
         inject_kernel,
         out_shape=(
-            jax.ShapeDtypeStruct((shots, TILE, TILE, DEPTH), F32),
+            jax.ShapeDtypeStruct(field.shape, F32),
             jax.ShapeDtypeStruct((shots * STEPS, 1, points), F32),
         ),
-        in_specs=[vmem] + [pl.BlockSpec(memory_space=pltpu.HBM)] * 2 + [vmem] * 2,
+        in_specs=[vmem] * 4,
         out_specs=(vmem, vmem),
         scratch_shapes=[
             pltpu.VMEM((shots * DEPTH, points), BF16),
             pltpu.VMEM((shots * DEPTH, points), BF16),
             pltpu.VMEM((TILE * TILE, shots * DEPTH), F32),
             pltpu.VMEM((shots * STEPS, points), F32),
-            pltpu.VMEM(rows_hot.shape, BF16),
-            pltpu.VMEM(lanes_hot.shape, BF16),
-            pltpu.SemaphoreType.DMA((2 * weights.shape[0],)),
         ],
         compiler_params=pltpu.CompilerParams(vmem_limit_bytes=12 << 20),
         cost_estimate=pl.CostEstimate(flops=4_000_000_000, bytes_accessed=4_000_000, transcendentals=0),
         name="inject",
-    )(em, *in_hbm(rows_hot, lanes_hot), weights, field)
-
-
-def pack_kernel(now, prev, speed, xtail, ytail, xhead, yhead, field, sems):
+    )(em, cells, weights, field)
+
+
+def pack_kernel(now, prev, speed, xtail, ytail, xhead, yhead, sems):
     shots = now.shape[0]
-    copies = [
-        pltpu.make_async_copy(now, field.at[pl.ds(0, shots)], sems.at[0]),
-        pltpu.make_async_copy(prev, field.at[pl.ds(shots, shots)], sems.at[1]),
-        pltpu.make_async_copy(speed, field.at[2 * shots], sems.at[2]),
-    ]
-    for copy in copies:
-        copy.start()
-    for copy in copies:
-        copy.wait()
-    head, tail = slice(0, BAND), slice(TILE - BAND, TILE)
-    xtail[...] = field[:, tail]
-    ytail[...] = field[:, :, tail]
-    xhead[...] = field[:, head]
-    yhead[...] = field[:, :, head]
+    whole, head, tail = slice(None), slice(0, BAND), slice(TILE - BAND, TILE)
+    copies = []
+    for out, xs, ys in (
+        (ytail, whole, tail), (xtail, tail, whole), (xhead, head, whole), (yhead, whole, head),
+    ):
+        for src, dst in (
+            (now.at[:, xs, ys], out.at[pl.ds(0, shots)]),
+            (prev.at[:, xs, ys], out.at[pl.ds(shots, shots)]),
+            (speed.at[xs, ys], out.at[2 * shots]),
+        ):
+            copies.append(pltpu.make_async_copy(src, dst, sems.at[len(copies)]))
+    run(copies)
 
 
 def packed(now, prev, speed):
@@ -384,10 +328,7 @@
         out_shape=(across, along, across, along),
         in_specs=[pl.BlockSpec(memory_space=pltpu.HBM)] * 3,
         out_specs=(vmem,) * 4,
-        scratch_shapes=[
-            pltpu.VMEM((fields, TILE, TILE, DEPTH), F32),
-            pltpu.SemaphoreType.DMA((3,)),
-        ],
+        scratch_shapes=[pltpu.SemaphoreType.DMA((12,))],
         compiler_params=pltpu.CompilerParams(vmem_limit_bytes=8 << 20),
         cost_estimate=pl.CostEstimate(flops=0, bytes_accessed=4_000_000, transcendentals=0),
         name="pack",
@@ -480,12 +421,9 @@
     halos = halo_blocks(wave_now, wave_prev, courant)
     wide_green = gathered_green(green)
     band = assemble(wave_now, wave_prev, courant, halos[:4])
-    records, near, before = stencil(
+    records, field, wave_last = stencil(
         *band, halos[4:], rows_hot, lanes_hot, rec_history.reshape(shots * HIST, -1)
     )[:3]
-    wave_last, field, cell_rows, cell_lanes = late(
-        *in_hbm(near), before, courant, emit_cells.reshape(emit_cells.shape[-2:])
-    )
     records = row_exchange(records)
     partial = columns(lag_delay, records, wide_green)
     partial = lax.all_to_all(partial.reshape(4, 512, 128), "tx", 0, 0, tiled=True)
@@ -500,7 +438,7 @@
         summed, "shot", 0, 0, tiled=True, axis_index_groups=COLUMN_GROUPS
     )
     wave_out, emission = inject(
-        em, cell_rows, cell_lanes, emit_weights.reshape(emit_weights.shape[-2:]), field
+        em, emit_cells.reshape(emit_cells.shape[-2:]), emit_weights.reshape(emit_weights.shape[-2:]), field
     )
     return wave_out, wave_last, emission.reshape(shots, STEPS, 1, 1, -1)
 

time: 140 us -> 134 us (0.957)
  blocking collectives: 28.8 us -> 43.9 us
  starting transfers between devices: 47.7 us -> 40.4 us
  Pallas kernels: 31.8 us -> 24.5 us
  local copies, waits for them, and re-layouts: 4.91 us -> 0.95 us
  waiting for transfers between devices: 24.4 us -> 21.6 us
    all_to_all x0 -> x1, blocking collectives: none -> 15.3 us  [block(): lax.all_to_all(summed, 'shot', 0, 0, tiled=True, axis_index_groups=COLUMN...]
    all_to_all x1 -> x0, starting transfers between devices: 7.18 us -> none  [block(): lax.all_to_all(summed, 'shot', 0, 0, tiled=True, axis_index_groups=COLUMN...]
    pallas_call x2 -> x1, Pallas kernels: 9.11 us -> 3.55 us  [inject(): pl.pallas_call(inject_kernel, out_shape=(jax.ShapeDtypeStruct(field.shape...]
    unnamed x22 -> x14, local copies, waits for them, and re-layouts: 4.18 us -> 0.85 us
    all_to_all x1 -> x0, waiting for transfers between devices: 2.77 us -> none  [block(): lax.all_to_all(summed, 'shot', 0, 0, tiled=True, axis_index_groups=COLUMN...]
    pallas_call x1, Pallas kernels: 3.79 us -> 1.78 us  [columns(): pl.pallas_call(columns_kernel, out_shape=jax.ShapeDtypeStruct((16, 128, 1...]
  transfers between devices with their start and end apart: 13 -> 12, of which waited for: 9 -> 8; matrix products, arithmetic and copies ran while one was open for 1% -> 1% of each run, Pallas kernels for 15% -> 13%
where the time goes in v5:
time: 134 us; the launch traced here: 133 us
  blocking collectives  43.9 us (33%)
  starting transfers between devices  40.4 us (30%)
  Pallas kernels  24.5 us (18%)
  waiting for transfers between devices  21.6 us (16%)
    all_to_all x1, blocking collectives, block(): lax.all_to_all(summed, 'shot', 0, 0, tiled=True, axis_index_groups=COLUMN...  15.3 us
    all_to_all x1, blocking collectives, block(): lax.all_to_all(partial.reshape(4, 512, 128), 'tx', 0, 0, tiled=True)  14.9 us
    all_to_all x1, blocking collectives, block(): lax.all_to_all(partial, ('shot', 'ty'), 0, 0, tiled=True, axis_index_grou...  13.8 us
    all_to_all x1, starting transfers between devices, row_exchange(): lax.all_to_all(x, 'shot', split_axis=0, concat_axis=0, tiled=True, axis_i...  12.9 us
    pallas_call x1, Pallas kernels, stencil(): pl.pallas_call(stencil_kernel, out_shape=(jax.ShapeDtypeStruct((8, shots...  12.7 us
    all_to_all x1, waiting for transfers between devices, row_exchange(): lax.all_to_all(x, 'shot', split_axis=0, concat_axis=0, tiled=True, axis_i...  9.17 us
    ppermute x3, starting transfers between devices, moved(): return lax.ppermute(block, 'shot', pairs)  6.94 us
    ppermute x1, starting transfers between devices, halo_blocks(): ym = lax.ppermute(ytail, 'ty', UP)  4.31 us
  transfers between devices with their start and end apart: 12, of which 8 were waited for; matrix products, arithmetic and copies ran while one was open for 1% of the time, Pallas kernels for 13%

profile of v5, /device:TPU:8, one launch (start us, length us, event | category | flops | bytes accessed | tf_op | source)
XLA Modules:
  0.0 133.4 jit_solution(5399916736623158921)
XLA Ops:
  0.6 1.7 %pack.1 = (f32[9,8,16,128]{3,2,1,0:T(8,128)S(1)}, f32[9,16,8,128]{3,2,1,0:T(8,128)S(1)}, f32[9,8,16,128]{3,2,1,0:T(8,128)S(1)}, f32[9,16,8,128]{3,2,1,0:T(8,128)S(1)}) custom-call(f32[4,16,16,128]{3,2,1,0:T(8,128)} %now.3, f32[4,16,16,128]{3,2,1,0:T(8,128)} %prev.3, f32[16,16,128]{2,1,0:T(8,128)} %speed.3), custom_call_target="tpu_custom_call" | custom-call | bytes 4000000 | tf_op jit(solution)/shard_map/pack/pallas_call | solution.py:326
  2.3 4.3 %collective-permute-start.2 = (f32[9,16,8,128]{3,2,1,0:T(8,128)S(1)}, f32[9,16,8,128]{3,2,1,0:T(8,128)S(1)}, u32[]{:S(2)}, u32[]{:S(2)}) collective-permute-start(f32[9,16,8,128]{3,2,1,0:T(8,128)S(1)} %get-tuple-element.17), channel_id=1, source_target_pairs={{0,1},{1,2},{2,3},{4,5},{5,6},{6,7},{8,9},{9,10},{10,11},{12,13},{... | collective-permute-start | bytes 1769480 | tf_op jit(solution)/shard_map/ppermute | solution.py:342
  6.7 3.4 %collective-permute-start = (f32[9,8,16,128]{3,2,1,0:T(8,128)S(1)}, f32[9,8,16,128]{3,2,1,0:T(8,128)S(1)}, u32[]{:S(2)}, u32[]{:S(2)}) collective-permute-start(f32[9,8,16,128]{3,2,1,0:T(8,128)S(1)} %get-tuple-element.15), channel_id=1, source_target_pairs={{0,4},{4,8},{8,12},{1,5},{5,9},{9,13},{2,6},{6,10},{10,14},{3,7},{... | collective-permute-start | bytes 1769480 | tf_op jit(solution)/shard_map/ppermute | solution.py:341
  10.1 1.3 collective-permute-start.1
  11.4 1.3 collective-permute-start.3
  12.7 2.6 %collective-permute-start.8 = (bf16[2,512,256]{2,1,0:T(8,128)(2,1)}, bf16[2,512,256]{2,1,0:T(8,128)(2,1)S(1)}, u32[]{:S(2)}, u32[]{:S(2)}) collective-permute-start(bf16[2,512,256]{2,1,0:T(8,128)(2,1)} %own_in.1), channel_id=1, source_target_pairs={{0,32},{16,48},{32,0},{48,16},{64,96},{80,112},{96,64},{112,80},{1... | collective-permute-start | bytes 1572872 | tf_op jit(solution)/shard_map/ppermute | solution.py:388
  16.0 3.2 %collective-permute-done.2.ym = f32[9,16,8,128]{3,2,1,0:T(8,128)S(1)} collective-permute-done((f32[9,16,8,128]{3,2,1,0:T(8,128)S(1)}, f32[9,16,8,128]{3,2,1,0:T(8,128)S(1)}, u32[]{:S(2)}, u32[]{:S(2)}) %collective-permute-start.2) | collective-permute-done | bytes 589856 | tf_op jit(solution)/shard_map/ppermute | solution.py:342
  19.2 3.4 %collective-permute-start.4 = (f32[9,8,8,128]{3,2,1,0:T(8,128)S(1)}, f32[9,8,8,128]{3,2,1,0:T(8,128)S(1)}, u32[]{:S(2)}, u32[]{:S(2)}) collective-permute-start(f32[9,8,8,128]{3,2,1,0:T(8,128)S(1)} %slice.16), channel_id=1, source_target_pairs={{0,4},{4,8},{8,12},{1,5},{5,9},{9,13},{2,6},{6,10},{10,14},{3,7},{... | collective-permute-start | bytes 884744 | tf_op jit(solution)/shard_map/ppermute | solution.py:345
  23.0 1.3 collective-permute-start.5
  24.3 2.2 %collective-permute-done.1.xp = f32[9,8,16,128]{3,2,1,0:T(8,128)S(1)} collective-permute-done((f32[9,8,16,128]{3,2,1,0:T(8,128)S(1)}, f32[9,8,16,128]{3,2,1,0:T(8,128)S(1)}, u32[]{:S(2)}, u32[]{:S(2)}) %collective-permute-start.1) | collective-permute-done | bytes 589856 | tf_op jit(solution)/shard_map/ppermute | solution.py:343
  26.5 4.3 %collective-permute-start.6 = (f32[9,8,8,128]{3,2,1,0:T(8,128)S(1)}, f32[9,8,8,128]{3,2,1,0:T(8,128)S(1)}, u32[]{:S(2)}, u32[]{:S(2)}) collective-permute-start(f32[9,8,8,128]{3,2,1,0:T(8,128)S(1)} %slice.18), channel_id=1, source_target_pairs={{0,1},{1,2},{2,3},{4,5},{5,6},{6,7},{8,9},{9,10},{10,11},{12,13},{... | collective-permute-start | bytes 884744 | tf_op jit(solution)/shard_map/ppermute | solution.py:346
  32.4 1.4 %assemble.1 = (f32[4,32,48,128]{3,2,1,0:T(8,128)S(1)}, f32[4,32,48,128]{3,2,1,0:T(8,128)S(1)}, f32[32,48,128]{2,1,0:T(8,128)S(1)}) custom-call(f32[4,16,16,128]{3,2,1,0:T(8,128)} %now.3, f32[4,16,16,128]{3,2,1,0:T(8,128)} %prev.3, f32[16,16,128]{2,1,0:T(8,128)} %speed.3, f32[9,8,16,128]{3,2,1,0:T(8,128)S(1)} %collective-permute-done.xm, ...), custom_call_target="tpu_custom_call" | custom-call | bytes 8000000 | tf_op jit(solution)/shard_map/assemble/pallas_call | solution.py:100
  35.6 4.2 %collective-permute-done.7.cpp = f32[9,8,8,128]{3,2,1,0:T(8,128)S(1)} collective-permute-done((f32[9,8,8,128]{3,2,1,0:T(8,128)S(1)}, f32[9,8,8,128]{3,2,1,0:T(8,128)S(1)}, u32[]{:S(2)}, u32[]{:S(2)}) %collective-permute-start.7) | collective-permute-done | bytes 294944 | tf_op jit(solution)/shard_map/ppermute | solution.py:347
  39.8 12.7 %stencil.1 = (bf16[8,64,512]{2,1,0:T(8,128)(2,1)}, f32[4,16,16,128]{3,2,1,0:T(8,128)S(1)}, f32[4,16,16,128]{3,2,1,0:T(8,128)}, f32[4,32,48,128]{3,2,1,0:T(8,128)...) custom-call(f32[4,32,48,128]{3,2,1,0:T(8,128)S(1)} %get-tuple-elemen, ...), custom_call_target="tpu_custom_call", output_to_operand_aliasing={{3}: (0, {}), {4}: (1, {}), {5}: (2, {})} | custom-call | flops 2000000000 | bytes 12000000 | tf_op jit(solution)/shard_map/stencil/pallas_call | solution.py:175
  52.5 12.9 %all-to-all-start = ((bf16[8,64,512]{2,1,0:T(8,128)(2,1)}), bf16[8,64,512]{2,1,0:T(8,128)(2,1)S(1)}, u32[]{:S(2)}, u32[]{:S(2)}) async-start(bf16[8,64,512]{2,1,0:T(8,128)(2,1)} %get-tuple-element.22), calls=%async_computation | async-start | bytes 1048576 | tf_op jit(solution)/shard_map/all_to_all | solution.py:51
  65.3 1.9 %collective-permute-start.9 = (bf16[2,512,256]{2,1,0:T(8,128)(2,1)S(1)}, bf16[2,512,256]{2,1,0:T(8,128)(2,1)S(1)}, u32[]{:S(2)}, u32[]{:S(2)}) collective-permute-start(bf16[2,512,256]{2,1,0:T(8,128)(2,1)S(1)} %copy-done.4), channel_id=1, source_target_pairs={{0,16},{16,0},{32,48},{48,32},{64,80},{80,64},{96,112},{112,96},{1... | collective-permute-start | bytes 1572872 | tf_op jit(solution)/shard_map/ppermute | solution.py:388
  67.3 2.4 %collective-permute-start.10 = (bf16[2,512,256]{2,1,0:T(8,128)(2,1)S(1)}, bf16[2,512,256]{2,1,0:T(8,128)(2,1)}, u32[]{:S(2)}, u32[]{:S(2)}) collective-permute-start(bf16[2,512,256]{2,1,0:T(8,128)(2,1)S(1)} %collective-permute-done.8.pair_in), channel_id=1, source_target_pairs={{0,16},{16,0},{32,48},{48,32},{64,80},{80,64},{96,112},{112,96},{1... | collective-permute-start | bytes 1572872 | tf_op jit(solution)/shard_map/ppermute | solution.py:388
  71.3 3.4 %order.1.green = bf16[2,512,1024]{2,1,0:T(8,128)(2,1)S(1)} custom-call(s32[2]{0:T(128)S(1)} %pad_add_fusion.place, bf16[2,512,256]{2,1,0:T(8,128)(2,1)} %own_in.1, bf16[2,512,256]{2,1,0:T(8,128)(2,1)} %copy-done.5, bf16[2,512,256]{2,1,0:T(8,128)(2,1)} %copy-done.6, bf16[2,512,256]{2,1,0:T(8,128)(2,1)} %collective-permute-done.10.diag_in), custom_call_target="tpu_custom_call" | custom-call | flops 1000000000 | bytes 4000000 | tf_op jit(solution)/shard_map/order/pallas_call | solution.py:397
  74.8 9.2 %all-to-all-done.records = bf16[8,64,512]{2,1,0:T(8,128)(2,1)S(1)} async-done(((bf16[8,64,512]{2,1,0:T(8,128)(2,1)}), bf16[8,64,512]{2,1,0:T(8,128)(2,1)S(1)}, u32[]{:S(2)}, u32[]{:S(2)}) %all-to-all-start) | async-done | bytes 524320 | tf_op jit(solution)/shard_map/all_to_all | solution.py:51
  83.9 1.8 %columns.1 = f32[16,128,128]{2,1,0:T(8,128)S(1)} custom-call(s32[2]{0:T(128)S(1)} %copy-done.3, bf16[8,64,512]{2,1,0:T(8,128)(2,1)S(1)} %all-to-all-done.records, bf16[2,512,1024]{2,1,0:T(8,128)(2,1)S(1)} %order.1.green), custom_call_target="tpu_custom_call" | custom-call | flops 1000000000 | bytes 4000000 | tf_op jit(solution)/shard_map/columns/pallas_call | solution.py:234
  85.7 14.9 %all_to_all.20 = f32[4,512,128]{2,1,0:T(8,128)S(1)} all-to-all(f32[4,512,128]{2,1,0:T(8,128)S(1)} %bitcast.21), channel_id=1, replica_groups=mesh['shot'=32,'tx'=4,'ty'=4] {'tx'}, dimensions={0} | all-to-all | bytes 2097152 | tf_op jit(solution)/shard_map/all_to_all | solution.py:429
  100.7 13.8 %all_to_all.21 = f32[8,64,128]{2,1,0:T(8,128)S(1)} all-to-all(f32[8,64,128]{2,1,0:T(8,128)S(1)} %bitcast.26), channel_id=1, replica_groups={{0,1,2,3,256,257,258,259},{16,17,18,19,272,273,274,275},{32,33,34,35,28..., dimensions={0} | all-to-all | bytes 524288 | tf_op jit(solution)/shard_map/all_to_all | solution.py:432
  114.5 15.3 %all_to_all.22.em = f32[4,2,16,128]{3,2,1,0:T(8,128)S(1)} all-to-all(f32[4,2,16,128]{3,2,1,0:T(8,128)S(1)} %bitcast.28), channel_id=1, replica_groups={{0,64,128,192},{16,80,144,208},{32,96,160,224},{48,112,176,240},{256,32..., dimensions={0} | all-to-all | bytes 131072 | tf_op jit(solution)/shard_map/all_to_all | solution.py:437
  129.8 3.5 %inject.1 = (f32[4,16,16,128]{3,2,1,0:T(8,128)}, f32[32,1,512]{2,1,0:T(1,128)}) custom-call(f32[4,2,16,128]{3,2,1,0:T(8,128)S(1)} %all_to_all.22.em, s32[8,512]{1,0:T(8,128)S(1)} %bitcast.23, f32[8,512]{1,0:T(8,128)S(1)} %bitcast.24, f32[4,16,16,128]{3,2,1,0:T(8,128)S(1)} %get-tuple-element.23.field), custom_call_target="tpu_custom_call" | custom-call | flops 4000000000 | bytes 4000000 | tf_op jit(solution)/shard_map/inject/pallas_call | solution.py:285
  (35 shorter events, 6.2 us)
Async XLA Ops:
  2.3 16.9 %collective-permute-start.2 = (f32[9,16,8,128]{3,2,1,0:T(8,128)S(1)}, f32[9,16,8,128]{3,2,1,0:T(8,128)S(1)}, u32[]{:S(2)}, u32[]{:S(2)}) collective-permute-start(f32[9,16,8,128]{3,2,1,0:T(8,128)S(1)} %get-tuple-element.17), channel_id=1, source_target_pairs={{0,1},{1,2},{2,3},{4,5},{5,6},{6,7},{8,9},{9,10},{10,11},{12,13},{... | collective-permute-start | bytes 1769480 | tf_op jit(solution)/shard_map/ppermute | solution.py:342
  6.7 16.3 %collective-permute-start = (f32[9,8,16,128]{3,2,1,0:T(8,128)S(1)}, f32[9,8,16,128]{3,2,1,0:T(8,128)S(1)}, u32[]{:S(2)}, u32[]{:S(2)}) collective-permute-start(f32[9,8,16,128]{3,2,1,0:T(8,128)S(1)} %get-tuple-element.15), channel_id=1, source_target_pairs={{0,4},{4,8},{8,12},{1,5},{5,9},{9,13},{2,6},{6,10},{10,14},{3,7},{... | collective-permute-start | bytes 1769480 | tf_op jit(solution)/shard_map/ppermute | solution.py:341
  10.1 16.4 %collective-permute-start.1 = (f32[9,8,16,128]{3,2,1,0:T(8,128)S(1)}, f32[9,8,16,128]{3,2,1,0:T(8,128)S(1)}, u32[]{:S(2)}, u32[]{:S(2)}) collective-permute-start(f32[9,8,16,128]{3,2,1,0:T(8,128)S(1)} %get-tuple-element.16), channel_id=1, source_target_pairs={{4,0},{8,4},{12,8},{5,1},{9,5},{13,9},{6,2},{10,6},{14,10},{7,3},{... | collective-permute-start | bytes 1769480 | tf_op jit(solution)/shard_map/ppermute | solution.py:343
  11.4 19.4 %collective-permute-start.3 = (f32[9,16,8,128]{3,2,1,0:T(8,128)S(1)}, f32[9,16,8,128]{3,2,1,0:T(8,128)S(1)}, u32[]{:S(2)}, u32[]{:S(2)}) collective-permute-start(f32[9,16,8,128]{3,2,1,0:T(8,128)S(1)} %get-tuple-element.18), channel_id=1, source_target_pairs={{1,0},{2,1},{3,2},{5,4},{6,5},{7,6},{9,8},{10,9},{11,10},{13,12},{... | collective-permute-start | bytes 1769480 | tf_op jit(solution)/shard_map/ppermute | solution.py:344
  12.7 54.6 %collective-permute-start.8 = (bf16[2,512,256]{2,1,0:T(8,128)(2,1)}, bf16[2,512,256]{2,1,0:T(8,128)(2,1)S(1)}, u32[]{:S(2)}, u32[]{:S(2)}) collective-permute-start(bf16[2,512,256]{2,1,0:T(8,128)(2,1)} %own_in.1), channel_id=1, source_target_pairs={{0,32},{16,48},{32,0},{48,16},{64,96},{80,112},{96,64},{112,80},{1... | collective-permute-start | bytes 1572872 | tf_op jit(solution)/shard_map/ppermute | solution.py:388
  16.0 23.8 %copy-start = (bf16[4,8,1,1,512]{4,1,3,2,0:T(8,128)(2,1)S(1)}, bf16[4,8,1,1,512]{4,1,3,2,0:T(8,128)(2,1)}, u32[]{:S(2)}) copy-start(bf16[4,8,1,1,512]{4,1,3,2,0:T(8,128)(2,1)} %param.13) | copy-start | bytes 98308
  19.2 14.6 %collective-permute-start.4 = (f32[9,8,8,128]{3,2,1,0:T(8,128)S(1)}, f32[9,8,8,128]{3,2,1,0:T(8,128)S(1)}, u32[]{:S(2)}, u32[]{:S(2)}) collective-permute-start(f32[9,8,8,128]{3,2,1,0:T(8,128)S(1)} %slice.16), channel_id=1, source_target_pairs={{0,4},{4,8},{8,12},{1,5},{5,9},{9,13},{2,6},{6,10},{10,14},{3,7},{... | collective-permute-start | bytes 884744 | tf_op jit(solution)/shard_map/ppermute | solution.py:345
  23.0 11.7 %collective-permute-start.5 = (f32[9,8,8,128]{3,2,1,0:T(8,128)S(1)}, f32[9,8,8,128]{3,2,1,0:T(8,128)S(1)}, u32[]{:S(2)}, u32[]{:S(2)}) collective-permute-start(f32[9,8,8,128]{3,2,1,0:T(8,128)S(1)} %slice.17), channel_id=1, source_target_pairs={{1,0},{2,1},{3,2},{5,4},{6,5},{7,6},{9,8},{10,9},{11,10},{13,12},{... | collective-permute-start | bytes 884744 | tf_op jit(solution)/shard_map/ppermute | solution.py:348
  26.5 9.1 %collective-permute-start.6 = (f32[9,8,8,128]{3,2,1,0:T(8,128)S(1)}, f32[9,8,8,128]{3,2,1,0:T(8,128)S(1)}, u32[]{:S(2)}, u32[]{:S(2)}) collective-permute-start(f32[9,8,8,128]{3,2,1,0:T(8,128)S(1)} %slice.18), channel_id=1, source_target_pairs={{0,1},{1,2},{2,3},{4,5},{5,6},{6,7},{8,9},{9,10},{10,11},{12,13},{... | collective-permute-start | bytes 884744 | tf_op jit(solution)/shard_map/ppermute | solution.py:346
  30.8 8.9 %collective-permute-start.7 = (f32[9,8,8,128]{3,2,1,0:T(8,128)S(1)}, f32[9,8,8,128]{3,2,1,0:T(8,128)S(1)}, u32[]{:S(2)}, u32[]{:S(2)}) collective-permute-start(f32[9,8,8,128]{3,2,1,0:T(8,128)S(1)} %slice.19), channel_id=1, source_target_pairs={{4,0},{8,4},{12,8},{5,1},{9,5},{13,9},{6,2},{10,6},{14,10},{7,3},{... | collective-permute-start | bytes 884744 | tf_op jit(solution)/shard_map/ppermute | solution.py:347
  39.8 25.6 %copy-start.4 = (bf16[2,512,256]{2,1,0:T(8,128)(2,1)S(1)}, bf16[2,512,256]{2,1,0:T(8,128)(2,1)}, u32[]{:S(2)}) copy-start(bf16[2,512,256]{2,1,0:T(8,128)(2,1)} %own_in.1) | copy-start | bytes 1572868
  52.5 31.5 %copy-start.3 = (s32[2]{0:T(128)S(1)}, s32[2]{0:T(128)}, u32[]{:S(2)}) copy-start(s32[2]{0:T(128)} %delay.1) | copy-start | bytes 28
  52.5 31.5 %all-to-all-start = ((bf16[8,64,512]{2,1,0:T(8,128)(2,1)}), bf16[8,64,512]{2,1,0:T(8,128)(2,1)S(1)}, u32[]{:S(2)}, u32[]{:S(2)}) async-start(bf16[8,64,512]{2,1,0:T(8,128)(2,1)} %get-tuple-element.22), calls=%async_computation | async-start | bytes 1048576 | tf_op jit(solution)/shard_map/all_to_all | solution.py:51
  65.3 4.5 %collective-permute-start.9 = (bf16[2,512,256]{2,1,0:T(8,128)(2,1)S(1)}, bf16[2,512,256]{2,1,0:T(8,128)(2,1)S(1)}, u32[]{:S(2)}, u32[]{:S(2)}) collective-permute-start(bf16[2,512,256]{2,1,0:T(8,128)(2,1)S(1)} %copy-done.4), channel_id=1, source_target_pairs={{0,16},{16,0},{32,48},{48,32},{64,80},{80,64},{96,112},{112,96},{1... | collective-permute-start | bytes 1572872 | tf_op jit(solution)/shard_map/ppermute | solution.py:388
  67.3 2.5 %copy-start.5 = (bf16[2,512,256]{2,1,0:T(8,128)(2,1)}, bf16[2,512,256]{2,1,0:T(8,128)(2,1)S(1)}, u32[]{:S(2)}) copy-start(bf16[2,512,256]{2,1,0:T(8,128)(2,1)S(1)} %collective-permute-done.8.pair_in) | copy-start | bytes 1572868
  67.3 4.1 %collective-permute-start.10 = (bf16[2,512,256]{2,1,0:T(8,128)(2,1)S(1)}, bf16[2,512,256]{2,1,0:T(8,128)(2,1)}, u32[]{:S(2)}, u32[]{:S(2)}) collective-permute-start(bf16[2,512,256]{2,1,0:T(8,128)(2,1)S(1)} %collective-permute-done.8.pair_in), channel_id=1, source_target_pairs={{0,16},{16,0},{32,48},{48,32},{64,80},{80,64},{96,112},{112,96},{1... | collective-permute-start | bytes 1572872 | tf_op jit(solution)/shard_map/ppermute | solution.py:388
  69.8 0.8 copy-start.6
  85.7 44.1 %copy-start.1 = (s32[1,1,8,512]{3,2,1,0:T(8,128)S(1)}, s32[1,1,8,512]{3,2,1,0:T(8,128)}, u32[]{:S(2)}) copy-start(s32[1,1,8,512]{3,2,1,0:T(8,128)} %param.16) | copy-start | bytes 49156
  85.7 44.1 %copy-start.2 = (f32[1,1,8,512]{3,2,1,0:T(8,128)S(1)}, f32[1,1,8,512]{3,2,1,0:T(8,128)}, u32[]{:S(2)}) copy-start(f32[1,1,8,512]{3,2,1,0:T(8,128)} %param.17) | copy-start | bytes 49156

commit v6 on v5

--- a/solution.py
+++ b/solution.py
@@ -225,15 +225,15 @@
     for m in range(width // 128):
         a = parts[0][:, m * 128 : (m + 1) * 128]
         b = parts[1][:, m * 128 : (m + 1) * 128]
-        out[2 * m] = jnp.where(lane < 64, a, pltpu.roll(b, 64, 1))
-        out[2 * m + 1] = jnp.where(lane < 64, pltpu.roll(a, 64, 1), b)
+        out[2 * m] = jnp.where(lane < 64, a, pltpu.roll(b, 64, 1)).astype(BF16)
+        out[2 * m + 1] = jnp.where(lane < 64, pltpu.roll(a, 64, 1), b).astype(BF16)
 
 
 def columns(delay, records, green):
     vmem = pl.BlockSpec(memory_space=pltpu.VMEM)
     return pl.pallas_call(
         columns_kernel,
-        out_shape=jax.ShapeDtypeStruct((16, 128, 128), F32),
+        out_shape=jax.ShapeDtypeStruct((16, 128, 128), BF16),
         in_specs=[pl.BlockSpec(memory_space=pltpu.SMEM), vmem, vmem],
         out_specs=vmem,
         compiler_params=pltpu.CompilerParams(vmem_limit_bytes=12 << 20),
@@ -302,20 +302,22 @@
     )(em, cells, weights, field)
 
 
-def pack_kernel(now, prev, speed, xtail, ytail, xhead, yhead, sems):
+def pack_kernel(now, prev, speed, xtail, ytail, xhead, yhead, field, sems):
     shots = now.shape[0]
-    whole, head, tail = slice(None), slice(0, BAND), slice(TILE - BAND, TILE)
-    copies = []
-    for out, xs, ys in (
-        (ytail, whole, tail), (xtail, tail, whole), (xhead, head, whole), (yhead, whole, head),
-    ):
-        for src, dst in (
-            (now.at[:, xs, ys], out.at[pl.ds(0, shots)]),
-            (prev.at[:, xs, ys], out.at[pl.ds(shots, shots)]),
-            (speed.at[xs, ys], out.at[2 * shots]),
-        ):
-            copies.append(pltpu.make_async_copy(src, dst, sems.at[len(copies)]))
-    run(copies)
+    copies = [
+        pltpu.make_async_copy(now, field.at[pl.ds(0, shots)], sems.at[0]),
+        pltpu.make_async_copy(prev, field.at[pl.ds(shots, shots)], sems.at[1]),
+        pltpu.make_async_copy(speed, field.at[2 * shots], sems.at[2]),
+    ]
+    for copy in copies:
+        copy.start()
+    for copy in copies:
+        copy.wait()
+    head, tail = slice(0, BAND), slice(TILE - BAND, TILE)
+    xtail[...] = field[:, tail]
+    ytail[...] = field[:, :, tail]
+    xhead[...] = field[:, head]
+    yhead[...] = field[:, :, head]
 
 
 def packed(now, prev, speed):
@@ -328,7 +330,10 @@
         out_shape=(across, along, across, along),
         in_specs=[pl.BlockSpec(memory_space=pltpu.HBM)] * 3,
         out_specs=(vmem,) * 4,
-        scratch_shapes=[pltpu.SemaphoreType.DMA((12,))],
+        scratch_shapes=[
+            pltpu.VMEM((fields, TILE, TILE, DEPTH), F32),
+            pltpu.SemaphoreType.DMA((3,)),
+        ],
         compiler_params=pltpu.CompilerParams(vmem_limit_bytes=8 << 20),
         cost_estimate=pl.CostEstimate(flops=0, bytes_accessed=4_000_000, transcendentals=0),
         name="pack",
@@ -427,7 +432,7 @@
     records = row_exchange(records)
     partial = columns(lag_delay, records, wide_green)
     partial = lax.all_to_all(partial.reshape(4, 512, 128), "tx", 0, 0, tiled=True)
-    partial = jnp.sum(partial, axis=0).reshape(4, 2, 64, 128)
+    partial = jnp.sum(partial.astype(F32), axis=0).reshape(4, 2, 64, 128)
     partial = jnp.swapaxes(partial, 0, 1).reshape(8, 64, 128)
     partial = lax.all_to_all(
         partial, ("shot", "ty"), 0, 0, tiled=True, axis_index_groups=RING_GROUPS

time: 134 us -> 128 us (0.955)
  blocking collectives: 43.9 us -> 38.3 us
    all_to_all x1, blocking collectives: 14.9 us -> 12 us  [block(): lax.all_to_all(partial.reshape(4, 512, 128), 'tx', 0, 0, tiled=True)]
    all_to_all x1, blocking collectives: 15.3 us -> 12.5 us  [block(): lax.all_to_all(summed, 'shot', 0, 0, tiled=True, axis_index_groups=COLUMN...]
  transfers between devices with their start and end apart: 12 -> 12, of which waited for: 8 -> 8; matrix products, arithmetic and copies ran while one was open for 1% -> 1% of each run, Pallas kernels for 13% -> 14%
where the time goes in v6:
time: 128 us; the launch traced here: 127 us
  starting transfers between devices  40.4 us (32%)
  blocking collectives  38.3 us (30%)
  Pallas kernels  24.2 us (19%)
  waiting for transfers between devices  21.6 us (17%)
    all_to_all x1, blocking collectives, block(): lax.all_to_all(partial, ('shot', 'ty'), 0, 0, tiled=True, axis_index_grou...  13.8 us
    all_to_all x1, starting transfers between devices, row_exchange(): lax.all_to_all(x, 'shot', split_axis=0, concat_axis=0, tiled=True, axis_i...  12.9 us
    pallas_call x1, Pallas kernels, stencil(): pl.pallas_call(stencil_kernel, out_shape=(jax.ShapeDtypeStruct((8, shots...  12.7 us
    all_to_all x1, blocking collectives, block(): lax.all_to_all(summed, 'shot', 0, 0, tiled=True, axis_index_groups=COLUMN...  12.5 us
    all_to_all x1, blocking collectives, block(): lax.all_to_all(partial.reshape(4, 512, 128), 'tx', 0, 0, tiled=True)  12 us
    all_to_all x1, waiting for transfers between devices, row_exchange(): lax.all_to_all(x, 'shot', split_axis=0, concat_axis=0, tiled=True, axis_i...  9.21 us
    ppermute x3, starting transfers between devices, moved(): return lax.ppermute(block, 'shot', pairs)  6.94 us
    ppermute x1, starting transfers between devices, halo_blocks(): ym = lax.ppermute(ytail, 'ty', UP)  4.31 us
  transfers between devices with their start and end apart: 12, of which 8 were waited for; matrix products, arithmetic and copies ran while one was open for 1% of the time, Pallas kernels for 14%

profile of v6, /device:TPU:8, one launch (start us, length us, event | category | flops | bytes accessed | tf_op | source)
XLA Modules:
  0.0 127.4 jit_solution(821264100212064977)
XLA Ops:
  0.6 1.4 %pack.1 = (f32[9,8,16,128]{3,2,1,0:T(8,128)S(1)}, f32[9,16,8,128]{3,2,1,0:T(8,128)S(1)}, f32[9,8,16,128]{3,2,1,0:T(8,128)S(1)}, f32[9,16,8,128]{3,2,1,0:T(8,128)S(1)}) custom-call(f32[4,16,16,128]{3,2,1,0:T(8,128)} %now.3, f32[4,16,16,128]{3,2,1,0:T(8,128)} %prev.3, f32[16,16,128]{2,1,0:T(8,128)} %speed.3), custom_call_target="tpu_custom_call" | custom-call | bytes 4000000 | tf_op jit(solution)/shard_map/pack/pallas_call | solution.py:328
  2.0 4.3 %collective-permute-start.2 = (f32[9,16,8,128]{3,2,1,0:T(8,128)S(1)}, f32[9,16,8,128]{3,2,1,0:T(8,128)S(1)}, u32[]{:S(2)}, u32[]{:S(2)}) collective-permute-start(f32[9,16,8,128]{3,2,1,0:T(8,128)S(1)} %get-tuple-element.17), channel_id=1, source_target_pairs={{0,1},{1,2},{2,3},{4,5},{5,6},{6,7},{8,9},{9,10},{10,11},{12,13},{... | collective-permute-start | bytes 1769480 | tf_op jit(solution)/shard_map/ppermute | solution.py:347
  6.4 3.4 %collective-permute-start = (f32[9,8,16,128]{3,2,1,0:T(8,128)S(1)}, f32[9,8,16,128]{3,2,1,0:T(8,128)S(1)}, u32[]{:S(2)}, u32[]{:S(2)}) collective-permute-start(f32[9,8,16,128]{3,2,1,0:T(8,128)S(1)} %get-tuple-element.15), channel_id=1, source_target_pairs={{0,4},{4,8},{8,12},{1,5},{5,9},{9,13},{2,6},{6,10},{10,14},{3,7},{... | collective-permute-start | bytes 1769480 | tf_op jit(solution)/shard_map/ppermute | solution.py:346
  9.8 1.3 %collective-permute-start.1 = (f32[9,8,16,128]{3,2,1,0:T(8,128)S(1)}, f32[9,8,16,128]{3,2,1,0:T(8,128)S(1)}, u32[]{:S(2)}, u32[]{:S(2)}) collective-permute-start(f32[9,8,16,128]{3,2,1,0:T(8,128)S(1)} %get-tuple-element.16), channel_id=1, source_target_pairs={{4,0},{8,4},{12,8},{5,1},{9,5},{13,9},{6,2},{10,6},{14,10},{7,3},{... | collective-permute-start | bytes 1769480 | tf_op jit(solution)/shard_map/ppermute | solution.py:348
  11.1 1.3 %collective-permute-start.3 = (f32[9,16,8,128]{3,2,1,0:T(8,128)S(1)}, f32[9,16,8,128]{3,2,1,0:T(8,128)S(1)}, u32[]{:S(2)}, u32[]{:S(2)}) collective-permute-start(f32[9,16,8,128]{3,2,1,0:T(8,128)S(1)} %get-tuple-element.18), channel_id=1, source_target_pairs={{1,0},{2,1},{3,2},{5,4},{6,5},{7,6},{9,8},{10,9},{11,10},{13,12},{... | collective-permute-start | bytes 1769480 | tf_op jit(solution)/shard_map/ppermute | solution.py:349
  12.4 2.6 %collective-permute-start.8 = (bf16[2,512,256]{2,1,0:T(8,128)(2,1)}, bf16[2,512,256]{2,1,0:T(8,128)(2,1)S(1)}, u32[]{:S(2)}, u32[]{:S(2)}) collective-permute-start(bf16[2,512,256]{2,1,0:T(8,128)(2,1)} %own_in.1), channel_id=1, source_target_pairs={{0,32},{16,48},{32,0},{48,16},{64,96},{80,112},{96,64},{112,80},{1... | collective-permute-start | bytes 1572872 | tf_op jit(solution)/shard_map/ppermute | solution.py:393
  15.7 3.2 %collective-permute-done.2.ym = f32[9,16,8,128]{3,2,1,0:T(8,128)S(1)} collective-permute-done((f32[9,16,8,128]{3,2,1,0:T(8,128)S(1)}, f32[9,16,8,128]{3,2,1,0:T(8,128)S(1)}, u32[]{:S(2)}, u32[]{:S(2)}) %collective-permute-start.2) | collective-permute-done | bytes 589856 | tf_op jit(solution)/shard_map/ppermute | solution.py:347
  18.9 3.4 %collective-permute-start.4 = (f32[9,8,8,128]{3,2,1,0:T(8,128)S(1)}, f32[9,8,8,128]{3,2,1,0:T(8,128)S(1)}, u32[]{:S(2)}, u32[]{:S(2)}) collective-permute-start(f32[9,8,8,128]{3,2,1,0:T(8,128)S(1)} %slice.16), channel_id=1, source_target_pairs={{0,4},{4,8},{8,12},{1,5},{5,9},{9,13},{2,6},{6,10},{10,14},{3,7},{... | collective-permute-start | bytes 884744 | tf_op jit(solution)/shard_map/ppermute | solution.py:350
  22.7 1.3 %collective-permute-start.5 = (f32[9,8,8,128]{3,2,1,0:T(8,128)S(1)}, f32[9,8,8,128]{3,2,1,0:T(8,128)S(1)}, u32[]{:S(2)}, u32[]{:S(2)}) collective-permute-start(f32[9,8,8,128]{3,2,1,0:T(8,128)S(1)} %slice.17), channel_id=1, source_target_pairs={{1,0},{2,1},{3,2},{5,4},{6,5},{7,6},{9,8},{10,9},{11,10},{13,12},{... | collective-permute-start | bytes 884744 | tf_op jit(solution)/shard_map/ppermute | solution.py:353
  24.0 2.2 %collective-permute-done.1.xp = f32[9,8,16,128]{3,2,1,0:T(8,128)S(1)} collective-permute-done((f32[9,8,16,128]{3,2,1,0:T(8,128)S(1)}, f32[9,8,16,128]{3,2,1,0:T(8,128)S(1)}, u32[]{:S(2)}, u32[]{:S(2)}) %collective-permute-start.1) | collective-permute-done | bytes 589856 | tf_op jit(solution)/shard_map/ppermute | solution.py:348
  26.2 4.3 %collective-permute-start.6 = (f32[9,8,8,128]{3,2,1,0:T(8,128)S(1)}, f32[9,8,8,128]{3,2,1,0:T(8,128)S(1)}, u32[]{:S(2)}, u32[]{:S(2)}) collective-permute-start(f32[9,8,8,128]{3,2,1,0:T(8,128)S(1)} %slice.18), channel_id=1, source_target_pairs={{0,1},{1,2},{2,3},{4,5},{5,6},{6,7},{8,9},{9,10},{10,11},{12,13},{... | collective-permute-start | bytes 884744 | tf_op jit(solution)/shard_map/ppermute | solution.py:351
  32.1 1.4 %assemble.1 = (f32[4,32,48,128]{3,2,1,0:T(8,128)S(1)}, f32[4,32,48,128]{3,2,1,0:T(8,128)S(1)}, f32[32,48,128]{2,1,0:T(8,128)S(1)}) custom-call(f32[4,16,16,128]{3,2,1,0:T(8,128)} %now.3, f32[4,16,16,128]{3,2,1,0:T(8,128)} %prev.3, f32[16,16,128]{2,1,0:T(8,128)} %speed.3, f32[9,8,16,128]{3,2,1,0:T(8,128)S(1)} %collective-permute-done.xm, ...), custom_call_target="tpu_custom_call" | custom-call | bytes 8000000 | tf_op jit(solution)/shard_map/assemble/pallas_call | solution.py:100
  35.3 4.2 %collective-permute-done.7.cpp = f32[9,8,8,128]{3,2,1,0:T(8,128)S(1)} collective-permute-done((f32[9,8,8,128]{3,2,1,0:T(8,128)S(1)}, f32[9,8,8,128]{3,2,1,0:T(8,128)S(1)}, u32[]{:S(2)}, u32[]{:S(2)}) %collective-permute-start.7) | collective-permute-done | bytes 294944 | tf_op jit(solution)/shard_map/ppermute | solution.py:352
  39.5 12.7 %stencil.1 = (bf16[8,64,512]{2,1,0:T(8,128)(2,1)}, f32[4,16,16,128]{3,2,1,0:T(8,128)S(1)}, f32[4,16,16,128]{3,2,1,0:T(8,128)}, f32[4,32,48,128]{3,2,1,0:T(8,128)...) custom-call(f32[4,32,48,128]{3,2,1,0:T(8,128)S(1)} %get-tuple-elemen, ...), custom_call_target="tpu_custom_call", output_to_operand_aliasing={{3}: (0, {}), {4}: (1, {}), {5}: (2, {})} | custom-call | flops 2000000000 | bytes 12000000 | tf_op jit(solution)/shard_map/stencil/pallas_call | solution.py:175
  52.2 12.9 %all-to-all-start = ((bf16[8,64,512]{2,1,0:T(8,128)(2,1)}), bf16[8,64,512]{2,1,0:T(8,128)(2,1)S(1)}, u32[]{:S(2)}, u32[]{:S(2)}) async-start(bf16[8,64,512]{2,1,0:T(8,128)(2,1)} %get-tuple-element.22), calls=%async_computation | async-start | bytes 1048576 | tf_op jit(solution)/shard_map/all_to_all | solution.py:51
  65.0 1.9 %collective-permute-start.9 = (bf16[2,512,256]{2,1,0:T(8,128)(2,1)S(1)}, bf16[2,512,256]{2,1,0:T(8,128)(2,1)S(1)}, u32[]{:S(2)}, u32[]{:S(2)}) collective-permute-start(bf16[2,512,256]{2,1,0:T(8,128)(2,1)S(1)} %copy-done.4), channel_id=1, source_target_pairs={{0,16},{16,0},{32,48},{48,32},{64,80},{80,64},{96,112},{112,96},{1... | collective-permute-start | bytes 1572872 | tf_op jit(solution)/shard_map/ppermute | solution.py:393
  67.0 2.4 %collective-permute-start.10 = (bf16[2,512,256]{2,1,0:T(8,128)(2,1)S(1)}, bf16[2,512,256]{2,1,0:T(8,128)(2,1)}, u32[]{:S(2)}, u32[]{:S(2)}) collective-permute-start(bf16[2,512,256]{2,1,0:T(8,128)(2,1)S(1)} %collective-permute-done.8.pair_in), channel_id=1, source_target_pairs={{0,16},{16,0},{32,48},{48,32},{64,80},{80,64},{96,112},{112,96},{1... | collective-permute-start | bytes 1572872 | tf_op jit(solution)/shard_map/ppermute | solution.py:393
  71.0 3.4 %order.1.green = bf16[2,512,1024]{2,1,0:T(8,128)(2,1)S(1)} custom-call(s32[2]{0:T(128)S(1)} %pad_add_fusion.place, bf16[2,512,256]{2,1,0:T(8,128)(2,1)} %own_in.1, bf16[2,512,256]{2,1,0:T(8,128)(2,1)} %copy-done.5, bf16[2,512,256]{2,1,0:T(8,128)(2,1)} %copy-done.6, bf16[2,512,256]{2,1,0:T(8,128)(2,1)} %collective-permute-done.10.diag_in), custom_call_target="tpu_custom_call" | custom-call | flops 1000000000 | bytes 4000000 | tf_op jit(solution)/shard_map/order/pallas_call | solution.py:402
  74.5 9.2 %all-to-all-done.records = bf16[8,64,512]{2,1,0:T(8,128)(2,1)S(1)} async-done(((bf16[8,64,512]{2,1,0:T(8,128)(2,1)}), bf16[8,64,512]{2,1,0:T(8,128)(2,1)S(1)}, u32[]{:S(2)}, u32[]{:S(2)}) %all-to-all-start) | async-done | bytes 524320 | tf_op jit(solution)/shard_map/all_to_all | solution.py:51
  83.7 1.8 %columns.1 = bf16[16,128,128]{2,1,0:T(8,128)(2,1)S(1)} custom-call(s32[2]{0:T(128)S(1)} %copy-done.3, bf16[8,64,512]{2,1,0:T(8,128)(2,1)S(1)} %all-to-all-done.records, bf16[2,512,1024]{2,1,0:T(8,128)(2,1)S(1)} %order.1.green), custom_call_target="tpu_custom_call" | custom-call | flops 1000000000 | bytes 4000000 | tf_op jit(solution)/shard_map/columns/pallas_call | solution.py:234
  85.5 12.0 %all_to_all.20 = bf16[4,512,128]{2,1,0:T(8,128)(2,1)S(1)} all-to-all(bf16[4,512,128]{2,1,0:T(8,128)(2,1)S(1)} %bitcast.21), channel_id=1, replica_groups=mesh['shot'=32,'tx'=4,'ty'=4] {'tx'}, dimensions={0} | all-to-all | bytes 1048576 | tf_op jit(solution)/shard_map/all_to_all | solution.py:434
  97.5 13.8 %all_to_all.21 = f32[8,64,128]{2,1,0:T(8,128)S(1)} all-to-all(f32[8,64,128]{2,1,0:T(8,128)S(1)} %bitcast.26), channel_id=1, replica_groups={{0,1,2,3,256,257,258,259},{16,17,18,19,272,273,274,275},{32,33,34,35,28..., dimensions={0} | all-to-all | bytes 524288 | tf_op jit(solution)/shard_map/all_to_all | solution.py:437
  111.4 12.5 %all_to_all.22.em = f32[4,2,16,128]{3,2,1,0:T(8,128)S(1)} all-to-all(f32[4,2,16,128]{3,2,1,0:T(8,128)S(1)} %bitcast.28), channel_id=1, replica_groups={{0,64,128,192},{16,80,144,208},{32,96,160,224},{48,112,176,240},{256,32..., dimensions={0} | all-to-all | bytes 131072 | tf_op jit(solution)/shard_map/all_to_all | solution.py:442
  123.9 3.5 %inject.1 = (f32[4,16,16,128]{3,2,1,0:T(8,128)}, f32[32,1,512]{2,1,0:T(1,128)}) custom-call(f32[4,2,16,128]{3,2,1,0:T(8,128)S(1)} %all_to_all.22.em, s32[8,512]{1,0:T(8,128)S(1)} %bitcast.23, f32[8,512]{1,0:T(8,128)S(1)} %bitcast.24, f32[4,16,16,128]{3,2,1,0:T(8,128)S(1)} %get-tuple-element.23.field), custom_call_target="tpu_custom_call" | custom-call | flops 4000000000 | bytes 4000000 | tf_op jit(solution)/shard_map/inject/pallas_call | solution.py:285
  (35 shorter events, 6.2 us)
Async XLA Ops:
  2.0 16.9 %collective-permute-start.2 = (f32[9,16,8,128]{3,2,1,0:T(8,128)S(1)}, f32[9,16,8,128]{3,2,1,0:T(8,128)S(1)}, u32[]{:S(2)}, u32[]{:S(2)}) collective-permute-start(f32[9,16,8,128]{3,2,1,0:T(8,128)S(1)} %get-tuple-element.17), channel_id=1, source_target_pairs={{0,1},{1,2},{2,3},{4,5},{5,6},{6,7},{8,9},{9,10},{10,11},{12,13},{... | collective-permute-start | bytes 1769480 | tf_op jit(solution)/shard_map/ppermute | solution.py:347
  6.4 16.3 %collective-permute-start = (f32[9,8,16,128]{3,2,1,0:T(8,128)S(1)}, f32[9,8,16,128]{3,2,1,0:T(8,128)S(1)}, u32[]{:S(2)}, u32[]{:S(2)}) collective-permute-start(f32[9,8,16,128]{3,2,1,0:T(8,128)S(1)} %get-tuple-element.15), channel_id=1, source_target_pairs={{0,4},{4,8},{8,12},{1,5},{5,9},{9,13},{2,6},{6,10},{10,14},{3,7},{... | collective-permute-start | bytes 1769480 | tf_op jit(solution)/shard_map/ppermute | solution.py:346
  9.8 16.4 %collective-permute-start.1 = (f32[9,8,16,128]{3,2,1,0:T(8,128)S(1)}, f32[9,8,16,128]{3,2,1,0:T(8,128)S(1)}, u32[]{:S(2)}, u32[]{:S(2)}) collective-permute-start(f32[9,8,16,128]{3,2,1,0:T(8,128)S(1)} %get-tuple-element.16), channel_id=1, source_target_pairs={{4,0},{8,4},{12,8},{5,1},{9,5},{13,9},{6,2},{10,6},{14,10},{7,3},{... | collective-permute-start | bytes 1769480 | tf_op jit(solution)/shard_map/ppermute | solution.py:348
  11.1 19.4 %collective-permute-start.3 = (f32[9,16,8,128]{3,2,1,0:T(8,128)S(1)}, f32[9,16,8,128]{3,2,1,0:T(8,128)S(1)}, u32[]{:S(2)}, u32[]{:S(2)}) collective-permute-start(f32[9,16,8,128]{3,2,1,0:T(8,128)S(1)} %get-tuple-element.18), channel_id=1, source_target_pairs={{1,0},{2,1},{3,2},{5,4},{6,5},{7,6},{9,8},{10,9},{11,10},{13,12},{... | collective-permute-start | bytes 1769480 | tf_op jit(solution)/shard_map/ppermute | solution.py:349
  12.4 54.6 %collective-permute-start.8 = (bf16[2,512,256]{2,1,0:T(8,128)(2,1)}, bf16[2,512,256]{2,1,0:T(8,128)(2,1)S(1)}, u32[]{:S(2)}, u32[]{:S(2)}) collective-permute-start(bf16[2,512,256]{2,1,0:T(8,128)(2,1)} %own_in.1), channel_id=1, source_target_pairs={{0,32},{16,48},{32,0},{48,16},{64,96},{80,112},{96,64},{112,80},{1... | collective-permute-start | bytes 1572872 | tf_op jit(solution)/shard_map/ppermute | solution.py:393
  15.7 23.8 %copy-start = (bf16[4,8,1,1,512]{4,1,3,2,0:T(8,128)(2,1)S(1)}, bf16[4,8,1,1,512]{4,1,3,2,0:T(8,128)(2,1)}, u32[]{:S(2)}) copy-start(bf16[4,8,1,1,512]{4,1,3,2,0:T(8,128)(2,1)} %param.13) | copy-start | bytes 98308
  18.9 14.6 %collective-permute-start.4 = (f32[9,8,8,128]{3,2,1,0:T(8,128)S(1)}, f32[9,8,8,128]{3,2,1,0:T(8,128)S(1)}, u32[]{:S(2)}, u32[]{:S(2)}) collective-permute-start(f32[9,8,8,128]{3,2,1,0:T(8,128)S(1)} %slice.16), channel_id=1, source_target_pairs={{0,4},{4,8},{8,12},{1,5},{5,9},{9,13},{2,6},{6,10},{10,14},{3,7},{... | collective-permute-start | bytes 884744 | tf_op jit(solution)/shard_map/ppermute | solution.py:350
  22.7 11.7 %collective-permute-start.5 = (f32[9,8,8,128]{3,2,1,0:T(8,128)S(1)}, f32[9,8,8,128]{3,2,1,0:T(8,128)S(1)}, u32[]{:S(2)}, u32[]{:S(2)}) collective-permute-start(f32[9,8,8,128]{3,2,1,0:T(8,128)S(1)} %slice.17), channel_id=1, source_target_pairs={{1,0},{2,1},{3,2},{5,4},{6,5},{7,6},{9,8},{10,9},{11,10},{13,12},{... | collective-permute-start | bytes 884744 | tf_op jit(solution)/shard_map/ppermute | solution.py:353
  26.2 9.1 %collective-permute-start.6 = (f32[9,8,8,128]{3,2,1,0:T(8,128)S(1)}, f32[9,8,8,128]{3,2,1,0:T(8,128)S(1)}, u32[]{:S(2)}, u32[]{:S(2)}) collective-permute-start(f32[9,8,8,128]{3,2,1,0:T(8,128)S(1)} %slice.18), channel_id=1, source_target_pairs={{0,1},{1,2},{2,3},{4,5},{5,6},{6,7},{8,9},{9,10},{10,11},{12,13},{... | collective-permute-start | bytes 884744 | tf_op jit(solution)/shard_map/ppermute | solution.py:351
  30.5 8.9 %collective-permute-start.7 = (f32[9,8,8,128]{3,2,1,0:T(8,128)S(1)}, f32[9,8,8,128]{3,2,1,0:T(8,128)S(1)}, u32[]{:S(2)}, u32[]{:S(2)}) collective-permute-start(f32[9,8,8,128]{3,2,1,0:T(8,128)S(1)} %slice.19), channel_id=1, source_target_pairs={{4,0},{8,4},{12,8},{5,1},{9,5},{13,9},{6,2},{10,6},{14,10},{7,3},{... | collective-permute-start | bytes 884744 | tf_op jit(solution)/shard_map/ppermute | solution.py:352
  39.5 25.6 %copy-start.4 = (bf16[2,512,256]{2,1,0:T(8,128)(2,1)S(1)}, bf16[2,512,256]{2,1,0:T(8,128)(2,1)}, u32[]{:S(2)}) copy-start(bf16[2,512,256]{2,1,0:T(8,128)(2,1)} %own_in.1) | copy-start | bytes 1572868
  52.2 31.6 %copy-start.3 = (s32[2]{0:T(128)S(1)}, s32[2]{0:T(128)}, u32[]{:S(2)}) copy-start(s32[2]{0:T(128)} %delay.1) | copy-start | bytes 28
  52.2 31.5 %all-to-all-start = ((bf16[8,64,512]{2,1,0:T(8,128)(2,1)}), bf16[8,64,512]{2,1,0:T(8,128)(2,1)S(1)}, u32[]{:S(2)}, u32[]{:S(2)}) async-start(bf16[8,64,512]{2,1,0:T(8,128)(2,1)} %get-tuple-element.22), calls=%async_computation | async-start | bytes 1048576 | tf_op jit(solution)/shard_map/all_to_all | solution.py:51
  65.0 4.5 %collective-permute-start.9 = (bf16[2,512,256]{2,1,0:T(8,128)(2,1)S(1)}, bf16[2,512,256]{2,1,0:T(8,128)(2,1)S(1)}, u32[]{:S(2)}, u32[]{:S(2)}) collective-permute-start(bf16[2,512,256]{2,1,0:T(8,128)(2,1)S(1)} %copy-done.4), channel_id=1, source_target_pairs={{0,16},{16,0},{32,48},{48,32},{64,80},{80,64},{96,112},{112,96},{1... | collective-permute-start | bytes 1572872 | tf_op jit(solution)/shard_map/ppermute | solution.py:393
  67.0 2.5 %copy-start.5 = (bf16[2,512,256]{2,1,0:T(8,128)(2,1)}, bf16[2,512,256]{2,1,0:T(8,128)(2,1)S(1)}, u32[]{:S(2)}) copy-start(bf16[2,512,256]{2,1,0:T(8,128)(2,1)S(1)} %collective-permute-done.8.pair_in) | copy-start | bytes 1572868
  67.0 4.1 %collective-permute-start.10 = (bf16[2,512,256]{2,1,0:T(8,128)(2,1)S(1)}, bf16[2,512,256]{2,1,0:T(8,128)(2,1)}, u32[]{:S(2)}, u32[]{:S(2)}) collective-permute-start(bf16[2,512,256]{2,1,0:T(8,128)(2,1)S(1)} %collective-permute-done.8.pair_in), channel_id=1, source_target_pairs={{0,16},{16,0},{32,48},{48,32},{64,80},{80,64},{96,112},{112,96},{1... | collective-permute-start | bytes 1572872 | tf_op jit(solution)/shard_map/ppermute | solution.py:393
  69.5 0.8 copy-start.6
  74.5 49.4 %copy-start.1 = (s32[1,1,8,512]{3,2,1,0:T(8,128)S(1)}, s32[1,1,8,512]{3,2,1,0:T(8,128)}, u32[]{:S(2)}) copy-start(s32[1,1,8,512]{3,2,1,0:T(8,128)} %param.16) | copy-start | bytes 49156
  74.5 49.4 %copy-start.2 = (f32[1,1,8,512]{3,2,1,0:T(8,128)S(1)}, f32[1,1,8,512]{3,2,1,0:T(8,128)}, u32[]{:S(2)}) copy-start(f32[1,1,8,512]{3,2,1,0:T(8,128)} %param.17) | copy-start | bytes 49156

commit v7 on v6

--- a/solution.py
+++ b/solution.py
@@ -29,15 +29,6 @@
     [shot_id(h, 2 * k + odd, c) for h in range(2) for k in range(4)]
     for odd in range(2)
     for c in range(2)
-]
-COLUMN_GROUPS = [
-    [shot_id(h, 2 * k + odd, c) for k in range(4)]
-    for h in range(2)
-    for odd in range(2)
-    for c in range(2)
-]
-RING_GROUPS = [
-    [shot_id(h, r, c) * 4 + b for h in range(2) for b in range(4)] for r in range(8) for c in range(2)
 ]
 UP = [(i, i + 1) for i in range(3)]
 DOWN = [(i + 1, i) for i in range(3)]
@@ -247,7 +238,7 @@
     points = cells.shape[1]
     lane = lax.broadcasted_iota(jnp.int32, (16, 128), 1)
     for tile in range(4):
-        even, odd = em[2 * tile % 4, tile // 2], em[2 * tile % 4 + 1, tile // 2]
+        even, odd = em[2 * tile], em[2 * tile + 1]
         emission[pl.ds(0, 16), pl.ds(tile * 128, 128)] = jnp.where(lane < 64, even, pltpu.roll(odd, 64, 1))
         emission[pl.ds(16, 16), pl.ds(tile * 128, 128)] = jnp.where(lane < 64, pltpu.roll(even, 64, 1), odd)
 
@@ -431,17 +422,9 @@
     )[:3]
     records = row_exchange(records)
     partial = columns(lag_delay, records, wide_green)
-    partial = lax.all_to_all(partial.reshape(4, 512, 128), "tx", 0, 0, tiled=True)
-    partial = jnp.sum(partial.astype(F32), axis=0).reshape(4, 2, 64, 128)
-    partial = jnp.swapaxes(partial, 0, 1).reshape(8, 64, 128)
-    partial = lax.all_to_all(
-        partial, ("shot", "ty"), 0, 0, tiled=True, axis_index_groups=RING_GROUPS
-    )
-    summed = jnp.sum(partial.reshape(2, 4, 64, 128), axis=1)
-    summed = jnp.swapaxes(summed.reshape(2, 4, 16, 128), 0, 1)
-    em = lax.all_to_all(
-        summed, "shot", 0, 0, tiled=True, axis_index_groups=COLUMN_GROUPS
-    )
+    partial = lax.all_to_all(partial, ("tx", "ty"), 0, 0, tiled=True)
+    summed = jnp.sum(partial.astype(F32), axis=0)
+    em = row_exchange(summed.reshape(8, 16, 128))
     wave_out, emission = inject(
         em, emit_cells.reshape(emit_cells.shape[-2:]), emit_weights.reshape(emit_weights.shape[-2:]), field
     )

time: 128 us -> 129 us (level)
    all_to_all x3 -> x2, blocking collectives: 38.3 us -> 39 us  [the longest x1 21 us: row_exchange(): lax.all_to_all(x, 'shot', split_axis=0, concat_axis=0, tiled=True, axis_i...]
where the time goes in v7:
time: 129 us; the launch traced here: 128 us
  starting transfers between devices  40.4 us (31%)
  blocking collectives  39 us (30%)
  Pallas kernels  24.2 us (19%)
  waiting for transfers between devices  21.6 us (17%)
    all_to_all x1, blocking collectives, row_exchange(): lax.all_to_all(x, 'shot', split_axis=0, concat_axis=0, tiled=True, axis_i...  21 us
    all_to_all x1, blocking collectives, block(): partial = lax.all_to_all(partial, ('tx', 'ty'), 0, 0, tiled=True)  18 us
    all_to_all x1, starting transfers between devices, row_exchange(): lax.all_to_all(x, 'shot', split_axis=0, concat_axis=0, tiled=True, axis_i...  12.9 us
    pallas_call x1, Pallas kernels, stencil(): pl.pallas_call(stencil_kernel, out_shape=(jax.ShapeDtypeStruct((8, shots...  12.7 us
    all_to_all x1, waiting for transfers between devices, row_exchange(): lax.all_to_all(x, 'shot', split_axis=0, concat_axis=0, tiled=True, axis_i...  9.21 us
    ppermute x3, starting transfers between devices, moved(): return lax.ppermute(block, 'shot', pairs)  6.94 us
    ppermute x1, starting transfers between devices, halo_blocks(): ym = lax.ppermute(ytail, 'ty', UP)  4.31 us
    ppermute x1, starting transfers between devices, halo_blocks(): cpm = lax.ppermute(xp[:, :, tail], 'ty', UP)  4.26 us
  transfers between devices with their start and end apart: 12, of which 8 were waited for; matrix products, arithmetic and copies ran while one was open for 1% of the time, Pallas kernels for 14%

profile of v7, /device:TPU:8, one launch (start us, length us, event | category | flops | bytes accessed | tf_op | source)
XLA Modules:
  0.0 128.1 jit_solution(6608436538373459015)
XLA Ops:
  0.6 1.4 %pack.1 = (f32[9,8,16,128]{3,2,1,0:T(8,128)S(1)}, f32[9,16,8,128]{3,2,1,0:T(8,128)S(1)}, f32[9,8,16,128]{3,2,1,0:T(8,128)S(1)}, f32[9,16,8,128]{3,2,1,0:T(8,128)S(1)}) custom-call(f32[4,16,16,128]{3,2,1,0:T(8,128)} %now.3, f32[4,16,16,128]{3,2,1,0:T(8,128)} %prev.3, f32[16,16,128]{2,1,0:T(8,128)} %speed.3), custom_call_target="tpu_custom_call" | custom-call | bytes 4000000 | tf_op jit(solution)/shard_map/pack/pallas_call | solution.py:319
  2.0 4.3 %collective-permute-start.2 = (f32[9,16,8,128]{3,2,1,0:T(8,128)S(1)}, f32[9,16,8,128]{3,2,1,0:T(8,128)S(1)}, u32[]{:S(2)}, u32[]{:S(2)}) collective-permute-start(f32[9,16,8,128]{3,2,1,0:T(8,128)S(1)} %get-tuple-element.17), channel_id=1, source_target_pairs={{0,1},{1,2},{2,3},{4,5},{5,6},{6,7},{8,9},{9,10},{10,11},{12,13},{... | collective-permute-start | bytes 1769480 | tf_op jit(solution)/shard_map/ppermute | solution.py:338
  6.4 3.4 %collective-permute-start = (f32[9,8,16,128]{3,2,1,0:T(8,128)S(1)}, f32[9,8,16,128]{3,2,1,0:T(8,128)S(1)}, u32[]{:S(2)}, u32[]{:S(2)}) collective-permute-start(f32[9,8,16,128]{3,2,1,0:T(8,128)S(1)} %get-tuple-element.15), channel_id=1, source_target_pairs={{0,4},{4,8},{8,12},{1,5},{5,9},{9,13},{2,6},{6,10},{10,14},{3,7},{... | collective-permute-start | bytes 1769480 | tf_op jit(solution)/shard_map/ppermute | solution.py:337
  9.8 1.3 %collective-permute-start.1 = (f32[9,8,16,128]{3,2,1,0:T(8,128)S(1)}, f32[9,8,16,128]{3,2,1,0:T(8,128)S(1)}, u32[]{:S(2)}, u32[]{:S(2)}) collective-permute-start(f32[9,8,16,128]{3,2,1,0:T(8,128)S(1)} %get-tuple-element.16), channel_id=1, source_target_pairs={{4,0},{8,4},{12,8},{5,1},{9,5},{13,9},{6,2},{10,6},{14,10},{7,3},{... | collective-permute-start | bytes 1769480 | tf_op jit(solution)/shard_map/ppermute | solution.py:339
  11.1 1.3 %collective-permute-start.3 = (f32[9,16,8,128]{3,2,1,0:T(8,128)S(1)}, f32[9,16,8,128]{3,2,1,0:T(8,128)S(1)}, u32[]{:S(2)}, u32[]{:S(2)}) collective-permute-start(f32[9,16,8,128]{3,2,1,0:T(8,128)S(1)} %get-tuple-element.18), channel_id=1, source_target_pairs={{1,0},{2,1},{3,2},{5,4},{6,5},{7,6},{9,8},{10,9},{11,10},{13,12},{... | collective-permute-start | bytes 1769480 | tf_op jit(solution)/shard_map/ppermute | solution.py:340
  12.4 2.6 %collective-permute-start.8 = (bf16[2,512,256]{2,1,0:T(8,128)(2,1)}, bf16[2,512,256]{2,1,0:T(8,128)(2,1)S(1)}, u32[]{:S(2)}, u32[]{:S(2)}) collective-permute-start(bf16[2,512,256]{2,1,0:T(8,128)(2,1)} %own_in.1), channel_id=1, source_target_pairs={{0,32},{16,48},{32,0},{48,16},{64,96},{80,112},{96,64},{112,80},{1... | collective-permute-start | bytes 1572872 | tf_op jit(solution)/shard_map/ppermute | solution.py:384
  15.7 3.2 %collective-permute-done.2.ym = f32[9,16,8,128]{3,2,1,0:T(8,128)S(1)} collective-permute-done((f32[9,16,8,128]{3,2,1,0:T(8,128)S(1)}, f32[9,16,8,128]{3,2,1,0:T(8,128)S(1)}, u32[]{:S(2)}, u32[]{:S(2)}) %collective-permute-start.2) | collective-permute-done | bytes 589856 | tf_op jit(solution)/shard_map/ppermute | solution.py:338
  18.9 3.4 %collective-permute-start.4 = (f32[9,8,8,128]{3,2,1,0:T(8,128)S(1)}, f32[9,8,8,128]{3,2,1,0:T(8,128)S(1)}, u32[]{:S(2)}, u32[]{:S(2)}) collective-permute-start(f32[9,8,8,128]{3,2,1,0:T(8,128)S(1)} %slice.16), channel_id=1, source_target_pairs={{0,4},{4,8},{8,12},{1,5},{5,9},{9,13},{2,6},{6,10},{10,14},{3,7},{... | collective-permute-start | bytes 884744 | tf_op jit(solution)/shard_map/ppermute | solution.py:341
  22.7 1.3 %collective-permute-start.5 = (f32[9,8,8,128]{3,2,1,0:T(8,128)S(1)}, f32[9,8,8,128]{3,2,1,0:T(8,128)S(1)}, u32[]{:S(2)}, u32[]{:S(2)}) collective-permute-start(f32[9,8,8,128]{3,2,1,0:T(8,128)S(1)} %slice.17), channel_id=1, source_target_pairs={{1,0},{2,1},{3,2},{5,4},{6,5},{7,6},{9,8},{10,9},{11,10},{13,12},{... | collective-permute-start | bytes 884744 | tf_op jit(solution)/shard_map/ppermute | solution.py:344
  24.0 2.2 %collective-permute-done.1.xp = f32[9,8,16,128]{3,2,1,0:T(8,128)S(1)} collective-permute-done((f32[9,8,16,128]{3,2,1,0:T(8,128)S(1)}, f32[9,8,16,128]{3,2,1,0:T(8,128)S(1)}, u32[]{:S(2)}, u32[]{:S(2)}) %collective-permute-start.1) | collective-permute-done | bytes 589856 | tf_op jit(solution)/shard_map/ppermute | solution.py:339
  26.2 4.3 %collective-permute-start.6 = (f32[9,8,8,128]{3,2,1,0:T(8,128)S(1)}, f32[9,8,8,128]{3,2,1,0:T(8,128)S(1)}, u32[]{:S(2)}, u32[]{:S(2)}) collective-permute-start(f32[9,8,8,128]{3,2,1,0:T(8,128)S(1)} %slice.18), channel_id=1, source_target_pairs={{0,1},{1,2},{2,3},{4,5},{5,6},{6,7},{8,9},{9,10},{10,11},{12,13},{... | collective-permute-start | bytes 884744 | tf_op jit(solution)/shard_map/ppermute | solution.py:342
  30.5 1.3 %collective-permute-start.7 = (f32[9,8,8,128]{3,2,1,0:T(8,128)S(1)}, f32[9,8,8,128]{3,2,1,0:T(8,128)S(1)}, u32[]{:S(2)}, u32[]{:S(2)}) collective-permute-start(f32[9,8,8,128]{3,2,1,0:T(8,128)S(1)} %slice.19), channel_id=1, source_target_pairs={{4,0},{8,4},{12,8},{5,1},{9,5},{13,9},{6,2},{10,6},{14,10},{7,3},{... | collective-permute-start | bytes 884744 | tf_op jit(solution)/shard_map/ppermute | solution.py:343
  32.1 1.4 %assemble.1 = (f32[4,32,48,128]{3,2,1,0:T(8,128)S(1)}, f32[4,32,48,128]{3,2,1,0:T(8,128)S(1)}, f32[32,48,128]{2,1,0:T(8,128)S(1)}) custom-call(f32[4,16,16,128]{3,2,1,0:T(8,128)} %now.3, f32[4,16,16,128]{3,2,1,0:T(8,128)} %prev.3, f32[16,16,128]{2,1,0:T(8,128)} %speed.3, f32[9,8,16,128]{3,2,1,0:T(8,128)S(1)} %collective-permute-done.xm, ...), custom_call_target="tpu_custom_call" | custom-call | bytes 8000000 | tf_op jit(solution)/shard_map/assemble/pallas_call | solution.py:91
  35.3 4.2 %collective-permute-done.7.cpp = f32[9,8,8,128]{3,2,1,0:T(8,128)S(1)} collective-permute-done((f32[9,8,8,128]{3,2,1,0:T(8,128)S(1)}, f32[9,8,8,128]{3,2,1,0:T(8,128)S(1)}, u32[]{:S(2)}, u32[]{:S(2)}) %collective-permute-start.7) | collective-permute-done | bytes 294944 | tf_op jit(solution)/shard_map/ppermute | solution.py:343
  39.5 12.7 %stencil.1 = (bf16[8,64,512]{2,1,0:T(8,128)(2,1)}, f32[4,16,16,128]{3,2,1,0:T(8,128)S(1)}, f32[4,16,16,128]{3,2,1,0:T(8,128)}, f32[4,32,48,128]{3,2,1,0:T(8,128)...) custom-call(f32[4,32,48,128]{3,2,1,0:T(8,128)S(1)} %get-tuple-elemen, ...), custom_call_target="tpu_custom_call", output_to_operand_aliasing={{3}: (0, {}), {4}: (1, {}), {5}: (2, {})} | custom-call | flops 2000000000 | bytes 12000000 | tf_op jit(solution)/shard_map/stencil/pallas_call | solution.py:166
  52.2 12.9 %all-to-all-start = ((bf16[8,64,512]{2,1,0:T(8,128)(2,1)}), bf16[8,64,512]{2,1,0:T(8,128)(2,1)S(1)}, u32[]{:S(2)}, u32[]{:S(2)}) async-start(bf16[8,64,512]{2,1,0:T(8,128)(2,1)} %get-tuple-element.22), calls=%async_computation | async-start | bytes 1048576 | tf_op jit(solution)/shard_map/all_to_all | solution.py:42
  65.0 1.9 %collective-permute-start.9 = (bf16[2,512,256]{2,1,0:T(8,128)(2,1)S(1)}, bf16[2,512,256]{2,1,0:T(8,128)(2,1)S(1)}, u32[]{:S(2)}, u32[]{:S(2)}) collective-permute-start(bf16[2,512,256]{2,1,0:T(8,128)(2,1)S(1)} %copy-done.4), channel_id=1, source_target_pairs={{0,16},{16,0},{32,48},{48,32},{64,80},{80,64},{96,112},{112,96},{1... | collective-permute-start | bytes 1572872 | tf_op jit(solution)/shard_map/ppermute | solution.py:384
  67.0 2.4 %collective-permute-start.10 = (bf16[2,512,256]{2,1,0:T(8,128)(2,1)S(1)}, bf16[2,512,256]{2,1,0:T(8,128)(2,1)}, u32[]{:S(2)}, u32[]{:S(2)}) collective-permute-start(bf16[2,512,256]{2,1,0:T(8,128)(2,1)S(1)} %collective-permute-done.8.pair_in), channel_id=1, source_target_pairs={{0,16},{16,0},{32,48},{48,32},{64,80},{80,64},{96,112},{112,96},{1... | collective-permute-start | bytes 1572872 | tf_op jit(solution)/shard_map/ppermute | solution.py:384
  71.0 3.4 %order.1.green = bf16[2,512,1024]{2,1,0:T(8,128)(2,1)S(1)} custom-call(s32[2]{0:T(128)S(1)} %pad_add_fusion.place, bf16[2,512,256]{2,1,0:T(8,128)(2,1)} %own_in.1, bf16[2,512,256]{2,1,0:T(8,128)(2,1)} %copy-done.5, bf16[2,512,256]{2,1,0:T(8,128)(2,1)} %copy-done.6, bf16[2,512,256]{2,1,0:T(8,128)(2,1)} %collective-permute-done.10.diag_in), custom_call_target="tpu_custom_call" | custom-call | flops 1000000000 | bytes 4000000 | tf_op jit(solution)/shard_map/order/pallas_call | solution.py:393
  74.5 9.2 %all-to-all-done.records = bf16[8,64,512]{2,1,0:T(8,128)(2,1)S(1)} async-done(((bf16[8,64,512]{2,1,0:T(8,128)(2,1)}), bf16[8,64,512]{2,1,0:T(8,128)(2,1)S(1)}, u32[]{:S(2)}, u32[]{:S(2)}) %all-to-all-start) | async-done | bytes 524320 | tf_op jit(solution)/shard_map/all_to_all | solution.py:42
  83.7 1.8 %columns.1 = bf16[16,128,128]{2,1,0:T(8,128)(2,1)S(1)} custom-call(s32[2]{0:T(128)S(1)} %copy-done.3, bf16[8,64,512]{2,1,0:T(8,128)(2,1)S(1)} %all-to-all-done.records, bf16[2,512,1024]{2,1,0:T(8,128)(2,1)S(1)} %order.1.green), custom_call_target="tpu_custom_call" | custom-call | flops 1000000000 | bytes 4000000 | tf_op jit(solution)/shard_map/columns/pallas_call | solution.py:225
  85.5 18.0 %all_to_all.15 = bf16[16,128,128]{2,1,0:T(8,128)(2,1)S(1)} all-to-all(bf16[16,128,128]{2,1,0:T(8,128)(2,1)S(1)} %columns.1), channel_id=1, replica_groups=mesh['shot'=32,'tx'=4,'ty'=4] {'tx','ty'}, dimensions={0} | all-to-all | bytes 1048576 | tf_op jit(solution)/shard_map/all_to_all | solution.py:425
  103.5 21.0 %all_to_all.16.em = f32[8,16,128]{2,1,0:T(8,128)S(1)} all-to-all(f32[8,16,128]{2,1,0:T(8,128)S(1)} %bitcast.14), channel_id=1, replica_groups={{0,64,128,192,256,320,384,448},{16,80,144,208,272,336,400,464},{32,96,1..., dimensions={0} | all-to-all | bytes 131072 | tf_op jit(solution)/shard_map/all_to_all | solution.py:42
  124.6 3.5 %inject.1 = (f32[4,16,16,128]{3,2,1,0:T(8,128)}, f32[32,1,512]{2,1,0:T(1,128)}) custom-call(f32[8,16,128]{2,1,0:T(8,128)S(1)} %all_to_all.16.em, s32[8,512]{1,0:T(8,128)S(1)} %bitcast.12, f32[8,512]{1,0:T(8,128)S(1)} %bitcast.13, f32[4,16,16,128]{3,2,1,0:T(8,128)S(1)} %get-tuple-element.23.field), custom_call_target="tpu_custom_call" | custom-call | flops 4000000000 | bytes 4000000 | tf_op jit(solution)/shard_map/inject/pallas_call | solution.py:276
  (31 shorter events, 4.9 us)
Async XLA Ops:
  2.0 16.9 %collective-permute-start.2 = (f32[9,16,8,128]{3,2,1,0:T(8,128)S(1)}, f32[9,16,8,128]{3,2,1,0:T(8,128)S(1)}, u32[]{:S(2)}, u32[]{:S(2)}) collective-permute-start(f32[9,16,8,128]{3,2,1,0:T(8,128)S(1)} %get-tuple-element.17), channel_id=1, source_target_pairs={{0,1},{1,2},{2,3},{4,5},{5,6},{6,7},{8,9},{9,10},{10,11},{12,13},{... | collective-permute-start | bytes 1769480 | tf_op jit(solution)/shard_map/ppermute | solution.py:338
  6.4 16.3 %collective-permute-start = (f32[9,8,16,128]{3,2,1,0:T(8,128)S(1)}, f32[9,8,16,128]{3,2,1,0:T(8,128)S(1)}, u32[]{:S(2)}, u32[]{:S(2)}) collective-permute-start(f32[9,8,16,128]{3,2,1,0:T(8,128)S(1)} %get-tuple-element.15), channel_id=1, source_target_pairs={{0,4},{4,8},{8,12},{1,5},{5,9},{9,13},{2,6},{6,10},{10,14},{3,7},{... | collective-permute-start | bytes 1769480 | tf_op jit(solution)/shard_map/ppermute | solution.py:337
  9.8 16.4 %collective-permute-start.1 = (f32[9,8,16,128]{3,2,1,0:T(8,128)S(1)}, f32[9,8,16,128]{3,2,1,0:T(8,128)S(1)}, u32[]{:S(2)}, u32[]{:S(2)}) collective-permute-start(f32[9,8,16,128]{3,2,1,0:T(8,128)S(1)} %get-tuple-element.16), channel_id=1, source_target_pairs={{4,0},{8,4},{12,8},{5,1},{9,5},{13,9},{6,2},{10,6},{14,10},{7,3},{... | collective-permute-start | bytes 1769480 | tf_op jit(solution)/shard_map/ppermute | solution.py:339
  11.1 19.4 %collective-permute-start.3 = (f32[9,16,8,128]{3,2,1,0:T(8,128)S(1)}, f32[9,16,8,128]{3,2,1,0:T(8,128)S(1)}, u32[]{:S(2)}, u32[]{:S(2)}) collective-permute-start(f32[9,16,8,128]{3,2,1,0:T(8,128)S(1)} %get-tuple-element.18), channel_id=1, source_target_pairs={{1,0},{2,1},{3,2},{5,4},{6,5},{7,6},{9,8},{10,9},{11,10},{13,12},{... | collective-permute-start | bytes 1769480 | tf_op jit(solution)/shard_map/ppermute | solution.py:340
  12.4 54.6 %collective-permute-start.8 = (bf16[2,512,256]{2,1,0:T(8,128)(2,1)}, bf16[2,512,256]{2,1,0:T(8,128)(2,1)S(1)}, u32[]{:S(2)}, u32[]{:S(2)}) collective-permute-start(bf16[2,512,256]{2,1,0:T(8,128)(2,1)} %own_in.1), channel_id=1, source_target_pairs={{0,32},{16,48},{32,0},{48,16},{64,96},{80,112},{96,64},{112,80},{1... | collective-permute-start | bytes 1572872 | tf_op jit(solution)/shard_map/ppermute | solution.py:384
  15.7 23.8 %copy-start = (bf16[4,8,1,1,512]{4,1,3,2,0:T(8,128)(2,1)S(1)}, bf16[4,8,1,1,512]{4,1,3,2,0:T(8,128)(2,1)}, u32[]{:S(2)}) copy-start(bf16[4,8,1,1,512]{4,1,3,2,0:T(8,128)(2,1)} %param.13) | copy-start | bytes 98308
  18.9 14.6 %collective-permute-start.4 = (f32[9,8,8,128]{3,2,1,0:T(8,128)S(1)}, f32[9,8,8,128]{3,2,1,0:T(8,128)S(1)}, u32[]{:S(2)}, u32[]{:S(2)}) collective-permute-start(f32[9,8,8,128]{3,2,1,0:T(8,128)S(1)} %slice.16), channel_id=1, source_target_pairs={{0,4},{4,8},{8,12},{1,5},{5,9},{9,13},{2,6},{6,10},{10,14},{3,7},{... | collective-permute-start | bytes 884744 | tf_op jit(solution)/shard_map/ppermute | solution.py:341
  22.7 11.7 %collective-permute-start.5 = (f32[9,8,8,128]{3,2,1,0:T(8,128)S(1)}, f32[9,8,8,128]{3,2,1,0:T(8,128)S(1)}, u32[]{:S(2)}, u32[]{:S(2)}) collective-permute-start(f32[9,8,8,128]{3,2,1,0:T(8,128)S(1)} %slice.17), channel_id=1, source_target_pairs={{1,0},{2,1},{3,2},{5,4},{6,5},{7,6},{9,8},{10,9},{11,10},{13,12},{... | collective-permute-start | bytes 884744 | tf_op jit(solution)/shard_map/ppermute | solution.py:344
  26.2 9.1 %collective-permute-start.6 = (f32[9,8,8,128]{3,2,1,0:T(8,128)S(1)}, f32[9,8,8,128]{3,2,1,0:T(8,128)S(1)}, u32[]{:S(2)}, u32[]{:S(2)}) collective-permute-start(f32[9,8,8,128]{3,2,1,0:T(8,128)S(1)} %slice.18), channel_id=1, source_target_pairs={{0,1},{1,2},{2,3},{4,5},{5,6},{6,7},{8,9},{9,10},{10,11},{12,13},{... | collective-permute-start | bytes 884744 | tf_op jit(solution)/shard_map/ppermute | solution.py:342
  30.5 8.9 %collective-permute-start.7 = (f32[9,8,8,128]{3,2,1,0:T(8,128)S(1)}, f32[9,8,8,128]{3,2,1,0:T(8,128)S(1)}, u32[]{:S(2)}, u32[]{:S(2)}) collective-permute-start(f32[9,8,8,128]{3,2,1,0:T(8,128)S(1)} %slice.19), channel_id=1, source_target_pairs={{4,0},{8,4},{12,8},{5,1},{9,5},{13,9},{6,2},{10,6},{14,10},{7,3},{... | collective-permute-start | bytes 884744 | tf_op jit(solution)/shard_map/ppermute | solution.py:343
  39.5 25.6 %copy-start.4 = (bf16[2,512,256]{2,1,0:T(8,128)(2,1)S(1)}, bf16[2,512,256]{2,1,0:T(8,128)(2,1)}, u32[]{:S(2)}) copy-start(bf16[2,512,256]{2,1,0:T(8,128)(2,1)} %own_in.1) | copy-start | bytes 1572868
  52.2 31.6 %copy-start.3 = (s32[2]{0:T(128)S(1)}, s32[2]{0:T(128)}, u32[]{:S(2)}) copy-start(s32[2]{0:T(128)} %delay.1) | copy-start | bytes 28
  52.2 31.5 %all-to-all-start = ((bf16[8,64,512]{2,1,0:T(8,128)(2,1)}), bf16[8,64,512]{2,1,0:T(8,128)(2,1)S(1)}, u32[]{:S(2)}, u32[]{:S(2)}) async-start(bf16[8,64,512]{2,1,0:T(8,128)(2,1)} %get-tuple-element.22), calls=%async_computation | async-start | bytes 1048576 | tf_op jit(solution)/shard_map/all_to_all | solution.py:42
  65.0 4.5 %collective-permute-start.9 = (bf16[2,512,256]{2,1,0:T(8,128)(2,1)S(1)}, bf16[2,512,256]{2,1,0:T(8,128)(2,1)S(1)}, u32[]{:S(2)}, u32[]{:S(2)}) collective-permute-start(bf16[2,512,256]{2,1,0:T(8,128)(2,1)S(1)} %copy-done.4), channel_id=1, source_target_pairs={{0,16},{16,0},{32,48},{48,32},{64,80},{80,64},{96,112},{112,96},{1... | collective-permute-start | bytes 1572872 | tf_op jit(solution)/shard_map/ppermute | solution.py:384
  67.0 2.5 %copy-start.5 = (bf16[2,512,256]{2,1,0:T(8,128)(2,1)}, bf16[2,512,256]{2,1,0:T(8,128)(2,1)S(1)}, u32[]{:S(2)}) copy-start(bf16[2,512,256]{2,1,0:T(8,128)(2,1)S(1)} %collective-permute-done.8.pair_in) | copy-start | bytes 1572868
  67.0 4.1 %collective-permute-start.10 = (bf16[2,512,256]{2,1,0:T(8,128)(2,1)S(1)}, bf16[2,512,256]{2,1,0:T(8,128)(2,1)}, u32[]{:S(2)}, u32[]{:S(2)}) collective-permute-start(bf16[2,512,256]{2,1,0:T(8,128)(2,1)S(1)} %collective-permute-done.8.pair_in), channel_id=1, source_target_pairs={{0,16},{16,0},{32,48},{48,32},{64,80},{80,64},{96,112},{112,96},{1... | collective-permute-start | bytes 1572872 | tf_op jit(solution)/shard_map/ppermute | solution.py:384
  69.5 0.8 copy-start.6
  74.5 50.1 %copy-start.1 = (s32[1,1,8,512]{3,2,1,0:T(8,128)S(1)}, s32[1,1,8,512]{3,2,1,0:T(8,128)}, u32[]{:S(2)}) copy-start(s32[1,1,8,512]{3,2,1,0:T(8,128)} %param.16) | copy-start | bytes 49156
  74.5 50.1 %copy-start.2 = (f32[1,1,8,512]{3,2,1,0:T(8,128)S(1)}, f32[1,1,8,512]{3,2,1,0:T(8,128)}, u32[]{:S(2)}) copy-start(f32[1,1,8,512]{3,2,1,0:T(8,128)} %param.17) | copy-start | bytes 49156
